TPU v7x, 32 devices: a whole 2x2x4 slice. The times are simulated.
32 devices in a mesh: tok: 8 (over z, core), par: 4 (over y, x).
Axes of the slice: x: 2, y: 2, z: 4, core: 2. Of those that a mesh axis runs over, the one named last changes fastest.
Arguments:
- query_grads: bfloat16 [4, 8192, 28672], P(None, 'tok', 'par'), as said below
- start_block: bfloat16 [28672, 128], P('par', 'tok'), may hold values from -6 to 6
- hooked_out: bfloat16 [2048, 8192], P('tok', 'par'), may hold values from -6 to 6
- hooked_in: bfloat16 [2048, 28672], P('tok', 'par'), may hold values from -6 to 6
Outputs:
- scores: float32 [4, 2048], P(None, 'tok')
Inputs may be any that keep to these rules, and one draw needn't show every extreme that they name: `query_grads`: Real-valued gradient matrices, of full rank.
All inputs are finite; a program needn't handle non-finite values.
Results may differ from a plain program's by a relative error of at most 0.006.
Values may be sent and summed in bfloat16 or wider, within the bound.
No kernel may reach another device: no remote copies, remote signals or barrier semaphores. Data moves between devices by JAX's collectives and lax.ppermute only.
A program may use at most 128 MiB of HBM per device.

v0:
```python
import jax
import jax.numpy as jnp
from jax import lax
from jax.sharding import PartitionSpec as P

RANK = 32
ITERS = 2


def local_gram(images):
    blocks = images.reshape(images.shape[0], images.shape[1] // RANK, RANK)
    return jnp.einsum("oqr,oqs->qrs", blocks, blocks, precision=lax.Precision.HIGHEST)


def from_gram(images, gram_sum):
    blocks = images.reshape(images.shape[0], images.shape[1] // RANK, RANK)
    chol_factor = jnp.linalg.cholesky(gram_sum)
    solved = lax.linalg.triangular_solve(
        chol_factor, jnp.transpose(blocks, (1, 2, 0)), left_side=True, lower=True
    )
    return jnp.transpose(solved, (2, 0, 1)).reshape(images.shape).astype(jnp.bfloat16)


def on_device(query_grads, start_block, hooked_out, hooked_in):
    queries = query_grads.shape[0]
    rows_tok = query_grads.shape[1]
    cols_par = hooked_out.shape[1]
    subspace = lax.all_gather(start_block, "tok", axis=1, tiled=True)
    local_basis = None
    for iteration in range(ITERS):
        sub_blocks = subspace.reshape(subspace.shape[0], queries, RANK)
        partial_value = jnp.einsum(
            "qoi,iqr->oqr", query_grads, sub_blocks, preferred_element_type=jnp.float32
        )
        images = lax.psum(partial_value.reshape(rows_tok, queries * RANK), "par")
        gram_sum = lax.psum(local_gram(images), "tok")
        local_basis = from_gram(images, gram_sum)
        basis_blocks = local_basis.reshape(rows_tok, queries, RANK)
        back_terms = jnp.einsum(
            "qoi,oqr->iqr", query_grads, basis_blocks, preferred_element_type=jnp.float32
        )
        summed = lax.psum(back_terms.reshape(back_terms.shape[0], queries * RANK), "tok")
        subspace = summed.astype(jnp.bfloat16)
    gathered = lax.all_gather(local_basis, "tok", axis=0, tiled=True)
    basis_par = lax.dynamic_slice_in_dim(gathered, lax.axis_index("par") * cols_par, cols_par, 0)
    out_proj = jnp.dot(hooked_out, basis_par, preferred_element_type=jnp.float32)
    in_proj = jnp.dot(hooked_in, subspace, preferred_element_type=jnp.float32)
    whole_out, whole_in = lax.psum((out_proj, in_proj), "par")
    token_scores = (whole_out * whole_in).reshape(whole_out.shape[0], queries, RANK).sum(axis=2)
    return token_scores.T


def solution(mesh):
    placed = (P(None, "tok", "par"), P("par", "tok"), P("tok", "par"), P("tok", "par"))
    return jax.shard_map(
        on_device, mesh=mesh, in_specs=placed, out_specs=P(None, "tok"), check_vma=False
    )
```

profile of v0, /device:TPU:0, one launch (start us, length us, event | category | flops | bytes accessed | tf_op | source)
XLA Modules:
  0.0 557.5 jit_solution(13918588205250995123)
XLA Ops:
  6.5 0.7 all-gather.3.cloned.1.call-update
  7.3 31.4 %all-gather.3.cloned.1.call-done = bf16[7168,128]{0,1:T(8,128)(2,1)} async-done(((bf16[7168,16]{0,1:T(8,128)(2,1)}), bf16[7168,128]{0,1:T(8,128)(2,1)}) %all-gather.3.cloned.1.call-update) | async-done | bytes 1835024 | tf_op jit(solution)/shard_map/all_gather | solution.py:28
  38.7 24.9 %convolution_bitcast_fusion.1 = f32[1024,4,32]{0,2,1:T(8,128)} fusion(bf16[7168,4,32]{0,2,1:T(8,128)(2,1)} %bitcast.67, bf16[4,1024,7168]{2,1,0:T(8,128)(2,1)} %param.7), kind=kOutput, calls=%fused_computation.3 | convolution fusion | flops 1879048192 | bytes 61079552 | tf_op jit(solution)/shard_map/qoi,iqr->oqr/dot_general | solution.py:32
  63.7 44.9 %all-reduce.7.cloned.1.call-done = f32[1024,4,32]{0,2,1:T(8,128)} async-done(((f32[1024,4,32]{0,2,1:T(8,128)}), f32[1024,4,32]{0,2,1:T(8,128)}) %all-reduce.7.cloned.1.call-update) | async-done | bytes 524304 | tf_op jit(solution)/shard_map/psum | solution.py:35
  108.5 1.8 fusion.16
  110.4 28.5 %psum.57 = f32[4,32,32]{1,2,0:T(8,128)S(1)} all-reduce(f32[4,32,32]{1,2,0:T(8,128)S(1)} %fusion.16), channel_id=1, replica_groups=mesh['tok'=8,'par'=4] {'tok'}, use_global_device_ids=true, to_apply=%region_1.0 | all-reduce | flops 4096 | bytes 32768 | tf_op jit(solution)/shard_map/psum | solution.py:36
  138.9 11.7 %custom-call.8 = f32[4,32,32]{2,1,0:T(8,128)S(1)} custom-call(f32[4,32,32]{2,1,0:T(8,128)S(1)} %fusion.14), custom_call_target="Cholesky" | custom-call | tf_op jit(solution)/shard_map/jit(cholesky)/cholesky | solution.py:17
  150.9 9.8 %custom-call.9 = f32[4,1,32,32]{2,3,1,0:T(8,128)S(1)} custom-call(f32[4,1,32,32]{3,2,1,0:T(8,128)S(1)} %select_bitcast_fusion.1), custom_call_target="InvertDiagBlocksLowerTriangular" | custom-call | tf_op jit(solution)/shard_map/triangular_solve/custom-call.0 | solution.py:18
  160.7 1.7 fusion.2
  162.4 22.4 %fusion.17 = f32[4,32,7168]{2,1,0:T(8,128)} fusion(bf16[1024,4,32]{0,2,1:T(8,128)(2,1)S(1)} %fusion.2, bf16[4,1024,7168]{2,1,0:T(8,128)(2,1)} %param.7), kind=kOutput, calls=%fused_computation.31 | convolution fusion | flops 1879048192 | bytes 62652416 | tf_op jit(solution)/shard_map/qoi,oqr->iqr/dot_general | solution.py:39
  184.8 76.4 %all-reduce.12 = bf16[7168,128]{0,1:T(8,128)(2,1)S(1)} all-reduce(f32[7168,128]{0,1:T(8,128)} %bitcast.65), channel_id=1, replica_groups=mesh['tok'=8,'par'=4] {'tok'}, use_global_device_ids=true, to_apply=%region_4.7 | all-reduce | flops 917504 | bytes 5505024 | tf_op jit(solution)/shard_map/psum | solution.py:42
  261.3 24.6 %convolution_bitcast_fusion = f32[1024,4,32]{0,2,1:T(8,128)} fusion(bf16[7168,4,32]{0,2,1:T(8,128)(2,1)S(1)} %bitcast.66, bf16[4,1024,7168]{2,1,0:T(8,128)(2,1)} %param.7), kind=kOutput, calls=%fused_computation.2 | convolution fusion | flops 1879048192 | bytes 61079552 | tf_op jit(solution)/shard_map/qoi,iqr->oqr/dot_general | solution.py:32
  285.9 44.9 %all-reduce.9.cloned.1.call-done = f32[1024,4,32]{0,2,1:T(8,128)} async-done(((f32[1024,4,32]{0,2,1:T(8,128)}), f32[1024,4,32]{0,2,1:T(8,128)}) %all-reduce.9.cloned.1.call-update) | async-done | bytes 524304 | tf_op jit(solution)/shard_map/psum | solution.py:35
  330.8 1.8 fusion.18
  332.6 28.5 %psum.60 = f32[4,32,32]{1,2,0:T(8,128)S(1)} all-reduce(f32[4,32,32]{1,2,0:T(8,128)S(1)} %fusion.18), channel_id=1, replica_groups=mesh['tok'=8,'par'=4] {'tok'}, use_global_device_ids=true, to_apply=%region_6.9 | all-reduce | flops 4096 | bytes 32768 | tf_op jit(solution)/shard_map/psum | solution.py:36
  361.2 11.7 %custom-call.10 = f32[4,32,32]{2,1,0:T(8,128)S(1)} custom-call(f32[4,32,32]{2,1,0:T(8,128)S(1)} %fusion.12), custom_call_target="Cholesky" | custom-call | tf_op jit(solution)/shard_map/jit(cholesky)/cholesky | solution.py:17
  373.2 9.8 %custom-call.11 = f32[4,1,32,32]{2,3,1,0:T(8,128)S(1)} custom-call(f32[4,1,32,32]{3,2,1,0:T(8,128)S(1)} %select_bitcast_fusion), custom_call_target="InvertDiagBlocksLowerTriangular" | custom-call | tf_op jit(solution)/shard_map/triangular_solve/custom-call.0 | solution.py:18
  383.0 1.7 convolution_convert_fusion
  384.7 22.5 %fusion.9 = f32[4,32,7168]{2,1,0:T(8,128)} fusion(bf16[4,1024,7168]{2,1,0:T(8,128)(2,1)} %param.7, bf16[4,32,1024]{2,1,0:T(8,128)(2,1)S(1)} %convolution_convert_fusion), kind=kOutput, calls=%fused_computation.12 | convolution fusion | flops 1879048192 | bytes 62652416 | tf_op jit(solution)/shard_map/qoi,oqr->iqr/dot_general | solution.py:39
  407.3 93.1 %all-reduce.13 = bf16[7168,128]{0,1:T(8,128)(2,1)S(1)} all-reduce(f32[7168,128]{0,1:T(8,128)} %bitcast.64), channel_id=1, replica_groups=mesh['tok'=8,'par'=4] {'tok'}, use_global_device_ids=true, to_apply=%region_8.11 | all-reduce | flops 917504 | bytes 5505024 | tf_op jit(solution)/shard_map/psum | solution.py:42
  500.4 4.0 fusion.3
  504.4 2.2 convolution_bitcast_fusion.2
  506.6 42.8 %all-reduce.11.cloned.1.call-done = (f32[256,128]{0,1:T(8,128)}, f32[256,128]{0,1:T(8,128)}) async-done(((f32[256,128]{0,1:T(8,128)}, f32[256,128]{0,1:T(8,128)}), (f32[256,128]{0,1:T(8,128)}, f32[256,128]{0,1:T(8,128)})) %all-reduce.11.cloned.1.call-update) | async-done | bytes 262160 | tf_op jit(solution)/shard_map/psum | solution.py:48
  549.4 1.6 bitcast_reduce_fusion
  (26 shorter events, 0.9 us)
Async XLA Ops:
  6.5 497.9 %copy-start = (bf16[256,2048]{1,0:T(8,128)(2,1)S(1)}, bf16[256,2048]{1,0:T(8,128)(2,1)}, u32[]{:S(2)}) copy-start(bf16[256,2048]{1,0:T(8,128)(2,1)} %param.9) | copy-start | bytes 3145732
  6.5 32.2 %all-gather.3.cloned.1.call-start = ((), (), s32[]{:S(2)}) async-start(), calls=%async_computation | async-start | bytes 2064384 | tf_op jit(solution)/shard_map/all_gather | solution.py:28
  7.3 101.3 %all-reduce.7.cloned.1.call-start = ((), (), s32[]{:S(2)}) async-start(), calls=%async_computation.1 | async-start | bytes 1048576 | tf_op jit(solution)/shard_map/psum | solution.py:35
  63.6 267.2 %all-reduce.9.cloned.1.call-start = ((), (), s32[]{:S(2)}) async-start(), calls=%async_computation.2 | async-start | bytes 1048576 | tf_op jit(solution)/shard_map/psum | solution.py:35
  285.9 218.5 %all-gather.5.cloned.1.call-start = ((), (), s32[]{:S(2)}) async-start(), calls=%async_computation.3 | async-start | bytes 2359296 | tf_op jit(solution)/shard_map/all_gather | solution.py:44
  384.7 22.5 %copy-start.1 = (bf16[4,32,1024]{2,1,0:T(8,128)(2,1)}, bf16[4,32,1024]{2,1,0:T(8,128)(2,1)S(1)}, u32[]{:S(2)}) copy-start(bf16[4,32,1024]{2,1,0:T(8,128)(2,1)S(1)} %convolution_convert_fusion) | copy-start | bytes 786436
  407.2 142.1 %all-reduce.11.cloned.1.call-start = ((), (), s32[]{:S(2)}) async-start(), calls=%async_computation.4 | async-start | bytes 524288 | tf_op jit(solution)/shard_map/psum | solution.py:48
Sparse Core Ops, SparseCore 0:
  9.0 29.6 all-gather.2
  63.7 44.7 all-reduce.6
  286.0 44.7 all-reduce.8
  407.4 38.7 all-gather.4
  506.7 42.6 all-reduce.10
where the time goes:
time: 558 us; the launch traced here: 557 us
  blocking collectives  226 us (41%)
  waiting for transfers between devices  165 us (30%)
  matrix products  108 us (19%)
  other arithmetic  45.2 us (8%)
  between operations  13.3 us (2%)
    psum x2, blocking collectives, on_device(): lax.psum(back_terms.reshape(back_terms.shape[0], queries * RANK), 'tok')  170 us
    psum x2, waiting for transfers between devices, on_device(): images = lax.psum(partial_value.reshape(rows_tok, queries * RANK), 'par')  89.8 us
    psum x2, blocking collectives, on_device(): gram_sum = lax.psum(local_gram(images), 'tok')  56.9 us
    dot_general x2, matrix products, on_device(): jnp.einsum('qoi,iqr->oqr', query_grads, sub_blocks, preferred_element_typ...  49.4 us
    dot_general x2, matrix products, on_device(): jnp.einsum('qoi,oqr->iqr', query_grads, basis_blocks, preferred_element_t...  44.9 us
    psum x1, waiting for transfers between devices, on_device(): whole_out, whole_in = lax.psum((out_proj, in_proj), 'par')  42.8 us
    all_gather x1, waiting for transfers between devices, on_device(): subspace = lax.all_gather(start_block, 'tok', axis=1, tiled=True)  31.4 us
    another operation x7, other arithmetic, from_gram(): chol_factor = jnp.linalg.cholesky(gram_sum)  23.8 us
  transfers between devices with their start and end apart: 5, of which 4 were waited for; matrix products, arithmetic and copies ran while one was open for 1% of the time, Pallas kernels for 0%

commit v1 on v0

v1 whole, which is shorter than its diff:
```python
import functools
import jax
import jax.numpy as jnp
from jax import lax
from jax.experimental import pallas as pl
from jax.experimental.pallas import tpu as pltpu
from jax.sharding import PartitionSpec as P

RANK = 32
ITERS = 2
CORES = 2
F32, BF16 = jnp.float32, jnp.bfloat16
HIGH = lax.Precision.HIGHEST
NT = (((1,), (1,)), ((), ()))
ANY = pl.BlockSpec(memory_space=pl.ANY)
VMEM = pl.BlockSpec(memory_space=pltpu.VMEM)
SMEM = pl.BlockSpec(memory_space=pltpu.SMEM)
VMEM_BYTES = 60 * 1024 * 1024


def params():
    return pltpu.CompilerParams(vmem_limit_bytes=VMEM_BYTES)


def cost(flops, nbytes):
    return pl.CostEstimate(flops=int(flops), bytes_accessed=int(nbytes), transcendentals=0)


ROW_CHUNKS = 8


def images_body(where, mine_ref, other_ref, grads_ref, *rest, slot, aliased):
    out_ref, buf, sems = rest[1:] if aliased else rest
    query, core = where[0], where[1]
    rows = buf.shape[1]

    def fetch(i):
        return pltpu.make_async_copy(
            grads_ref.at[query, pl.ds(i * rows, rows), :], buf.at[i], sems.at[i]
        )

    for i in range(ROW_CHUNKS):
        fetch(i).start()
    mine, other = mine_ref[...], other_ref[...]
    vectors = jnp.concatenate(
        [jnp.where(core == 0, mine, other), jnp.where(core == 0, other, mine)], axis=0
    )

    def body(i, carry):
        fetch(i).wait()
        out_ref[0, :, pl.ds(pl.multiple_of(i * rows, 128), rows)] = lax.dot_general(
            vectors, buf[i], NT, preferred_element_type=F32
        )
        return carry

    lax.fori_loop(0, ROW_CHUNKS, body, 0)


def images_of_query(where, mine, other, grads, slot, slots, earlier=None):
    _, rows, cols = grads.shape
    aliased = earlier is not None
    return pl.pallas_call(
        functools.partial(images_body, slot=slot, aliased=aliased),
        grid=(1,),
        in_specs=[SMEM, VMEM, VMEM, ANY] + ([ANY] if aliased else []),
        out_specs=pl.BlockSpec((1, RANK, rows), lambda i: (slot, 0, 0)),
        out_shape=jax.ShapeDtypeStruct((slots, RANK, rows), F32),
        scratch_shapes=[
            pltpu.VMEM((ROW_CHUNKS, rows // ROW_CHUNKS, cols), BF16),
            pltpu.SemaphoreType.DMA((ROW_CHUNKS,)),
        ],
        input_output_aliases={4: 0} if aliased else {},
        cost_estimate=cost(2 * RANK * rows * cols * 8, 2 * rows * cols),
        compiler_params=params(),
    )(where, mine, other, grads, *([earlier] if aliased else []))


SLOTS = 8


def back_body(where, basis_ref, grads_ref, mine_ref, other_ref, buf, sems, *, first, width):
    core = where[1]
    queries, half, cols = mine_ref.shape
    steps = queries * (cols // width)

    def fetch(step):
        query, block = lax.rem(step, queries), lax.div(step, queries)
        slot = lax.rem(step, SLOTS)
        start = pl.multiple_of(first + block * width, 128)
        return pltpu.make_async_copy(
            grads_ref.at[query, :, pl.ds(start, width)], buf.at[slot], sems.at[slot]
        )

    for step in range(min(SLOTS - 1, steps)):
        fetch(jnp.int32(step)).start()

    def body(step, carry):
        @pl.when(step + SLOTS - 1 < steps)
        def _():
            fetch(step + SLOTS - 1).start()

        query, block = lax.rem(step, queries), lax.div(step, queries)
        fetch(step).wait()
        product = jnp.dot(
            basis_ref[query], buf[lax.rem(step, SLOTS)], preferred_element_type=F32
        )
        low, high = product[:half], product[half:]
        where_to = pl.ds(pl.multiple_of(block * width, 128), width)
        mine_ref[query, :, where_to] = jnp.where(core == 0, low, high)
        other_ref[query, :, where_to] = jnp.where(core == 0, high, low).astype(BF16)
        return carry

    lax.fori_loop(0, steps, body, 0)


def back_project(where, basis, grads, first, cols, width):
    queries, rows, _ = grads.shape
    half = RANK // CORES
    return pl.pallas_call(
        functools.partial(back_body, first=first, width=width),
        in_specs=[SMEM, VMEM, ANY],
        out_specs=[VMEM, VMEM],
        out_shape=[
            jax.ShapeDtypeStruct((queries, half, cols), F32),
            jax.ShapeDtypeStruct((queries, half, cols), BF16),
        ],
        scratch_shapes=[
            pltpu.VMEM((SLOTS, rows, width), BF16),
            pltpu.SemaphoreType.DMA((SLOTS,)),
        ],
        cost_estimate=cost(2 * RANK * queries * rows * cols * 8, 2 * queries * rows * cols),
        compiler_params=params(),
    )(where, basis, grads)


def gram_body(where, *refs):
    pairs, (images_ref, gram_ref) = refs[:-2], refs[-2:]
    chip = where[0]
    queries = images_ref.shape[0]
    slot = 0
    for held, received in zip(pairs[0::2], pairs[1::2]):
        for i in range(held.shape[0]):
            images_ref[chip ^ slot] = held[i] + received[i]
            slot += 1
    for query in range(queries):
        block = images_ref[query]
        gram_ref[:, query * RANK : (query + 1) * RANK] = lax.dot_general(
            block, block, NT, precision=HIGH, preferred_element_type=F32
        )


def local_gram(where, pairs):
    flat = [part for pair in pairs for part in pair]
    queries = sum(held.shape[0] for held, _ in pairs)
    rows = flat[0].shape[2]
    return pl.pallas_call(
        gram_body,
        in_specs=[SMEM] + [VMEM] * len(flat),
        out_specs=[VMEM, VMEM],
        out_shape=[
            jax.ShapeDtypeStruct((queries, RANK, rows), F32),
            jax.ShapeDtypeStruct((RANK, queries * RANK), F32),
        ],
        cost_estimate=cost(12 * RANK * RANK * queries * rows, 16 * queries * RANK * rows),
        compiler_params=params(),
    )(where, *flat)


def basis_body(gram_ref, received_ref, images_ref, basis_ref):
    queries = images_ref.shape[0]
    total = queries * RANK
    gram = gram_ref[...] + received_ref[...]
    stacked = jnp.concatenate(
        [gram[:, q * RANK : (q + 1) * RANK] for q in range(queries)], axis=0
    )
    row = lax.broadcasted_iota(jnp.int32, (total, RANK), 0) % RANK
    col = lax.broadcasted_iota(jnp.int32, (total, RANK), 1)
    table = jnp.concatenate([stacked, jnp.where(row == col, 1.0, 0.0).astype(F32)], axis=1)
    row = lax.broadcasted_iota(jnp.int32, (total, 2 * RANK), 0) % RANK
    table = table.reshape(queries, RANK, 2 * RANK)
    row = row.reshape(queries, RANK, 2 * RANK)
    scales = jnp.zeros((queries, RANK, 1), F32)
    for k in range(RANK):
        pivot_row = table[:, k : k + 1, :]
        pivot = pivot_row[:, :, k : k + 1]
        factor = table[:, :, k : k + 1] / pivot
        scales = jnp.where(row[:, :, :1] == k, lax.rsqrt(pivot), scales)
        table = table - jnp.where(row > k, factor * pivot_row, 0.0)
    inverse = table[:, :, RANK:] * scales
    for q in range(queries):
        basis_ref[q] = jnp.dot(
            inverse[q], images_ref[q], precision=HIGH, preferred_element_type=F32
        ).astype(BF16)


def orthonormal(gram, received, images):
    return pl.pallas_call(
        basis_body,
        in_specs=[VMEM] * 3,
        out_specs=VMEM,
        out_shape=jax.ShapeDtypeStruct(images.shape, BF16),
        cost_estimate=cost(12 * RANK * images.size + 10**9, 6 * images.size),
        compiler_params=params(),
    )(gram, received, images)


def combine_body(where, mine_ref, received_ref, own_ref, *send_refs):
    chip = where[0]
    own_ref[...] = mine_ref[chip] + received_ref[chip].astype(F32)
    for d, send_ref in enumerate(send_refs, 1):
        send_ref[...] = (mine_ref[chip ^ d] + received_ref[chip ^ d].astype(F32)).astype(BF16)


def combine(where, mine, received):
    chips, half, cols = mine.shape
    return pl.pallas_call(
        combine_body,
        in_specs=[SMEM, VMEM, VMEM],
        out_specs=[VMEM] * chips,
        out_shape=[jax.ShapeDtypeStruct((half, cols), F32)]
        + [jax.ShapeDtypeStruct((half, cols), BF16)] * (chips - 1),
        cost_estimate=cost(mine.size, 10 * mine.size),
        compiler_params=params(),
    )(where, mine, received)


def xor_permute(x, axis, size, bits):
    return lax.ppermute(x, axis, [(i, i ^ bits) for i in range(size)])


def fast(query_grads, start_block, hooked_out, hooked_in, *, toks, pars):
    queries, rows, cols = query_grads.shape
    chips = toks // CORES
    tok, par = lax.axis_index("tok"), lax.axis_index("par")
    chip, core = tok // CORES, tok % CORES
    where = [jnp.stack([chip ^ d, core]).astype(jnp.int32) for d in range(chips)]

    def tok_swap(x, bits):
        return xor_permute(x, "tok", toks, bits)

    def images_from(piece):
        pieces = [piece] + [tok_swap(piece, CORES * d) for d in range(1, chips)]
        held, parts = None, []
        for d in range(chips):
            other = tok_swap(pieces[d], 1)
            held = images_of_query(where[d], pieces[d], other, query_grads, d % 2, 2, held)
            if d % 2 == 1:
                parts.append(held)
                held = None
        bits = [1 << i for i in range(pars.bit_length() - 1)]
        pairs = []
        for i, part in enumerate(parts):
            order = bits if i % 2 == 0 else bits[::-1]
            for b in order[:-1]:
                part = part + xor_permute(part, "par", pars, b)
            pairs.append((part, xor_permute(part, "par", pars, order[-1])))
        return pairs

    def basis_from(pairs):
        images, gram = local_gram(where[0], pairs)
        bits = [1 << i for i in range(toks.bit_length() - 1)]
        for b in bits[:-1]:
            gram = gram + tok_swap(gram, b)
        return orthonormal(gram, tok_swap(gram, bits[-1]), images)

    def back_piece(basis):
        mine, other = back_project(where[0], basis, query_grads, 0, cols, cols // 8)
        received = tok_swap(other, 1)
        own, *sends = combine(where[0], mine, received)
        total = own
        for d, send in enumerate(sends, 1):
            total = total + tok_swap(send, CORES * d).astype(F32)
        return total.astype(BF16)

    piece = start_block.T
    basis = None
    for _ in range(ITERS):
        basis = basis_from(images_from(piece))
        piece = back_piece(basis)

    flat = basis.reshape(queries * RANK, rows)
    got = jnp.where(chip == par, flat, jnp.zeros_like(flat))
    for d in range(1, chips):
        sends = [
            ((p * CORES + c) * pars + p, ((p ^ d) * CORES + c) * pars + p)
            for p in range(pars)
            for c in range(CORES)
        ]
        got = got + lax.ppermute(flat, ("tok", "par"), sends)
    mate = tok_swap(got, 1)
    low, high = jnp.where(core == 0, got, mate), jnp.where(core == 0, mate, got)
    basis_par = jnp.concatenate([low, high], axis=1)
    out_proj = lax.dot_general(basis_par, hooked_out, NT, preferred_element_type=F32)

    half = RANK // CORES
    in_parts = []
    for d in range(chips):
        mine = piece if d == 0 else tok_swap(piece, CORES * d)
        mate = tok_swap(mine, 1)
        both = jnp.concatenate([jnp.where(core == 0, mine, mate), jnp.where(core == 0, mate, mine)])
        in_parts.append(lax.dot_general(both, hooked_in, NT, preferred_element_type=F32))
    in_rel = jnp.stack(in_parts)
    out_rel = out_proj.reshape(queries, RANK, -1)
    order = jnp.stack([chip ^ d for d in range(chips)])
    out_rel = jnp.stack([out_rel[chip ^ d] for d in range(chips)])
    whole = jnp.stack([out_rel, in_rel])
    for b in [1 << i for i in range(pars.bit_length() - 1)]:
        whole = whole + xor_permute(whole, "par", pars, b)
    rel = (whole[0] * whole[1]).sum(axis=1)
    return jnp.stack([rel[chip ^ q] for q in range(queries)])


def plain(query_grads, start_block, hooked_out, hooked_in):
    queries, rows_tok = query_grads.shape[:2]
    cols_par = hooked_out.shape[1]

    def blocked(x):
        return x.reshape(x.shape[0], queries, RANK)

    subspace = lax.all_gather(start_block, "tok", axis=1, tiled=True)
    basis = None
    for _ in range(ITERS):
        partial = jnp.einsum(
            "qoi,iqr->oqr", query_grads, blocked(subspace), preferred_element_type=F32
        )
        images = lax.psum(partial.reshape(rows_tok, queries * RANK), "par")
        blocks = blocked(images)
        gram = lax.psum(jnp.einsum("oqr,oqs->qrs", blocks, blocks, precision=HIGH), "tok")
        solved = lax.linalg.triangular_solve(
            jnp.linalg.cholesky(gram), jnp.transpose(blocks, (1, 2, 0)), left_side=True, lower=True
        )
        basis = jnp.transpose(solved, (2, 0, 1)).reshape(images.shape).astype(BF16)
        back = jnp.einsum(
            "qoi,oqr->iqr", query_grads, blocked(basis), preferred_element_type=F32
        )
        subspace = lax.psum(back.reshape(back.shape[0], queries * RANK), "tok").astype(BF16)
    gathered = lax.all_gather(basis, "tok", axis=0, tiled=True)
    basis_par = lax.dynamic_slice_in_dim(gathered, lax.axis_index("par") * cols_par, cols_par, 0)
    out_proj = jnp.dot(hooked_out, basis_par, preferred_element_type=F32)
    in_proj = jnp.dot(hooked_in, subspace, preferred_element_type=F32)
    whole_out, whole_in = lax.psum((out_proj, in_proj), "par")
    return (whole_out * whole_in).reshape(whole_out.shape[0], queries, RANK).sum(axis=2).T


def solution(mesh):
    toks, pars = mesh.shape["tok"], mesh.shape["par"]

    def on_device(query_grads, start_block, hooked_out, hooked_in):
        if toks == CORES * query_grads.shape[0] and toks == CORES * pars:
            run = functools.partial(fast, toks=toks, pars=pars)
        else:
            run = plain
        return run(query_grads, start_block, hooked_out, hooked_in)

    placed = (P(None, "tok", "par"), P("par", "tok"), P("tok", "par"), P("tok", "par"))
    return jax.shard_map(
        on_device, mesh=mesh, in_specs=placed, out_specs=P(None, "tok"), check_vma=False
    )
```

time: 558 us -> 354 us (0.63)
  blocking collectives: 226 us -> 0 us
  Pallas kernels: 0 us -> 136 us
  matrix products: 108 us -> 5.23 us
  starting transfers between devices: 0.17 us -> 61.6 us
  other arithmetic: 45.2 us -> 8.71 us
  waiting for transfers between devices: 165 us -> 130 us
  between operations: 13.3 us -> 0.62 us
  local copies, waits for them, and re-layouts: 0.17 us -> 10.1 us
    psum x4 -> x0, blocking collectives: 226 us -> none  [the longest x2 170 us: on_device(): lax.psum(back_terms.reshape(back_terms.shape[0], queries * RANK), 'tok')]
    pallas_call x0 -> x16, Pallas kernels: none -> 136 us  [the longest x8 71.5 us: images_of_query(): pl.pallas_call(functools.partial(images_body, slot=slot, aliased=aliased)...]
    psum x3 -> x0, waiting for transfers between devices: 133 us -> none  [the longest x2 89.8 us: on_device(): images = lax.psum(partial_value.reshape(rows_tok, queries * RANK), 'par')]
    ppermute x0 -> x49, waiting for transfers between devices: none -> 130 us  [the longest x46 130 us: xor_permute(): return lax.ppermute(x, axis, [(i, i ^ bits) for i in range(size)])]
    dot_general x8 -> x5, matrix products: 104 us -> 5.23 us  [the longest x4 4.75 us: fast(): lax.dot_general(both, hooked_in, NT, preferred_element_type=F32)]
    ppermute x0 -> x49, starting transfers between devices: none -> 61.6 us  [the longest x46 55.4 us: xor_permute(): return lax.ppermute(x, axis, [(i, i ^ bits) for i in range(size)])]
    another operation x12 -> x7, other arithmetic: 43.6 us -> 2.57 us  [the longest x3 1.91 us: fast(): jnp.stack([chip ^ d, core]).astype(jnp.int32)]
    all_gather x2 -> x0, waiting for transfers between devices: 31.4 us -> none  [the longest x1 31.4 us: on_device(): subspace = lax.all_gather(start_block, 'tok', axis=1, tiled=True)]
  transfers between devices with their start and end apart: 5 -> 49, of which waited for: 4 -> 26; matrix products, arithmetic and copies ran while one was open for 1% -> 2% of each run, Pallas kernels for 0% -> 26%
where the time goes in v1:
time: 354 us; the launch traced here: 352 us
  Pallas kernels  136 us (38%)
  waiting for transfers between devices  130 us (37%)
  starting transfers between devices  61.6 us (17%)
  local copies, waits for them, and re-layouts  10.1 us (3%)
  other arithmetic  8.71 us (2%)
  matrix products  5.23 us (1%)
    ppermute x46, waiting for transfers between devices, xor_permute(): return lax.ppermute(x, axis, [(i, i ^ bits) for i in range(size)])  130 us
    pallas_call x8, Pallas kernels, images_of_query(): pl.pallas_call(functools.partial(images_body, slot=slot, aliased=aliased)...  71.5 us
    ppermute x46, starting transfers between devices, xor_permute(): return lax.ppermute(x, axis, [(i, i ^ bits) for i in range(size)])  55.4 us
    pallas_call x2, Pallas kernels, back_project(): pl.pallas_call(functools.partial(back_body, first=first, width=width), in...  42.4 us
    pallas_call x2, Pallas kernels, orthonormal(): pl.pallas_call(basis_body, in_specs=[VMEM] * 3, out_specs=VMEM, out_shape...  11.3 us
    unnamed x68, local copies, waits for them, and re-layouts  10.1 us
  transfers between devices with their start and end apart: 49, of which 26 were waited for; matrix products, arithmetic and copies ran while one was open for 2% of the time, Pallas kernels for 26%

profile of v1, /device:TPU:0, one launch (start us, length us, event | category | flops | bytes accessed | tf_op | source)
XLA Modules:
  0.0 352.3 jit_solution(8456984588883576085)
XLA Ops:
  7.6 13.0 %collective-permute-done.7.mine_ref = bf16[16,7168]{1,0:T(8,128)(2,1)S(1)} collective-permute-done((bf16[16,7168]{1,0:T(8,128)(2,1)}, bf16[16,7168]{1,0:T(8,128)(2,1)S(1)}, u32[]{:S(2)}, u32[]{:S(2)}) %collective-permute-start.7) | collective-permute-done | bytes 229408 | tf_op jit(solution)/shard_map/ppermute | solution.py:228
  23.1 8.9 %shard_map.46.rest_0_ = f32[2,32,1024]{2,1,0:T(8,128)} custom-call(s32[2]{0:T(128)} %pad_add_fusion.where, bf16[16,7168]{1,0:T(8,128)(2,1)} %bitcast.33, bf16[16,7168]{1,0:T(8,128)(2,1)} %copy-done.19, bf16[4,1024,7168]{2,1,0:T(8,128)(2,1)} %grads_ref.19), custom_call_target="tpu_custom_call" | custom-call | flops 3758096384 | bytes 14680064 | tf_op jit(solution)/shard_map/pallas_call | solution.py:62
  32.7 9.0 %shard_map.47 = f32[2,32,1024]{2,1,0:T(8,128)} custom-call(s32[2]{0:T(128)} %pad_add_fusion.1.where, bf16[16,7168]{1,0:T(8,128)(2,1)} %copy-done.18, bf16[16,7168]{1,0:T(8,128)(2,1)} %copy-done.29, bf16[4,1024,7168]{2,1,0:T(8,128)(2,1)} %grads_ref.19, f32[2,32,1024]{2,1,0:T(8,128)} %shard_map.46.rest_0_), custom_call_target="tpu_custom_call", output_to_operand_aliasing={{}: (4, {})} | custom-call | flops 3758096384 | bytes 14680064 | tf_op jit(solution)/shard_map/pallas_call | solution.py:62
  44.0 8.9 %shard_map.48.rest_0_ = f32[2,32,1024]{2,1,0:T(8,128)} custom-call(s32[2]{0:T(128)} %get-tuple-element.56.where, bf16[16,7168]{1,0:T(8,128)(2,1)} %copy-done.17, bf16[16,7168]{1,0:T(8,128)(2,1)} %copy-done.25, bf16[4,1024,7168]{2,1,0:T(8,128)(2,1)} %grads_ref.19), custom_call_target="tpu_custom_call" | custom-call | flops 3758096384 | bytes 14680064 | tf_op jit(solution)/shard_map/pallas_call | solution.py:62
  53.6 9.0 %shard_map.49 = f32[2,32,1024]{2,1,0:T(8,128)} custom-call(s32[2]{0:T(128)} %get-tuple-element.55.where, bf16[16,7168]{1,0:T(8,128)(2,1)} %copy-done.16, bf16[16,7168]{1,0:T(8,128)(2,1)} %copy-done.26, bf16[4,1024,7168]{2,1,0:T(8,128)(2,1)} %grads_ref.19, f32[2,32,1024]{2,1,0:T(8,128)} %shard_map.48.rest_0_), custom_call_target="tpu_custom_call", output_to_operand_aliasing={{}: (4, {})} | custom-call | flops 3758096384 | bytes 14680064 | tf_op jit(solution)/shard_map/pallas_call | solution.py:62
  64.8 7.2 %collective-permute-done.9 = f32[2,32,1024]{2,1,0:T(8,128)S(1)} collective-permute-done((f32[2,32,1024]{2,1,0:T(8,128)}, f32[2,32,1024]{2,1,0:T(8,128)S(1)}, u32[]{:S(2)}, u32[]{:S(2)}) %collective-permute-start.9) | collective-permute-done | bytes 262176 | tf_op jit(solution)/shard_map/ppermute | solution.py:228
  96.3 5.7 %shard_map.51.basis_ref = bf16[4,32,1024]{2,1,0:T(8,128)(2,1)} custom-call(f32[32,128]{1,0:T(8,128)} %copy-done.30, f32[32,128]{1,0:T(8,128)} %copy-done.32, f32[4,32,1024]{2,1,0:T(8,128)} %get-tuple-element.22.images_ref), custom_call_target="tpu_custom_call" | custom-call | flops 1050331648 | bytes 786432 | tf_op jit(solution)/shard_map/pallas_call | solution.py:197
  101.9 21.2 %shard_map.52 = (f32[4,16,7168]{2,1,0:T(8,128)}, bf16[4,16,7168]{2,1,0:T(8,128)(2,1)}) custom-call(s32[2]{0:T(128)} %pad_add_fusion.where, bf16[4,32,1024]{2,1,0:T(8,128)(2,1)} %shard_map.51.basis_ref, bf16[4,1024,7168]{2,1,0:T(8,128)(2,1)} %grads_ref.19), custom_call_target="tpu_custom_call" | custom-call | flops 15032385536 | bytes 58720256 | tf_op jit(solution)/shard_map/pallas_call | solution.py:119
  134.1 8.2 %collective-permute-done.15 = bf16[16,7168]{1,0:T(8,128)(2,1)S(1)} collective-permute-done((bf16[16,7168]{1,0:T(8,128)(2,1)}, bf16[16,7168]{1,0:T(8,128)(2,1)S(1)}, u32[]{:S(2)}, u32[]{:S(2)}) %collective-permute-start.15) | collective-permute-done | bytes 229408 | tf_op jit(solution)/shard_map/ppermute | solution.py:228
  142.3 7.9 %collective-permute-done.16 = bf16[16,7168]{1,0:T(8,128)(2,1)S(1)} collective-permute-done((bf16[16,7168]{1,0:T(8,128)(2,1)}, bf16[16,7168]{1,0:T(8,128)(2,1)S(1)}, u32[]{:S(2)}, u32[]{:S(2)}) %collective-permute-start.16) | collective-permute-done | bytes 229408 | tf_op jit(solution)/shard_map/ppermute | solution.py:228
  151.4 6.3 %collective-permute-start.25 = (bf16[16,7168]{1,0:T(8,128)(2,1)S(1)}, bf16[16,7168]{1,0:T(8,128)(2,1)S(1)}, u32[]{:S(2)}, u32[]{:S(2)}) collective-permute-start(bf16[16,7168]{1,0:T(8,128)(2,1)S(1)} %add_convert_fusion.1.mine_ref), channel_id=1, source_target_pairs={{0,16},{4,20},{8,24},{12,28},{16,0},{20,4},{24,8},{28,12},{1,17},{... | collective-permute-start | bytes 688136 | tf_op jit(solution)/shard_map/ppermute | solution.py:228
  158.3 14.4 %collective-permute-done.25.mine_ref = bf16[16,7168]{1,0:T(8,128)(2,1)S(1)} collective-permute-done((bf16[16,7168]{1,0:T(8,128)(2,1)S(1)}, bf16[16,7168]{1,0:T(8,128)(2,1)S(1)}, u32[]{:S(2)}, u32[]{:S(2)}) %collective-permute-start.25) | collective-permute-done | bytes 229408 | tf_op jit(solution)/shard_map/ppermute | solution.py:228
  174.4 8.9 %shard_map.54.rest_0_ = f32[2,32,1024]{2,1,0:T(8,128)} custom-call(s32[2]{0:T(128)} %pad_add_fusion.where, bf16[16,7168]{1,0:T(8,128)(2,1)} %copy-done.11, bf16[16,7168]{1,0:T(8,128)(2,1)} %copy-done.27, bf16[4,1024,7168]{2,1,0:T(8,128)(2,1)} %grads_ref.19), custom_call_target="tpu_custom_call" | custom-call | flops 3758096384 | bytes 14680064 | tf_op jit(solution)/shard_map/pallas_call | solution.py:62
  184.1 9.0 %shard_map.55 = f32[2,32,1024]{2,1,0:T(8,128)} custom-call(s32[2]{0:T(128)} %pad_add_fusion.1.where, bf16[16,7168]{1,0:T(8,128)(2,1)} %copy-done.24, bf16[16,7168]{1,0:T(8,128)(2,1)} %copy-done.28, bf16[4,1024,7168]{2,1,0:T(8,128)(2,1)} %grads_ref.19, f32[2,32,1024]{2,1,0:T(8,128)} %shard_map.54.rest_0_), custom_call_target="tpu_custom_call", output_to_operand_aliasing={{}: (4, {})} | custom-call | flops 3758096384 | bytes 14680064 | tf_op jit(solution)/shard_map/pallas_call | solution.py:62
  194.3 8.9 %shard_map.56.rest_0_ = f32[2,32,1024]{2,1,0:T(8,128)} custom-call(s32[2]{0:T(128)} %get-tuple-element.56.where, bf16[16,7168]{1,0:T(8,128)(2,1)} %copy-done.21, bf16[16,7168]{1,0:T(8,128)(2,1)} %copy-done.22, bf16[4,1024,7168]{2,1,0:T(8,128)(2,1)} %grads_ref.19), custom_call_target="tpu_custom_call" | custom-call | flops 3758096384 | bytes 14680064 | tf_op jit(solution)/shard_map/pallas_call | solution.py:62
  204.0 8.9 %shard_map.57 = f32[2,32,1024]{2,1,0:T(8,128)} custom-call(s32[2]{0:T(128)} %get-tuple-element.55.where, bf16[16,7168]{1,0:T(8,128)(2,1)} %copy-done.20, bf16[16,7168]{1,0:T(8,128)(2,1)} %copy-done.23, bf16[4,1024,7168]{2,1,0:T(8,128)(2,1)} %grads_ref.19, f32[2,32,1024]{2,1,0:T(8,128)} %shard_map.56.rest_0_), custom_call_target="tpu_custom_call", output_to_operand_aliasing={{}: (4, {})} | custom-call | flops 3758096384 | bytes 14680064 | tf_op jit(solution)/shard_map/pallas_call | solution.py:62
  215.1 7.2 %collective-permute-done.27 = f32[2,32,1024]{2,1,0:T(8,128)S(1)} collective-permute-done((f32[2,32,1024]{2,1,0:T(8,128)}, f32[2,32,1024]{2,1,0:T(8,128)S(1)}, u32[]{:S(2)}, u32[]{:S(2)}) %collective-permute-start.27) | collective-permute-done | bytes 262176 | tf_op jit(solution)/shard_map/ppermute | solution.py:228
  246.7 5.7 %shard_map.59.basis_ref = bf16[4,32,1024]{2,1,0:T(8,128)(2,1)} custom-call(f32[32,128]{1,0:T(8,128)} %copy-done.31, f32[32,128]{1,0:T(8,128)} %copy-done.33, f32[4,32,1024]{2,1,0:T(8,128)} %get-tuple-element.30.images_ref), custom_call_target="tpu_custom_call" | custom-call | flops 1050331648 | bytes 786432 | tf_op jit(solution)/shard_map/pallas_call | solution.py:197
  258.6 21.2 %shard_map.60 = (f32[4,16,7168]{2,1,0:T(8,128)}, bf16[4,16,7168]{2,1,0:T(8,128)(2,1)}) custom-call(s32[2]{0:T(128)} %pad_add_fusion.where, bf16[4,32,1024]{2,1,0:T(8,128)(2,1)} %shard_map.59.basis_ref, bf16[4,1024,7168]{2,1,0:T(8,128)(2,1)} %grads_ref.19), custom_call_target="tpu_custom_call" | custom-call | flops 15032385536 | bytes 58720256 | tf_op jit(solution)/shard_map/pallas_call | solution.py:119
  296.0 10.4 %collective-permute-done.38 = bf16[16,7168]{1,0:T(8,128)(2,1)S(1)} collective-permute-done((bf16[16,7168]{1,0:T(8,128)(2,1)}, bf16[16,7168]{1,0:T(8,128)(2,1)S(1)}, u32[]{:S(2)}, u32[]{:S(2)}) %collective-permute-start.38) | collective-permute-done | bytes 229408 | tf_op jit(solution)/shard_map/ppermute | solution.py:228
  307.5 4.7 %collective-permute-start.43 = (bf16[16,7168]{1,0:T(8,128)(2,1)S(1)}, bf16[16,7168]{1,0:T(8,128)(2,1)S(1)}, u32[]{:S(2)}, u32[]{:S(2)}) collective-permute-start(bf16[16,7168]{1,0:T(8,128)(2,1)S(1)} %add_convert_fusion), channel_id=1, source_target_pairs={{0,16},{4,20},{8,24},{12,28},{16,0},{20,4},{24,8},{28,12},{1,17},{... | collective-permute-start | bytes 688136 | tf_op jit(solution)/shard_map/ppermute | solution.py:228
  314.6 9.8 %collective-permute-done.43 = bf16[16,7168]{1,0:T(8,128)(2,1)S(1)} collective-permute-done((bf16[16,7168]{1,0:T(8,128)(2,1)S(1)}, bf16[16,7168]{1,0:T(8,128)(2,1)S(1)}, u32[]{:S(2)}, u32[]{:S(2)}) %collective-permute-start.43) | collective-permute-done | bytes 229408 | tf_op jit(solution)/shard_map/ppermute | solution.py:228
  336.4 7.0 %collective-permute-done.47 = f32[2,4,32,256]{3,2,1,0:T(8,128)S(1)} collective-permute-done((f32[2,4,32,256]{3,2,1,0:T(8,128)S(1)}, f32[2,4,32,256]{3,2,1,0:T(8,128)S(1)}, u32[]{:S(2)}, u32[]{:S(2)}) %collective-permute-start.47) | collective-permute-done | bytes 262176 | tf_op jit(solution)/shard_map/ppermute | solution.py:228
  345.1 6.4 %collective-permute-done.48 = f32[2,4,32,256]{3,2,1,0:T(8,128)S(1)} collective-permute-done((f32[2,4,32,256]{3,2,1,0:T(8,128)S(1)}, f32[2,4,32,256]{3,2,1,0:T(8,128)S(1)}, u32[]{:S(2)}, u32[]{:S(2)}) %collective-permute-start.48) | collective-permute-done | bytes 262176 | tf_op jit(solution)/shard_map/ppermute | solution.py:228
  (191 shorter events, 123.8 us)
Async XLA Ops:
  0.0 20.6 %collective-permute-start.7 = (bf16[16,7168]{1,0:T(8,128)(2,1)}, bf16[16,7168]{1,0:T(8,128)(2,1)S(1)}, u32[]{:S(2)}, u32[]{:S(2)}) collective-permute-start(bf16[16,7168]{1,0:T(8,128)(2,1)} %bitcast.29), channel_id=1, source_target_pairs={{0,16},{4,20},{8,24},{12,28},{16,0},{20,4},{24,8},{28,12},{1,17},{... | collective-permute-start | bytes 688136 | tf_op jit(solution)/shard_map/ppermute | solution.py:228
  4.1 16.5 %collective-permute-start.5 = (bf16[16,7168]{1,0:T(8,128)(2,1)}, bf16[16,7168]{1,0:T(8,128)(2,1)S(1)}, u32[]{:S(2)}, u32[]{:S(2)}) collective-permute-start(bf16[16,7168]{1,0:T(8,128)(2,1)} %bitcast.30), channel_id=1, source_target_pairs={{0,24},{4,28},{8,16},{12,20},{16,8},{20,12},{24,0},{28,4},{1,25},{... | collective-permute-start | bytes 688136 | tf_op jit(solution)/shard_map/ppermute | solution.py:228
  5.4 16.9 %collective-permute-start.2 = (bf16[16,7168]{1,0:T(8,128)(2,1)}, bf16[16,7168]{1,0:T(8,128)(2,1)S(1)}, u32[]{:S(2)}, u32[]{:S(2)}) collective-permute-start(bf16[16,7168]{1,0:T(8,128)(2,1)} %bitcast.31), channel_id=1, source_target_pairs={{0,4},{4,0},{8,12},{12,8},{16,20},{20,16},{24,28},{28,24},{1,5},{5... | collective-permute-start | bytes 688136 | tf_op jit(solution)/shard_map/ppermute | solution.py:228
  5.4 16.9 %collective-permute-start = (bf16[16,7168]{1,0:T(8,128)(2,1)}, bf16[16,7168]{1,0:T(8,128)(2,1)S(1)}, u32[]{:S(2)}, u32[]{:S(2)}) collective-permute-start(bf16[16,7168]{1,0:T(8,128)(2,1)} %bitcast.32), channel_id=1, source_target_pairs={{0,8},{4,12},{8,0},{12,4},{16,24},{20,28},{24,16},{28,20},{1,9},{5... | collective-permute-start | bytes 688136 | tf_op jit(solution)/shard_map/ppermute | solution.py:228
  20.6 22.7 %collective-permute-start.8 = (bf16[16,7168]{1,0:T(8,128)(2,1)S(1)}, bf16[16,7168]{1,0:T(8,128)(2,1)S(1)}, u32[]{:S(2)}, u32[]{:S(2)}) collective-permute-start(bf16[16,7168]{1,0:T(8,128)(2,1)S(1)} %collective-permute-done.7.mine_ref), channel_id=1, source_target_pairs={{0,4},{4,0},{8,12},{12,8},{16,20},{20,16},{24,28},{28,24},{1,5},{5... | collective-permute-start | bytes 688136 | tf_op jit(solution)/shard_map/ppermute | solution.py:228
  20.6 32.3 %collective-permute-start.6 = (bf16[16,7168]{1,0:T(8,128)(2,1)S(1)}, bf16[16,7168]{1,0:T(8,128)(2,1)S(1)}, u32[]{:S(2)}, u32[]{:S(2)}) collective-permute-start(bf16[16,7168]{1,0:T(8,128)(2,1)S(1)} %collective-permute-done.5.mine_ref), channel_id=1, source_target_pairs={{0,4},{4,0},{8,12},{12,8},{16,20},{20,16},{24,28},{28,24},{1,5},{5... | collective-permute-start | bytes 688136 | tf_op jit(solution)/shard_map/ppermute | solution.py:228
  41.7 22.5 %collective-permute-start.3 = (f32[2,32,1024]{2,1,0:T(8,128)}, f32[2,32,1024]{2,1,0:T(8,128)S(1)}, u32[]{:S(2)}, u32[]{:S(2)}) collective-permute-start(f32[2,32,1024]{2,1,0:T(8,128)} %shard_map.47), channel_id=1, source_target_pairs={{0,1},{1,0},{2,3},{3,2},{4,5},{5,4},{6,7},{7,6},{8,9},{9,8},{10,11... | collective-permute-start | bytes 786440 | tf_op jit(solution)/shard_map/ppermute | solution.py:228
  130.8 19.4 %collective-permute-start.16 = (bf16[16,7168]{1,0:T(8,128)(2,1)}, bf16[16,7168]{1,0:T(8,128)(2,1)S(1)}, u32[]{:S(2)}, u32[]{:S(2)}) collective-permute-start(bf16[16,7168]{1,0:T(8,128)(2,1)} %get-tuple-element.27), channel_id=1, source_target_pairs={{0,16},{4,20},{8,24},{12,28},{16,0},{20,4},{24,8},{28,12},{1,17},{... | collective-permute-start | bytes 688136 | tf_op jit(solution)/shard_map/ppermute | solution.py:228
  132.6 17.6 %collective-permute-start.17 = (bf16[16,7168]{1,0:T(8,128)(2,1)}, bf16[16,7168]{1,0:T(8,128)(2,1)S(1)}, u32[]{:S(2)}, u32[]{:S(2)}) collective-permute-start(bf16[16,7168]{1,0:T(8,128)(2,1)} %get-tuple-element.28), channel_id=1, source_target_pairs={{0,24},{4,28},{8,16},{12,20},{16,8},{20,12},{24,0},{28,4},{1,25},{... | collective-permute-start | bytes 688136 | tf_op jit(solution)/shard_map/ppermute | solution.py:228
  151.4 21.3 %collective-permute-start.25 = (bf16[16,7168]{1,0:T(8,128)(2,1)S(1)}, bf16[16,7168]{1,0:T(8,128)(2,1)S(1)}, u32[]{:S(2)}, u32[]{:S(2)}) collective-permute-start(bf16[16,7168]{1,0:T(8,128)(2,1)S(1)} %add_convert_fusion.1.mine_ref), channel_id=1, source_target_pairs={{0,16},{4,20},{8,24},{12,28},{16,0},{20,4},{24,8},{28,12},{1,17},{... | collective-permute-start | bytes 688136 | tf_op jit(solution)/shard_map/ppermute | solution.py:228
  157.7 15.1 %collective-permute-start.23 = (bf16[16,7168]{1,0:T(8,128)(2,1)S(1)}, bf16[16,7168]{1,0:T(8,128)(2,1)S(1)}, u32[]{:S(2)}, u32[]{:S(2)}) collective-permute-start(bf16[16,7168]{1,0:T(8,128)(2,1)S(1)} %add_convert_fusion.1.mine_ref), channel_id=1, source_target_pairs={{0,24},{4,28},{8,16},{12,20},{16,8},{20,12},{24,0},{28,4},{1,25},{... | collective-permute-start | bytes 688136 | tf_op jit(solution)/shard_map/ppermute | solution.py:228
  158.2 15.5 %collective-permute-start.18 = (bf16[16,7168]{1,0:T(8,128)(2,1)S(1)}, bf16[16,7168]{1,0:T(8,128)(2,1)S(1)}, u32[]{:S(2)}, u32[]{:S(2)}) collective-permute-start(bf16[16,7168]{1,0:T(8,128)(2,1)S(1)} %add_convert_fusion.1.mine_ref), channel_id=1, source_target_pairs={{0,8},{4,12},{8,0},{12,4},{16,24},{20,28},{24,16},{28,20},{1,9},{5... | collective-permute-start | bytes 688136 | tf_op jit(solution)/shard_map/ppermute | solution.py:228
  158.3 15.4 %collective-permute-start.20 = (bf16[16,7168]{1,0:T(8,128)(2,1)S(1)}, bf16[16,7168]{1,0:T(8,128)(2,1)S(1)}, u32[]{:S(2)}, u32[]{:S(2)}) collective-permute-start(bf16[16,7168]{1,0:T(8,128)(2,1)S(1)} %add_convert_fusion.1.mine_ref), channel_id=1, source_target_pairs={{0,4},{4,0},{8,12},{12,8},{16,20},{20,16},{24,28},{28,24},{1,5},{5... | collective-permute-start | bytes 688136 | tf_op jit(solution)/shard_map/ppermute | solution.py:228
  172.7 20.9 %collective-permute-start.26 = (bf16[16,7168]{1,0:T(8,128)(2,1)S(1)}, bf16[16,7168]{1,0:T(8,128)(2,1)S(1)}, u32[]{:S(2)}, u32[]{:S(2)}) collective-permute-start(bf16[16,7168]{1,0:T(8,128)(2,1)S(1)} %collective-permute-done.25.mine_ref), channel_id=1, source_target_pairs={{0,4},{4,0},{8,12},{12,8},{16,20},{20,16},{24,28},{28,24},{1,5},{5... | collective-permute-start | bytes 688136 | tf_op jit(solution)/shard_map/ppermute | solution.py:228
  172.7 30.6 %collective-permute-start.24 = (bf16[16,7168]{1,0:T(8,128)(2,1)S(1)}, bf16[16,7168]{1,0:T(8,128)(2,1)S(1)}, u32[]{:S(2)}, u32[]{:S(2)}) collective-permute-start(bf16[16,7168]{1,0:T(8,128)(2,1)S(1)} %collective-permute-done.23.mine_ref), channel_id=1, source_target_pairs={{0,4},{4,0},{8,12},{12,8},{16,20},{20,16},{24,28},{28,24},{1,5},{5... | collective-permute-start | bytes 688136 | tf_op jit(solution)/shard_map/ppermute | solution.py:228
  193.0 21.5 %collective-permute-start.21 = (f32[2,32,1024]{2,1,0:T(8,128)}, f32[2,32,1024]{2,1,0:T(8,128)S(1)}, u32[]{:S(2)}, u32[]{:S(2)}) collective-permute-start(f32[2,32,1024]{2,1,0:T(8,128)} %shard_map.55), channel_id=1, source_target_pairs={{0,1},{1,0},{2,3},{3,2},{4,5},{5,4},{6,7},{7,6},{8,9},{9,8},{10,11... | collective-permute-start | bytes 786440 | tf_op jit(solution)/shard_map/ppermute | solution.py:228
  252.4 27.6 %collective-permute-start.33 = (bf16[128,1024]{1,0:T(8,128)(2,1)}, bf16[128,1024]{1,0:T(8,128)(2,1)S(1)}, u32[]{:S(2)}, u32[]{:S(2)}) collective-permute-start(bf16[128,1024]{1,0:T(8,128)(2,1)} %bitcast.26), channel_id=1, source_target_pairs={{0,16},{4,20},{9,25},{13,29},{18,2},{22,6},{27,11},{31,15}} | collective-permute-start | bytes 786440 | tf_op jit(solution)/shard_map/ppermute | solution.py:289
  255.5 24.4 %collective-permute-start.32 = (bf16[128,1024]{1,0:T(8,128)(2,1)}, bf16[128,1024]{1,0:T(8,128)(2,1)S(1)}, u32[]{:S(2)}, u32[]{:S(2)}) collective-permute-start(bf16[128,1024]{1,0:T(8,128)(2,1)} %bitcast.27), channel_id=1, source_target_pairs={{0,8},{4,12},{9,1},{13,5},{18,26},{22,30},{27,19},{31,23}} | collective-permute-start | bytes 786440 | tf_op jit(solution)/shard_map/ppermute | solution.py:289
  257.1 22.8 %collective-permute-start.34 = (bf16[128,1024]{1,0:T(8,128)(2,1)}, bf16[128,1024]{1,0:T(8,128)(2,1)S(1)}, u32[]{:S(2)}, u32[]{:S(2)}) collective-permute-start(bf16[128,1024]{1,0:T(8,128)(2,1)} %bitcast.28), channel_id=1, source_target_pairs={{0,24},{4,28},{9,17},{13,21},{18,10},{22,14},{27,3},{31,7}} | collective-permute-start | bytes 786440 | tf_op jit(solution)/shard_map/ppermute | solution.py:289
  286.8 19.5 %collective-permute-start.38 = (bf16[16,7168]{1,0:T(8,128)(2,1)}, bf16[16,7168]{1,0:T(8,128)(2,1)S(1)}, u32[]{:S(2)}, u32[]{:S(2)}) collective-permute-start(bf16[16,7168]{1,0:T(8,128)(2,1)} %get-tuple-element.35), channel_id=1, source_target_pairs={{0,16},{4,20},{8,24},{12,28},{16,0},{20,4},{24,8},{28,12},{1,17},{... | collective-permute-start | bytes 688136 | tf_op jit(solution)/shard_map/ppermute | solution.py:228
  286.9 19.4 %collective-permute-start.39 = (bf16[16,7168]{1,0:T(8,128)(2,1)}, bf16[16,7168]{1,0:T(8,128)(2,1)S(1)}, u32[]{:S(2)}, u32[]{:S(2)}) collective-permute-start(bf16[16,7168]{1,0:T(8,128)(2,1)} %get-tuple-element.36), channel_id=1, source_target_pairs={{0,24},{4,28},{8,16},{12,20},{16,8},{20,12},{24,0},{28,4},{1,25},{... | collective-permute-start | bytes 688136 | tf_op jit(solution)/shard_map/ppermute | solution.py:228
  307.5 16.9 %collective-permute-start.43 = (bf16[16,7168]{1,0:T(8,128)(2,1)S(1)}, bf16[16,7168]{1,0:T(8,128)(2,1)S(1)}, u32[]{:S(2)}, u32[]{:S(2)}) collective-permute-start(bf16[16,7168]{1,0:T(8,128)(2,1)S(1)} %add_convert_fusion), channel_id=1, source_target_pairs={{0,16},{4,20},{8,24},{12,28},{16,0},{20,4},{24,8},{28,12},{1,17},{... | collective-permute-start | bytes 688136 | tf_op jit(solution)/shard_map/ppermute | solution.py:228
  312.3 17.0 %collective-permute-start.45 = (bf16[16,7168]{1,0:T(8,128)(2,1)S(1)}, bf16[16,7168]{1,0:T(8,128)(2,1)S(1)}, u32[]{:S(2)}, u32[]{:S(2)}) collective-permute-start(bf16[16,7168]{1,0:T(8,128)(2,1)S(1)} %add_convert_fusion), channel_id=1, source_target_pairs={{0,24},{4,28},{8,16},{12,20},{16,8},{20,12},{24,0},{28,4},{1,25},{... | collective-permute-start | bytes 688136 | tf_op jit(solution)/shard_map/ppermute | solution.py:228
  314.6 14.7 %collective-permute-start.40 = (bf16[16,7168]{1,0:T(8,128)(2,1)S(1)}, bf16[16,7168]{1,0:T(8,128)(2,1)S(1)}, u32[]{:S(2)}, u32[]{:S(2)}) collective-permute-start(bf16[16,7168]{1,0:T(8,128)(2,1)S(1)} %add_convert_fusion), channel_id=1, source_target_pairs={{0,4},{4,0},{8,12},{12,8},{16,20},{20,16},{24,28},{28,24},{1,5},{5... | collective-permute-start | bytes 688136 | tf_op jit(solution)/shard_map/ppermute | solution.py:228
  (59 other events, 718.7 us)

commit v2 on v1

v2 whole, which is shorter than its diff:
```python
import functools
import jax
import jax.numpy as jnp
from jax import lax
from jax.experimental import pallas as pl
from jax.experimental.pallas import tpu as pltpu
from jax.sharding import PartitionSpec as P

RANK = 32
ITERS = 2
CORES = 2
F32, BF16 = jnp.float32, jnp.bfloat16
HIGH = lax.Precision.HIGHEST
NT = (((1,), (1,)), ((), ()))
ANY = pl.BlockSpec(memory_space=pl.ANY)
VMEM = pl.BlockSpec(memory_space=pltpu.VMEM)
SMEM = pl.BlockSpec(memory_space=pltpu.SMEM)
MIB = 1024 * 1024


def params(mebibytes=4):
    return pltpu.CompilerParams(vmem_limit_bytes=mebibytes * MIB)


def cost(flops, nbytes):
    return pl.CostEstimate(flops=int(flops), bytes_accessed=int(nbytes), transcendentals=0)


ROW_CHUNKS = 4
COL_CHUNKS = 8
STREAM_BANDS = 2
STREAM_COLS = 4
STREAMED = 1


def images_body(where, mine_ref, other_ref, grads_ref, *rest, mode, aliased, offset):
    out_ref, *rest = rest[1:] if aliased else rest
    query, core = where[0] ^ offset, where[1]
    rows = out_ref.shape[2] // ROW_CHUNKS

    def band(i):
        return pl.ds(pl.multiple_of(i * rows, 128), rows)

    def view(i):
        if mode == "stream":
            return rest[0].at[lax.rem(i, STREAM_BANDS)]
        return (grads_ref if mode == "held" else rest[0]).at[band(i), :]

    def fetch(i):
        return pltpu.make_async_copy(grads_ref.at[query, band(i), :], view(i), rest[1].at[i])

    if mode != "held":
        for i in range(STREAM_BANDS if mode == "stream" else ROW_CHUNKS):
            fetch(i).start()
    mine, other = mine_ref[...], other_ref[...]
    vectors = jnp.concatenate(
        [jnp.where(core == 0, mine, other), jnp.where(core == 0, other, mine)], axis=0
    )

    def body(i, carry):
        if mode != "held":
            fetch(i).wait()
        out_ref[0, :, band(i)] = lax.dot_general(
            vectors, view(i)[...], NT, preferred_element_type=F32
        )
        if mode == "stream":

            @pl.when(i + STREAM_BANDS < ROW_CHUNKS)
            def _():
                fetch(i + STREAM_BANDS).start()

        return carry

    lax.fori_loop(0, ROW_CHUNKS, body, 0)


def images_of_query(where, offset, mine, other, grads, mode, slot, slots, earlier=None):
    rows, cols = grads.shape[-2:]
    aliased, load = earlier is not None, mode == "load"
    scratch = []
    if mode == "stream":
        scratch.append(pltpu.VMEM((STREAM_BANDS, rows // ROW_CHUNKS, cols), BF16))
    if mode != "held":
        scratch.append(pltpu.SemaphoreType.DMA((ROW_CHUNKS,)))
    return pl.pallas_call(
        functools.partial(images_body, mode=mode, aliased=aliased, offset=offset),
        grid=(1,),
        in_specs=[SMEM, VMEM, VMEM, VMEM if mode == "held" else ANY] + [ANY] * aliased,
        out_specs=[pl.BlockSpec((1, RANK, rows), lambda i: (slot, 0, 0))] + [VMEM] * load,
        out_shape=[jax.ShapeDtypeStruct((slots, RANK, rows), F32)]
        + [pltpu.VMEM((rows, cols), BF16)] * load,
        scratch_shapes=scratch,
        input_output_aliases={4: 0} if aliased else {},
        cost_estimate=cost(2 * RANK * rows * cols * 8, 2 * rows * cols),
        compiler_params=params(12 if mode == "stream" else 3),
    )(where, mine, other, grads, *([earlier] if aliased else []))


def back_body(where, basis_ref, grads_ref, *rest, stream, ties, offset):
    mine_ref, other_ref, *rest = rest[ties:]
    query, core = where[0] ^ offset, where[1]
    half = mine_ref.shape[0]
    width = mine_ref.shape[1] // COL_CHUNKS
    vectors = basis_ref[query]

    def band(i):
        return pl.ds(pl.multiple_of(i * width, 128), width)

    def view(i):
        return rest[0].at[lax.rem(i, STREAM_COLS)] if stream else grads_ref.at[:, band(i)]

    def fetch(i):
        return pltpu.make_async_copy(grads_ref.at[query, :, band(i)], view(i), rest[1].at[i])

    if stream:
        for i in range(STREAM_COLS):
            fetch(i).start()

    def body(i, carry):
        if stream:
            fetch(i).wait()
        product = jnp.dot(vectors, view(i)[...], preferred_element_type=F32)
        low, high = product[:half], product[half:]
        mine_ref[:, band(i)] = jnp.where(core == 0, low, high)
        other_ref[:, band(i)] = jnp.where(core == 0, high, low).astype(BF16)
        if stream:

            @pl.when(i + STREAM_COLS < COL_CHUNKS)
            def _():
                fetch(i + STREAM_COLS).start()

        return carry

    lax.fori_loop(0, COL_CHUNKS, body, 0)


def back_of_query(where, offset, basis, grads, after):
    rows, cols = grads.shape[-2:]
    stream = grads.ndim == 3
    half = RANK // CORES
    scratch = [
        pltpu.VMEM((STREAM_COLS, rows, cols // COL_CHUNKS), BF16),
        pltpu.SemaphoreType.DMA((COL_CHUNKS,)),
    ]
    return pl.pallas_call(
        functools.partial(back_body, stream=stream, ties=len(after), offset=offset),
        in_specs=[SMEM, VMEM, ANY if stream else VMEM] + [ANY] * len(after),
        out_specs=[VMEM, VMEM],
        out_shape=[
            jax.ShapeDtypeStruct((half, cols), F32),
            jax.ShapeDtypeStruct((half, cols), BF16),
        ],
        scratch_shapes=scratch if stream else [],
        cost_estimate=cost(2 * RANK * rows * cols * 8, 2 * rows * cols),
        compiler_params=params(12 if stream else 3),
    )(where, basis, grads, *after)


def gram_body(where, *refs):
    pairs, (images_ref, gram_ref) = refs[:-2], refs[-2:]
    chip = where[0]
    queries = images_ref.shape[0]
    slot = 0
    for held, received in zip(pairs[0::2], pairs[1::2]):
        for i in range(held.shape[0]):
            images_ref[chip ^ slot] = held[i] + received[i]
            slot += 1
    for query in range(queries):
        block = images_ref[query]
        gram_ref[:, query * RANK : (query + 1) * RANK] = lax.dot_general(
            block, block, NT, precision=HIGH, preferred_element_type=F32
        )


def local_gram(where, pairs):
    flat = [part for pair in pairs for part in pair]
    queries = sum(held.shape[0] for held, _ in pairs)
    rows = flat[0].shape[2]
    return pl.pallas_call(
        gram_body,
        in_specs=[SMEM] + [VMEM] * len(flat),
        out_specs=[VMEM, VMEM],
        out_shape=[
            jax.ShapeDtypeStruct((queries, RANK, rows), F32),
            jax.ShapeDtypeStruct((RANK, queries * RANK), F32),
        ],
        cost_estimate=cost(12 * RANK * RANK * queries * rows, 16 * queries * RANK * rows),
        compiler_params=params(),
    )(where, *flat)


def basis_body(images_ref, *refs):
    gram_refs, basis_ref = refs[:-1], refs[-1]
    queries = images_ref.shape[0]
    total = queries * RANK
    gram = gram_refs[0][...]
    for ref in gram_refs[1:]:
        gram = gram + ref[...]
    stacked = jnp.concatenate(
        [gram[:, q * RANK : (q + 1) * RANK] for q in range(queries)], axis=0
    )
    row = lax.broadcasted_iota(jnp.int32, (total, RANK), 0) % RANK
    col = lax.broadcasted_iota(jnp.int32, (total, RANK), 1)
    table = jnp.concatenate([stacked, jnp.where(row == col, 1.0, 0.0).astype(F32)], axis=1)
    row = lax.broadcasted_iota(jnp.int32, (total, 2 * RANK), 0) % RANK
    table = table.reshape(queries, RANK, 2 * RANK)
    row = row.reshape(queries, RANK, 2 * RANK)
    scales = jnp.zeros((queries, RANK, 1), F32)
    for k in range(RANK):
        pivot_row = table[:, k : k + 1, :]
        pivot = pivot_row[:, :, k : k + 1]
        factor = table[:, :, k : k + 1] / pivot
        scales = jnp.where(row[:, :, :1] == k, lax.rsqrt(pivot), scales)
        table = table - jnp.where(row > k, factor * pivot_row, 0.0)
    inverse = table[:, :, RANK:] * scales
    for q in range(queries):
        basis_ref[q] = jnp.dot(
            inverse[q], images_ref[q], precision=HIGH, preferred_element_type=F32
        ).astype(BF16)


def orthonormal(images, grams):
    return pl.pallas_call(
        basis_body,
        in_specs=[VMEM] * (1 + len(grams)),
        out_specs=VMEM,
        out_shape=jax.ShapeDtypeStruct(images.shape, BF16),
        cost_estimate=cost(12 * RANK * images.size + 10**9, 6 * images.size),
        compiler_params=params(),
    )(images, *grams)


def choose_body(where, held_ref, received_ref, out_ref, *, owners):
    wanted = where[2]
    own = functools.reduce(jnp.logical_or, [where[0] == wanted ^ bits for bits in owners])
    out_ref[...] = jnp.where(own, held_ref[...], received_ref[...])


def choose(where, held, received, owners):
    return pl.pallas_call(
        functools.partial(choose_body, owners=owners),
        in_specs=[SMEM, VMEM, VMEM],
        out_specs=VMEM,
        out_shape=jax.ShapeDtypeStruct(held.shape, held.dtype),
        cost_estimate=cost(held.size, 6 * held.size),
        compiler_params=params(),
    )(where, held, received)


def both_cores(core, mine, other, axis):
    return jnp.concatenate(
        [jnp.where(core == 0, mine, other), jnp.where(core == 0, other, mine)], axis=axis
    )


def project_out_body(where, mine_ref, other_ref, hooked_ref, out_ref, scratch):
    vectors = both_cores(where[1], mine_ref[...], other_ref[...], 1)
    queries = scratch.shape[0]
    scratch[...] = lax.dot_general(
        vectors, hooked_ref[...], NT, preferred_element_type=F32
    ).reshape(scratch.shape)
    for d in range(queries):
        out_ref[d] = scratch[where[0] ^ d]


def project_out(where, mine, other, hooked):
    shape = (mine.shape[0] // RANK, RANK, hooked.shape[0])
    return pl.pallas_call(
        project_out_body,
        in_specs=[SMEM, VMEM, VMEM, VMEM],
        out_specs=VMEM,
        out_shape=jax.ShapeDtypeStruct(shape, F32),
        scratch_shapes=[pltpu.VMEM(shape, F32)],
        cost_estimate=cost(4 * mine.size * hooked.shape[0], 2 * hooked.size),
        compiler_params=params(),
    )(where, mine, other, hooked)


def project_in_body(where, mine_ref, other_ref, hooked_ref, *rest):
    vectors = both_cores(where[1], mine_ref[...], other_ref[...], 0)
    rest[-1][0] = lax.dot_general(vectors, hooked_ref[...], NT, preferred_element_type=F32)


def project_in(where, mine, other, hooked, slot, slots, earlier=None):
    tokens = hooked.shape[0]
    aliased = earlier is not None
    return pl.pallas_call(
        project_in_body,
        grid=(1,),
        in_specs=[SMEM, VMEM, VMEM, VMEM] + [ANY] * aliased,
        out_specs=pl.BlockSpec((1, RANK, tokens), lambda i: (slot, 0, 0)),
        out_shape=jax.ShapeDtypeStruct((slots, RANK, tokens), F32),
        input_output_aliases={4: 0} if aliased else {},
        cost_estimate=cost(4 * mine.size * tokens, 2 * hooked.size),
        compiler_params=params(),
    )(where, mine, other, hooked, *([earlier] if aliased else []))


def scores_body(where, *refs):
    sums, score_ref = [], refs[-1]
    for held_ref, received_ref in zip(refs[:-1:2], refs[1:-1:2]):
        sums += [held_ref[i] + received_ref[i] for i in range(held_ref.shape[0])]
    queries = len(sums) // 2
    for d in range(queries):
        score = (sums[d] * sums[queries + d]).sum(axis=0, keepdims=True)
        score_ref[pl.ds(where[0] ^ d, 1), :] = score


def token_scores(where, pairs):
    flat = [part for pair in pairs for part in pair]
    queries = sum(held.shape[0] for held, _ in pairs) // 2
    return pl.pallas_call(
        scores_body,
        in_specs=[SMEM] + [VMEM] * len(flat),
        out_specs=VMEM,
        out_shape=jax.ShapeDtypeStruct((queries, flat[0].shape[2]), F32),
        compiler_params=params(),
    )(where, *flat)


def xor_permute(x, axis, size, bits):
    return lax.ppermute(x, axis, [(i, i ^ bits) for i in range(size)])


def fast(query_grads, start_block, hooked_out, hooked_in, *, toks, pars):
    queries, rows, _ = query_grads.shape
    chips = toks // CORES
    tok, par = lax.axis_index("tok"), lax.axis_index("par")
    chip, core = tok // CORES, tok % CORES
    where = jnp.stack([chip, core, par]).astype(jnp.int32)
    par_bits = [1 << i for i in range(pars.bit_length() - 1)]
    held = [query_grads] * chips

    def tok_swap(x, bits):
        return xor_permute(x, "tok", toks, bits)

    def par_pair(x):
        for b in par_bits[:-1]:
            x = x + xor_permute(x, "par", pars, b)
        return x, xor_permute(x, "par", pars, par_bits[-1])

    def gathered(piece, step):
        pieces = [piece] + [tok_swap(piece, CORES * d) for d in range(1, chips)]
        for d in range(chips):
            other = tok_swap(pieces[d], 1)
            step(d, pieces[d], other)

    def images_from(piece):
        done = []

        def step(d, mine, other):
            earlier = done[-1] if d % 2 else None
            if d < STREAMED:
                mode = "stream"
            else:
                mode = "load" if held[d] is query_grads else "held"
            images, *block = images_of_query(
                where, d, mine, other, held[d], mode, d % 2, 2, earlier
            )
            held[d] = block[0] if block else held[d]
            done.append(images)

        gathered(piece, step)
        return [par_pair(part) for part in done[1::2]]

    def basis_from(pairs):
        images, gram = local_gram(where, pairs)
        gram = gram + tok_swap(gram, 1)
        others = [tok_swap(gram, CORES * d) for d in range(1, chips)]
        return orthonormal(images, [gram] + others)

    def back_piece(basis):
        after, arrived, total = [], [], None
        for d in reversed(range(chips)):
            mine, other = back_of_query(where, d, basis, held[d], after)
            after = [other]
            total = mine + tok_swap(other, 1).astype(F32)
            if d:
                arrived.append(tok_swap(total.astype(BF16), CORES * d))
        for part in arrived:
            total = total + part.astype(F32)
        return total.astype(BF16)

    piece = start_block.T
    basis = None
    for _ in range(ITERS):
        basis = basis_from(images_from(piece))
        piece = back_piece(basis)

    got = flat = basis.reshape(queries * RANK, rows)
    owners = [0]
    for bits in [1 << i for i in reversed(range(chips.bit_length() - 1))]:
        sends = [
            (((p ^ o) * CORES + c) * pars + p, ((p ^ o ^ bits) * CORES + c) * pars + p)
            for p in range(pars)
            for o in owners
            for c in range(CORES)
        ]
        received = lax.ppermute(got, ("tok", "par"), sends)
        got = choose(where, got, received, owners)
        owners = owners + [o ^ bits for o in owners]
    out_proj = project_out(where, got, tok_swap(got, 1), hooked_out)

    parts = []

    def in_proj(d, mine, other):
        earlier = parts[-1] if d > 1 else None
        slot, slots = max(d - 1, 0), chips - 1 if d else 1
        parts.append(project_in(where, mine, other, hooked_in, slot, slots, earlier))

    gathered(piece, in_proj)
    pairs = [par_pair(out_proj), par_pair(parts[0]), par_pair(parts[-1])]
    return token_scores(where, pairs)


def plain(query_grads, start_block, hooked_out, hooked_in):
    queries, rows_tok = query_grads.shape[:2]
    cols_par = hooked_out.shape[1]

    def blocked(x):
        return x.reshape(x.shape[0], queries, RANK)

    subspace = lax.all_gather(start_block, "tok", axis=1, tiled=True)
    basis = None
    for _ in range(ITERS):
        partial = jnp.einsum(
            "qoi,iqr->oqr", query_grads, blocked(subspace), preferred_element_type=F32
        )
        images = lax.psum(partial.reshape(rows_tok, queries * RANK), "par")
        blocks = blocked(images)
        gram = lax.psum(jnp.einsum("oqr,oqs->qrs", blocks, blocks, precision=HIGH), "tok")
        solved = lax.linalg.triangular_solve(
            jnp.linalg.cholesky(gram), jnp.transpose(blocks, (1, 2, 0)), left_side=True, lower=True
        )
        basis = jnp.transpose(solved, (2, 0, 1)).reshape(images.shape).astype(BF16)
        back = jnp.einsum(
            "qoi,oqr->iqr", query_grads, blocked(basis), preferred_element_type=F32
        )
        subspace = lax.psum(back.reshape(back.shape[0], queries * RANK), "tok").astype(BF16)
    gathered = lax.all_gather(basis, "tok", axis=0, tiled=True)
    basis_par = lax.dynamic_slice_in_dim(gathered, lax.axis_index("par") * cols_par, cols_par, 0)
    out_proj = jnp.dot(hooked_out, basis_par, preferred_element_type=F32)
    in_proj = jnp.dot(hooked_in, subspace, preferred_element_type=F32)
    whole_out, whole_in = lax.psum((out_proj, in_proj), "par")
    return (whole_out * whole_in).reshape(whole_out.shape[0], queries, RANK).sum(axis=2).T


def solution(mesh):
    toks, pars = mesh.shape["tok"], mesh.shape["par"]
    placed = (P(None, "tok", "par"), P("par", "tok"), P("tok", "par"), P("tok", "par"))

    def mapped(body):
        return jax.shard_map(
            body, mesh=mesh, in_specs=placed, out_specs=P(None, "tok"), check_vma=False
        )

    def suited(queries):
        return toks == CORES * queries == CORES * pars == 8

    paired = mapped(functools.partial(fast, toks=toks, pars=pars))

    def step(query_grads, *others):
        run = paired if suited(query_grads.shape[0]) else mapped(plain)
        return run(query_grads, *others)

    return step
```

time: 354 us -> 295 us (0.83)
  Pallas kernels: 136 us -> 111 us
  waiting for transfers between devices: 130 us -> 119 us
  local copies, waits for them, and re-layouts: 10.1 us -> 0.95 us
  other arithmetic: 8.71 us -> 0.76 us
  matrix products: 5.23 us -> 0 us
    pallas_call x14 -> x26, Pallas kernels: 131 us -> 108 us  [the longest x8 54.2 us: images_of_query(): pl.pallas_call(functools.partial(images_body, mode=mode, aliased=aliased,...]
    ppermute x46 -> x58, waiting for transfers between devices: 130 us -> 119 us  [xor_permute(): return lax.ppermute(x, axis, [(i, i ^ bits) for i in range(size)])]
    unnamed x68 -> x6, local copies, waits for them, and re-layouts: 10.1 us -> 0.95 us
    dot_general x5 -> x0, matrix products: 5.23 us -> none  [the longest x4 4.75 us: fast(): lax.dot_general(both, hooked_in, NT, preferred_element_type=F32)]
    ppermute x46 -> x58, starting transfers between devices: 55.4 us -> 57.6 us  [xor_permute(): return lax.ppermute(x, axis, [(i, i ^ bits) for i in range(size)])]
  transfers between devices with their start and end apart: 49 -> 60, of which waited for: 26 -> 23; matrix products, arithmetic and copies ran while one was open for 2% -> 0% of each run, Pallas kernels for 26% -> 29%
where the time goes in v2:
time: 295 us; the launch traced here: 294 us
  waiting for transfers between devices  119 us (40%)
  Pallas kernels  111 us (38%)
  starting transfers between devices  62 us (21%)
    ppermute x58, waiting for transfers between devices, xor_permute(): return lax.ppermute(x, axis, [(i, i ^ bits) for i in range(size)])  119 us
    ppermute x58, starting transfers between devices, xor_permute(): return lax.ppermute(x, axis, [(i, i ^ bits) for i in range(size)])  57.6 us
    pallas_call x8, Pallas kernels, images_of_query(): pl.pallas_call(functools.partial(images_body, mode=mode, aliased=aliased,...  54.2 us
    pallas_call x8, Pallas kernels, back_of_query(): pl.pallas_call(functools.partial(back_body, stream=stream, ties=len(after...  36.5 us
    pallas_call x2, Pallas kernels, orthonormal(): pl.pallas_call(basis_body, in_specs=[VMEM] * (1 + len(grams)), out_specs=...  7.72 us
    pallas_call x4, Pallas kernels, project_in(): pl.pallas_call(project_in_body, grid=(1,), in_specs=[SMEM, VMEM, VMEM, VM...  6.67 us
  transfers between devices with their start and end apart: 60, of which 23 were waited for; matrix products, arithmetic and copies ran while one was open for 0% of the time, Pallas kernels for 29%

profile of v2, /device:TPU:0, one launch (start us, length us, event | category | flops | bytes accessed | tf_op | source)
XLA Modules:
  0.0 294.0 jit_solution(17024208706721474868)
XLA Ops:
  5.7 14.9 %collective-permute-done.7.mine_ref = bf16[16,7168]{1,0:T(8,128)(2,1)S(1)} collective-permute-done((bf16[16,7168]{1,0:T(8,128)(2,1)}, bf16[16,7168]{1,0:T(8,128)(2,1)S(1)}, u32[]{:S(2)}, u32[]{:S(2)}) %collective-permute-start.7) | collective-permute-done | bytes 229408 | tf_op jit(solution)/shard_map/ppermute | solution.py:322
  22.1 8.3 %shard_map.46.rest_0_ = f32[2,32,1024]{2,1,0:T(8,128)S(1)} custom-call(s32[3]{0:T(128)S(1)} %pad_add_fusion.where, bf16[16,7168]{1,0:T(8,128)(2,1)S(1)} %bitcast.11, bf16[16,7168]{1,0:T(8,128)(2,1)S(1)} %collective-permute-done.2.other_ref, bf16[4,1024,7168]{2,1,0:T(8,128)(2,1)} %grads_ref.13), custom_call_target="tpu_custom_call" | custom-call | flops 3758096384 | bytes 14680064 | tf_op jit(solution)/shard_map/pallas_call | solution.py:85
  30.4 7.3 %shard_map.47 = (f32[2,32,1024]{2,1,0:T(8,128)S(1)}, bf16[1024,7168]{1,0:T(8,128)(2,1)S(1)}) custom-call(s32[3]{0:T(128)S(1)} %pad_add_fusion.where, bf16[16,7168]{1,0:T(8,128)(2,1)S(1)} %collective-permute-done.mine_ref, bf16[16,7168]{1,0:T(8,128)(2,1)S(1)} %collective-permute-done.1.other_ref, ...), custom_call_target="tpu_custom_call", output_to_operand_aliasing={{0}: (4, {})} | custom-call | flops 3758096384 | bytes 14680064 | tf_op jit(solution)/shard_map/pallas_call | solution.py:85
  39.6 7.3 %shard_map.48 = (f32[2,32,1024]{2,1,0:T(8,128)S(1)}, bf16[1024,7168]{1,0:T(8,128)(2,1)S(1)}) custom-call(s32[3]{0:T(128)S(1)} %pad_add_fusion.where, bf16[16,7168]{1,0:T(8,128)(2,1)S(1)} %collective-permute-done.7.mine_ref, bf16[16,7168]{1,0:T(8,128)(2,1)S(1)} %collective-permute-done.8.other_ref, bf16[4,1024,7168]{2,1,0:T(8,128)(2,1)} %grads_ref.13), custom_call_target="tpu_custom_call" | custom-call | flops 3758096384 | bytes 14680064 | tf_op jit(solution)/shard_map/pallas_call | solution.py:85
  47.0 7.3 %shard_map.49 = (f32[2,32,1024]{2,1,0:T(8,128)S(1)}, bf16[1024,7168]{1,0:T(8,128)(2,1)S(1)}) custom-call(s32[3]{0:T(128)S(1)} %pad_add_fusion.where, bf16[16,7168]{1,0:T(8,128)(2,1)S(1)} %collective-permute-done.5.mine_ref, bf16[16,7168]{1,0:T(8,128)(2,1)S(1)} %collective-permute-done.6.other_ref, ...), custom_call_target="tpu_custom_call", output_to_operand_aliasing={{0}: (4, {})} | custom-call | flops 3758096384 | bytes 14680064 | tf_op jit(solution)/shard_map/pallas_call | solution.py:85
  56.6 6.2 %collective-permute-done.9 = f32[2,32,1024]{2,1,0:T(8,128)S(1)} collective-permute-done((f32[2,32,1024]{2,1,0:T(8,128)S(1)}, f32[2,32,1024]{2,1,0:T(8,128)S(1)}, u32[]{:S(2)}, u32[]{:S(2)}) %collective-permute-start.9) | collective-permute-done | bytes 262176 | tf_op jit(solution)/shard_map/ppermute | solution.py:322
  64.4 6.0 %collective-permute-done.10.refs_3_ = f32[2,32,1024]{2,1,0:T(8,128)S(1)} collective-permute-done((f32[2,32,1024]{2,1,0:T(8,128)S(1)}, f32[2,32,1024]{2,1,0:T(8,128)S(1)}, u32[]{:S(2)}, u32[]{:S(2)}) %collective-permute-start.10) | collective-permute-done | bytes 262176 | tf_op jit(solution)/shard_map/ppermute | solution.py:322
  98.4 6.6 %shard_map.55 = (f32[16,7168]{1,0:T(8,128)S(1)}, bf16[16,7168]{1,0:T(8,128)(2,1)S(1)}) custom-call(s32[3]{0:T(128)S(1)} %pad_add_fusion.where, bf16[4,32,1024]{2,1,0:T(8,128)(2,1)S(1)} %shard_map.51.basis_ref, bf16[4,1024,7168]{2,1,0:T(8,128)(2,1)} %grads_ref.13, bf16[16,7168]{1,0:T(8,128)(2,1)S(1)} %get-tuple-element.41.rest_0_), custom_call_target="tpu_custom_call" | custom-call | flops 3758096384 | bytes 14680064 | tf_op jit(solution)/shard_map/pallas_call | solution.py:145
  110.2 5.8 %collective-permute-done.17 = bf16[16,7168]{1,0:T(8,128)(2,1)S(1)} collective-permute-done((bf16[16,7168]{1,0:T(8,128)(2,1)S(1)}, bf16[16,7168]{1,0:T(8,128)(2,1)S(1)}, u32[]{:S(2)}, u32[]{:S(2)}) %collective-permute-start.17) | collective-permute-done | bytes 229408 | tf_op jit(solution)/shard_map/ppermute | solution.py:322
  116.0 12.7 %collective-permute-done.19 = bf16[16,7168]{1,0:T(8,128)(2,1)S(1)} collective-permute-done((bf16[16,7168]{1,0:T(8,128)(2,1)S(1)}, bf16[16,7168]{1,0:T(8,128)(2,1)S(1)}, u32[]{:S(2)}, u32[]{:S(2)}) %collective-permute-start.19) | collective-permute-done | bytes 229408 | tf_op jit(solution)/shard_map/ppermute | solution.py:322
  132.4 13.0 %collective-permute-done.29.mine_ref = bf16[16,7168]{1,0:T(8,128)(2,1)S(1)} collective-permute-done((bf16[16,7168]{1,0:T(8,128)(2,1)S(1)}, bf16[16,7168]{1,0:T(8,128)(2,1)S(1)}, u32[]{:S(2)}, u32[]{:S(2)}) %collective-permute-start.29) | collective-permute-done | bytes 229408 | tf_op jit(solution)/shard_map/ppermute | solution.py:322
  146.8 8.3 %shard_map.56.rest_0_ = f32[2,32,1024]{2,1,0:T(8,128)S(1)} custom-call(s32[3]{0:T(128)S(1)} %pad_add_fusion.where, bf16[16,7168]{1,0:T(8,128)(2,1)S(1)} %add_convert_fusion.4.mine_ref, bf16[16,7168]{1,0:T(8,128)(2,1)S(1)} %collective-permute-done.24.other_ref, bf16[4,1024,7168]{2,1,0:T(8,128)(2,1)} %grads_ref.13), custom_call_target="tpu_custom_call" | custom-call | flops 3758096384 | bytes 14680064 | tf_op jit(solution)/shard_map/pallas_call | solution.py:85
  155.1 5.2 %shard_map.57 = f32[2,32,1024]{2,1,0:T(8,128)S(1)} custom-call(s32[3]{0:T(128)S(1)} %pad_add_fusion.where, bf16[16,7168]{1,0:T(8,128)(2,1)S(1)} %collective-permute-done.22.mine_ref, bf16[16,7168]{1,0:T(8,128)(2,1)S(1)} %collective-permute-done.23.other_ref, bf16[1024,7168]{1,0:T(8,128)(2,1)S(1)} %get-tuple-element.36.grads_ref, ...), custom_call_target="tpu_custom_call", output_to_operand_aliasing={{}: (4, {})} | custom-call | flops 3758096384 | bytes 14680064 | tf_op jit(solution)/shard_map/pallas_call | solution.py:85
  160.9 5.2 %shard_map.58.rest_0_ = f32[2,32,1024]{2,1,0:T(8,128)S(1)} custom-call(s32[3]{0:T(128)S(1)} %pad_add_fusion.where, bf16[16,7168]{1,0:T(8,128)(2,1)S(1)} %collective-permute-done.29.mine_ref, bf16[16,7168]{1,0:T(8,128)(2,1)S(1)} %collective-permute-done.30.other_ref, bf16[1024,7168]{1,0:T(8,128)(2,1)S(1)} %get-tuple-element.37.grads_ref), custom_call_target="tpu_custom_call" | custom-call | flops 3758096384 | bytes 14680064 | tf_op jit(solution)/shard_map/pallas_call | solution.py:85
  166.1 5.3 %shard_map.59 = f32[2,32,1024]{2,1,0:T(8,128)S(1)} custom-call(s32[3]{0:T(128)S(1)} %pad_add_fusion.where, bf16[16,7168]{1,0:T(8,128)(2,1)S(1)} %collective-permute-done.27.mine_ref, bf16[16,7168]{1,0:T(8,128)(2,1)S(1)} %collective-permute-done.28.other_ref, bf16[1024,7168]{1,0:T(8,128)(2,1)S(1)} %get-tuple-element.38.grads_ref, ...), custom_call_target="tpu_custom_call", output_to_operand_aliasing={{}: (4, {})} | custom-call | flops 3758096384 | bytes 14680064 | tf_op jit(solution)/shard_map/pallas_call | solution.py:85
  174.6 5.3 %collective-permute-done.31 = f32[2,32,1024]{2,1,0:T(8,128)S(1)} collective-permute-done((f32[2,32,1024]{2,1,0:T(8,128)S(1)}, f32[2,32,1024]{2,1,0:T(8,128)S(1)}, u32[]{:S(2)}, u32[]{:S(2)}) %collective-permute-start.31) | collective-permute-done | bytes 262176 | tf_op jit(solution)/shard_map/ppermute | solution.py:322
  181.5 6.1 %collective-permute-done.32.refs_3_ = f32[2,32,1024]{2,1,0:T(8,128)S(1)} collective-permute-done((f32[2,32,1024]{2,1,0:T(8,128)S(1)}, f32[2,32,1024]{2,1,0:T(8,128)S(1)}, u32[]{:S(2)}, u32[]{:S(2)}) %collective-permute-start.32) | collective-permute-done | bytes 262176 | tf_op jit(solution)/shard_map/ppermute | solution.py:322
  218.0 6.6 %shard_map.68 = (f32[16,7168]{1,0:T(8,128)S(1)}, bf16[16,7168]{1,0:T(8,128)(2,1)S(1)}) custom-call(s32[3]{0:T(128)S(1)} %pad_add_fusion.where, bf16[4,32,1024]{2,1,0:T(8,128)(2,1)S(1)} %shard_map.61.basis_ref, bf16[4,1024,7168]{2,1,0:T(8,128)(2,1)} %grads_ref.13, bf16[16,7168]{1,0:T(8,128)(2,1)S(1)} %get-tuple-element.51.rest_0_), custom_call_target="tpu_custom_call" | custom-call | flops 3758096384 | bytes 14680064 | tf_op jit(solution)/shard_map/pallas_call | solution.py:145
  231.5 4.1 %collective-permute-done.48 = bf16[16,7168]{1,0:T(8,128)(2,1)S(1)} collective-permute-done((bf16[16,7168]{1,0:T(8,128)(2,1)S(1)}, bf16[16,7168]{1,0:T(8,128)(2,1)S(1)}, u32[]{:S(2)}, u32[]{:S(2)}) %collective-permute-start.48) | collective-permute-done | bytes 229408 | tf_op jit(solution)/shard_map/ppermute | solution.py:322
  235.5 8.8 %collective-permute-done.46 = bf16[16,7168]{1,0:T(8,128)(2,1)S(1)} collective-permute-done((bf16[16,7168]{1,0:T(8,128)(2,1)S(1)}, bf16[16,7168]{1,0:T(8,128)(2,1)S(1)}, u32[]{:S(2)}, u32[]{:S(2)}) %collective-permute-start.46) | collective-permute-done | bytes 229408 | tf_op jit(solution)/shard_map/ppermute | solution.py:322
  244.5 4.9 %collective-permute-start.56 = (bf16[16,7168]{1,0:T(8,128)(2,1)S(1)}, bf16[16,7168]{1,0:T(8,128)(2,1)S(1)}, u32[]{:S(2)}, u32[]{:S(2)}) collective-permute-start(bf16[16,7168]{1,0:T(8,128)(2,1)S(1)} %add_convert_fusion.mine_ref), channel_id=1, source_target_pairs={{0,8},{4,12},{8,0},{12,4},{16,24},{20,28},{24,16},{28,20},{1,9},{5... | collective-permute-start | bytes 688136 | tf_op jit(solution)/shard_map/ppermute | solution.py:322
  252.5 5.7 %collective-permute-done.56.mine_ref = bf16[16,7168]{1,0:T(8,128)(2,1)S(1)} collective-permute-done((bf16[16,7168]{1,0:T(8,128)(2,1)S(1)}, bf16[16,7168]{1,0:T(8,128)(2,1)S(1)}, u32[]{:S(2)}, u32[]{:S(2)}) %collective-permute-start.56) | collective-permute-done | bytes 229408 | tf_op jit(solution)/shard_map/ppermute | solution.py:322
  258.2 10.4 %collective-permute-done.54.mine_ref = bf16[16,7168]{1,0:T(8,128)(2,1)S(1)} collective-permute-done((bf16[16,7168]{1,0:T(8,128)(2,1)S(1)}, bf16[16,7168]{1,0:T(8,128)(2,1)S(1)}, u32[]{:S(2)}, u32[]{:S(2)}) %collective-permute-start.54) | collective-permute-done | bytes 229408 | tf_op jit(solution)/shard_map/ppermute | solution.py:322
  278.8 4.1 %collective-permute-done.58 = f32[3,32,256]{2,1,0:T(8,128)S(1)} collective-permute-done((f32[3,32,256]{2,1,0:T(8,128)S(1)}, f32[3,32,256]{2,1,0:T(8,128)S(1)}, u32[]{:S(2)}, u32[]{:S(2)}) %collective-permute-start.58) | collective-permute-done | bytes 98336 | tf_op jit(solution)/shard_map/ppermute | solution.py:322
  (148 shorter events, 118.2 us)
Async XLA Ops:
  0.0 20.6 %collective-permute-start.7 = (bf16[16,7168]{1,0:T(8,128)(2,1)}, bf16[16,7168]{1,0:T(8,128)(2,1)S(1)}, u32[]{:S(2)}, u32[]{:S(2)}) collective-permute-start(bf16[16,7168]{1,0:T(8,128)(2,1)} %bitcast.7), channel_id=1, source_target_pairs={{0,16},{4,20},{8,24},{12,28},{16,0},{20,4},{24,8},{28,12},{1,17},{... | collective-permute-start | bytes 688136 | tf_op jit(solution)/shard_map/ppermute | solution.py:322
  4.1 16.5 %collective-permute-start.5 = (bf16[16,7168]{1,0:T(8,128)(2,1)}, bf16[16,7168]{1,0:T(8,128)(2,1)S(1)}, u32[]{:S(2)}, u32[]{:S(2)}) collective-permute-start(bf16[16,7168]{1,0:T(8,128)(2,1)} %bitcast.8), channel_id=1, source_target_pairs={{0,24},{4,28},{8,16},{12,20},{16,8},{20,12},{24,0},{28,4},{1,25},{... | collective-permute-start | bytes 688136 | tf_op jit(solution)/shard_map/ppermute | solution.py:322
  5.4 15.7 %collective-permute-start = (bf16[16,7168]{1,0:T(8,128)(2,1)}, bf16[16,7168]{1,0:T(8,128)(2,1)S(1)}, u32[]{:S(2)}, u32[]{:S(2)}) collective-permute-start(bf16[16,7168]{1,0:T(8,128)(2,1)} %bitcast.9), channel_id=1, source_target_pairs={{0,8},{4,12},{8,0},{12,4},{16,24},{20,28},{24,16},{28,20},{1,9},{5... | collective-permute-start | bytes 688136 | tf_op jit(solution)/shard_map/ppermute | solution.py:322
  5.6 15.6 %collective-permute-start.2 = (bf16[16,7168]{1,0:T(8,128)(2,1)}, bf16[16,7168]{1,0:T(8,128)(2,1)S(1)}, u32[]{:S(2)}, u32[]{:S(2)}) collective-permute-start(bf16[16,7168]{1,0:T(8,128)(2,1)} %bitcast.10), channel_id=1, source_target_pairs={{0,4},{4,0},{8,12},{12,8},{16,20},{20,16},{24,28},{28,24},{1,5},{5... | collective-permute-start | bytes 688136 | tf_op jit(solution)/shard_map/ppermute | solution.py:322
  20.6 19.0 %collective-permute-start.8 = (bf16[16,7168]{1,0:T(8,128)(2,1)S(1)}, bf16[16,7168]{1,0:T(8,128)(2,1)S(1)}, u32[]{:S(2)}, u32[]{:S(2)}) collective-permute-start(bf16[16,7168]{1,0:T(8,128)(2,1)S(1)} %collective-permute-done.7.mine_ref), channel_id=1, source_target_pairs={{0,4},{4,0},{8,12},{12,8},{16,20},{20,16},{24,28},{28,24},{1,5},{5... | collective-permute-start | bytes 688136 | tf_op jit(solution)/shard_map/ppermute | solution.py:322
  20.6 26.4 %collective-permute-start.6 = (bf16[16,7168]{1,0:T(8,128)(2,1)S(1)}, bf16[16,7168]{1,0:T(8,128)(2,1)S(1)}, u32[]{:S(2)}, u32[]{:S(2)}) collective-permute-start(bf16[16,7168]{1,0:T(8,128)(2,1)S(1)} %collective-permute-done.5.mine_ref), channel_id=1, source_target_pairs={{0,4},{4,0},{8,12},{12,8},{16,20},{20,16},{24,28},{28,24},{1,5},{5... | collective-permute-start | bytes 688136 | tf_op jit(solution)/shard_map/ppermute | solution.py:322
  37.8 16.9 %collective-permute-start.3 = (f32[2,32,1024]{2,1,0:T(8,128)S(1)}, f32[2,32,1024]{2,1,0:T(8,128)S(1)}, u32[]{:S(2)}, u32[]{:S(2)}) collective-permute-start(f32[2,32,1024]{2,1,0:T(8,128)S(1)} %get-tuple-element.31), channel_id=1, source_target_pairs={{0,1},{1,0},{2,3},{3,2},{4,5},{5,4},{6,7},{7,6},{8,9},{9,8},{10,11... | collective-permute-start | bytes 786440 | tf_op jit(solution)/shard_map/ppermute | solution.py:322
  89.8 15.6 %collective-permute-start.16 = (bf16[16,7168]{1,0:T(8,128)(2,1)S(1)}, bf16[16,7168]{1,0:T(8,128)(2,1)S(1)}, u32[]{:S(2)}, u32[]{:S(2)}) collective-permute-start(bf16[16,7168]{1,0:T(8,128)(2,1)S(1)} %get-tuple-element.39.rest_0_), channel_id=1, source_target_pairs={{0,4},{4,0},{8,12},{12,8},{16,20},{20,16},{24,28},{28,24},{1,5},{5... | collective-permute-start | bytes 688136 | tf_op jit(solution)/shard_map/ppermute | solution.py:322
  93.8 14.6 %collective-permute-start.18 = (bf16[16,7168]{1,0:T(8,128)(2,1)S(1)}, bf16[16,7168]{1,0:T(8,128)(2,1)S(1)}, u32[]{:S(2)}, u32[]{:S(2)}) collective-permute-start(bf16[16,7168]{1,0:T(8,128)(2,1)S(1)} %get-tuple-element.40.rest_0_), channel_id=1, source_target_pairs={{0,4},{4,0},{8,12},{12,8},{16,20},{20,16},{24,28},{28,24},{1,5},{5... | collective-permute-start | bytes 688136 | tf_op jit(solution)/shard_map/ppermute | solution.py:322
  108.5 20.2 %collective-permute-start.19 = (bf16[16,7168]{1,0:T(8,128)(2,1)S(1)}, bf16[16,7168]{1,0:T(8,128)(2,1)S(1)}, u32[]{:S(2)}, u32[]{:S(2)}) collective-permute-start(bf16[16,7168]{1,0:T(8,128)(2,1)S(1)} %add_convert_fusion.6), channel_id=1, source_target_pairs={{0,16},{4,20},{8,24},{12,28},{16,0},{20,4},{24,8},{28,12},{1,17},{... | collective-permute-start | bytes 688136 | tf_op jit(solution)/shard_map/ppermute | solution.py:322
  108.6 20.1 %collective-permute-start.21 = (bf16[16,7168]{1,0:T(8,128)(2,1)S(1)}, bf16[16,7168]{1,0:T(8,128)(2,1)S(1)}, u32[]{:S(2)}, u32[]{:S(2)}) collective-permute-start(bf16[16,7168]{1,0:T(8,128)(2,1)S(1)} %add_convert_fusion.5), channel_id=1, source_target_pairs={{0,8},{4,12},{8,0},{12,4},{16,24},{20,28},{24,16},{28,20},{1,9},{5... | collective-permute-start | bytes 688136 | tf_op jit(solution)/shard_map/ppermute | solution.py:322
  128.9 16.6 %collective-permute-start.29 = (bf16[16,7168]{1,0:T(8,128)(2,1)S(1)}, bf16[16,7168]{1,0:T(8,128)(2,1)S(1)}, u32[]{:S(2)}, u32[]{:S(2)}) collective-permute-start(bf16[16,7168]{1,0:T(8,128)(2,1)S(1)} %add_convert_fusion.4.mine_ref), channel_id=1, source_target_pairs={{0,16},{4,20},{8,24},{12,28},{16,0},{20,4},{24,8},{28,12},{1,17},{... | collective-permute-start | bytes 688136 | tf_op jit(solution)/shard_map/ppermute | solution.py:322
  128.9 16.5 %collective-permute-start.27 = (bf16[16,7168]{1,0:T(8,128)(2,1)S(1)}, bf16[16,7168]{1,0:T(8,128)(2,1)S(1)}, u32[]{:S(2)}, u32[]{:S(2)}) collective-permute-start(bf16[16,7168]{1,0:T(8,128)(2,1)S(1)} %add_convert_fusion.4.mine_ref), channel_id=1, source_target_pairs={{0,24},{4,28},{8,16},{12,20},{16,8},{20,12},{24,0},{28,4},{1,25},{... | collective-permute-start | bytes 688136 | tf_op jit(solution)/shard_map/ppermute | solution.py:322
  130.6 16.2 %collective-permute-start.22 = (bf16[16,7168]{1,0:T(8,128)(2,1)S(1)}, bf16[16,7168]{1,0:T(8,128)(2,1)S(1)}, u32[]{:S(2)}, u32[]{:S(2)}) collective-permute-start(bf16[16,7168]{1,0:T(8,128)(2,1)S(1)} %add_convert_fusion.4.mine_ref), channel_id=1, source_target_pairs={{0,8},{4,12},{8,0},{12,4},{16,24},{20,28},{24,16},{28,20},{1,9},{5... | collective-permute-start | bytes 688136 | tf_op jit(solution)/shard_map/ppermute | solution.py:322
  145.5 15.4 %collective-permute-start.30 = (bf16[16,7168]{1,0:T(8,128)(2,1)S(1)}, bf16[16,7168]{1,0:T(8,128)(2,1)S(1)}, u32[]{:S(2)}, u32[]{:S(2)}) collective-permute-start(bf16[16,7168]{1,0:T(8,128)(2,1)S(1)} %collective-permute-done.29.mine_ref), channel_id=1, source_target_pairs={{0,4},{4,0},{8,12},{12,8},{16,20},{20,16},{24,28},{28,24},{1,5},{5... | collective-permute-start | bytes 688136 | tf_op jit(solution)/shard_map/ppermute | solution.py:322
  145.5 20.6 %collective-permute-start.28 = (bf16[16,7168]{1,0:T(8,128)(2,1)S(1)}, bf16[16,7168]{1,0:T(8,128)(2,1)S(1)}, u32[]{:S(2)}, u32[]{:S(2)}) collective-permute-start(bf16[16,7168]{1,0:T(8,128)(2,1)S(1)} %collective-permute-done.27.mine_ref), channel_id=1, source_target_pairs={{0,4},{4,0},{8,12},{12,8},{16,20},{20,16},{24,28},{28,24},{1,5},{5... | collective-permute-start | bytes 688136 | tf_op jit(solution)/shard_map/ppermute | solution.py:322
  225.0 19.3 %collective-permute-start.46 = (bf16[16,7168]{1,0:T(8,128)(2,1)S(1)}, bf16[16,7168]{1,0:T(8,128)(2,1)S(1)}, u32[]{:S(2)}, u32[]{:S(2)}) collective-permute-start(bf16[16,7168]{1,0:T(8,128)(2,1)S(1)} %add_convert_fusion.2), channel_id=1, source_target_pairs={{0,16},{4,20},{8,24},{12,28},{16,0},{20,4},{24,8},{28,12},{1,17},{... | collective-permute-start | bytes 688136 | tf_op jit(solution)/shard_map/ppermute | solution.py:322
  225.9 18.4 %collective-permute-start.44 = (bf16[16,7168]{1,0:T(8,128)(2,1)S(1)}, bf16[16,7168]{1,0:T(8,128)(2,1)S(1)}, u32[]{:S(2)}, u32[]{:S(2)}) collective-permute-start(bf16[16,7168]{1,0:T(8,128)(2,1)S(1)} %add_convert_fusion.3), channel_id=1, source_target_pairs={{0,24},{4,28},{8,16},{12,20},{16,8},{20,12},{24,0},{28,4},{1,25},{... | collective-permute-start | bytes 688136 | tf_op jit(solution)/shard_map/ppermute | solution.py:322
  230.1 21.7 %collective-permute-start.38 = (bf16[128,1024]{1,0:T(8,128)(2,1)S(1)}, bf16[128,1024]{1,0:T(8,128)(2,1)S(1)}, u32[]{:S(2)}, u32[]{:S(2)}) collective-permute-start(bf16[128,1024]{1,0:T(8,128)(2,1)S(1)} %shard_map.62.held_ref), channel_id=1, source_target_pairs={{0,8},{4,12},{16,24},{20,28},{9,1},{13,5},{25,17},{29,21},{18,26},... | collective-permute-start | bytes 786440 | tf_op jit(solution)/shard_map/ppermute | solution.py:399
  249.4 19.2 %collective-permute-start.54 = (bf16[16,7168]{1,0:T(8,128)(2,1)S(1)}, bf16[16,7168]{1,0:T(8,128)(2,1)S(1)}, u32[]{:S(2)}, u32[]{:S(2)}) collective-permute-start(bf16[16,7168]{1,0:T(8,128)(2,1)S(1)} %add_convert_fusion.mine_ref), channel_id=1, source_target_pairs={{0,16},{4,20},{8,24},{12,28},{16,0},{20,4},{24,8},{28,12},{1,17},{... | collective-permute-start | bytes 688136 | tf_op jit(solution)/shard_map/ppermute | solution.py:322
  249.5 19.1 %collective-permute-start.52 = (bf16[16,7168]{1,0:T(8,128)(2,1)S(1)}, bf16[16,7168]{1,0:T(8,128)(2,1)S(1)}, u32[]{:S(2)}, u32[]{:S(2)}) collective-permute-start(bf16[16,7168]{1,0:T(8,128)(2,1)S(1)} %add_convert_fusion.mine_ref), channel_id=1, source_target_pairs={{0,24},{4,28},{8,16},{12,20},{16,8},{20,12},{24,0},{28,4},{1,25},{... | collective-permute-start | bytes 688136 | tf_op jit(solution)/shard_map/ppermute | solution.py:322
  252.4 16.7 %collective-permute-start.39 = (bf16[128,1024]{1,0:T(8,128)(2,1)S(1)}, bf16[128,1024]{1,0:T(8,128)(2,1)S(1)}, u32[]{:S(2)}, u32[]{:S(2)}) collective-permute-start(bf16[128,1024]{1,0:T(8,128)(2,1)S(1)} %shard_map.63.mine_ref), channel_id=1, source_target_pairs={{0,4},{4,0},{8,12},{12,8},{16,20},{20,16},{24,28},{28,24},{1,5},{5... | collective-permute-start | bytes 786440 | tf_op jit(solution)/shard_map/ppermute | solution.py:322
  258.2 14.7 %collective-permute-start.57 = (bf16[16,7168]{1,0:T(8,128)(2,1)S(1)}, bf16[16,7168]{1,0:T(8,128)(2,1)S(1)}, u32[]{:S(2)}, u32[]{:S(2)}) collective-permute-start(bf16[16,7168]{1,0:T(8,128)(2,1)S(1)} %collective-permute-done.56.mine_ref), channel_id=1, source_target_pairs={{0,4},{4,0},{8,12},{12,8},{16,20},{20,16},{24,28},{28,24},{1,5},{5... | collective-permute-start | bytes 688136 | tf_op jit(solution)/shard_map/ppermute | solution.py:322
  278.1 14.7 %collective-permute-start.41 = (f32[4,32,256]{2,1,0:T(8,128)S(1)}, f32[4,32,256]{2,1,0:T(8,128)S(1)}, u32[]{:S(2)}, u32[]{:S(2)}) collective-permute-start(f32[4,32,256]{2,1,0:T(8,128)S(1)} %add.88.refs_0_), channel_id=1, source_target_pairs={{0,2},{1,3},{2,0},{3,1},{4,6},{5,7},{6,4},{7,5},{8,10},{9,11},{10,... | collective-permute-start | bytes 393224 | tf_op jit(solution)/shard_map/ppermute | solution.py:322
  (39 other events, 401.4 us)

commit v3 on v2

--- a/solution.py
+++ b/solution.py
@@ -18,85 +18,93 @@
 MIB = 1024 * 1024
 
 
-def params(mebibytes=4):
+def params(mebibytes=1):
     return pltpu.CompilerParams(vmem_limit_bytes=mebibytes * MIB)
 
 
 def cost(flops, nbytes):
     return pl.CostEstimate(flops=int(flops), bytes_accessed=int(nbytes), transcendentals=0)
+
+
+def both_cores(core, mine, other, axis):
+    return jnp.concatenate(
+        [jnp.where(core == 0, mine, other), jnp.where(core == 0, other, mine)], axis=axis
+    )
 
 
 ROW_CHUNKS = 4
 COL_CHUNKS = 8
 STREAM_BANDS = 2
 STREAM_COLS = 4
-STREAMED = 1
-
-
-def images_body(where, mine_ref, other_ref, grads_ref, *rest, mode, aliased, offset):
-    out_ref, *rest = rest[1:] if aliased else rest
+STREAM_MIB = 9
+
+
+def images_body(where, mine_ref, other_ref, *refs, carried, mode, offset):
+    refs = list(refs)
+    carry_ref = refs.pop(0) if carried else None
+    source_ref, out_ref = refs.pop(0), refs.pop(0)
     query, core = where[0] ^ offset, where[1]
-    rows = out_ref.shape[2] // ROW_CHUNKS
+    rows = out_ref.shape[1] // ROW_CHUNKS
+    ahead = STREAM_BANDS if mode == "stream" else ROW_CHUNKS
 
     def band(i):
         return pl.ds(pl.multiple_of(i * rows, 128), rows)
 
     def view(i):
         if mode == "stream":
-            return rest[0].at[lax.rem(i, STREAM_BANDS)]
-        return (grads_ref if mode == "held" else rest[0]).at[band(i), :]
+            return refs[0].at[lax.rem(i, STREAM_BANDS)]
+        return (source_ref if mode == "held" else refs[0]).at[band(i), :]
 
     def fetch(i):
-        return pltpu.make_async_copy(grads_ref.at[query, band(i), :], view(i), rest[1].at[i])
-
-    if mode != "held":
-        for i in range(STREAM_BANDS if mode == "stream" else ROW_CHUNKS):
-            fetch(i).start()
-    mine, other = mine_ref[...], other_ref[...]
-    vectors = jnp.concatenate(
-        [jnp.where(core == 0, mine, other), jnp.where(core == 0, other, mine)], axis=0
-    )
+        return pltpu.make_async_copy(source_ref.at[query, band(i), :], view(i), refs[1].at[i])
+
+    for i in range(0 if mode == "held" else ahead):
+        fetch(i).start()
+    if carried:
+        out_ref[:carried] = carry_ref[...]
+    vectors = both_cores(core, mine_ref[...], other_ref[...], 0)
 
     def body(i, carry):
         if mode != "held":
             fetch(i).wait()
-        out_ref[0, :, band(i)] = lax.dot_general(
+        out_ref[carried:, band(i)] = lax.dot_general(
             vectors, view(i)[...], NT, preferred_element_type=F32
         )
         if mode == "stream":
 
-            @pl.when(i + STREAM_BANDS < ROW_CHUNKS)
+            @pl.when(i + ahead < ROW_CHUNKS)
             def _():
-                fetch(i + STREAM_BANDS).start()
+                fetch(i + ahead).start()
 
         return carry
 
     lax.fori_loop(0, ROW_CHUNKS, body, 0)
 
 
-def images_of_query(where, offset, mine, other, grads, mode, slot, slots, earlier=None):
-    rows, cols = grads.shape[-2:]
-    aliased, load = earlier is not None, mode == "load"
+def images_of_query(where, offset, mine, other, carry, source, mode):
+    rows, cols = source.shape[-2:]
+    carried = carry.shape[0] if carry is not None else 0
+    load = mode == "load"
     scratch = []
     if mode == "stream":
         scratch.append(pltpu.VMEM((STREAM_BANDS, rows // ROW_CHUNKS, cols), BF16))
     if mode != "held":
         scratch.append(pltpu.SemaphoreType.DMA((ROW_CHUNKS,)))
     return pl.pallas_call(
-        functools.partial(images_body, mode=mode, aliased=aliased, offset=offset),
-        grid=(1,),
-        in_specs=[SMEM, VMEM, VMEM, VMEM if mode == "held" else ANY] + [ANY] * aliased,
-        out_specs=[pl.BlockSpec((1, RANK, rows), lambda i: (slot, 0, 0))] + [VMEM] * load,
-        out_shape=[jax.ShapeDtypeStruct((slots, RANK, rows), F32)]
+        functools.partial(images_body, carried=carried, mode=mode, offset=offset),
+        in_specs=[SMEM, VMEM, VMEM]
+        + [VMEM] * bool(carried)
+        + [VMEM if mode == "held" else ANY],
+        out_specs=[VMEM] * (1 + load),
+        out_shape=[jax.ShapeDtypeStruct((carried + RANK, rows), F32)]
         + [pltpu.VMEM((rows, cols), BF16)] * load,
         scratch_shapes=scratch,
-        input_output_aliases={4: 0} if aliased else {},
         cost_estimate=cost(2 * RANK * rows * cols * 8, 2 * rows * cols),
-        compiler_params=params(12 if mode == "stream" else 3),
-    )(where, mine, other, grads, *([earlier] if aliased else []))
-
-
-def back_body(where, basis_ref, grads_ref, *rest, stream, ties, offset):
+        compiler_params=params(STREAM_MIB if mode == "stream" else 1),
+    )(where, mine, other, *([carry] if carried else []), source)
+
+
+def back_body(where, basis_ref, source_ref, *rest, stream, ties, offset):
     mine_ref, other_ref, *rest = rest[ties:]
     query, core = where[0] ^ offset, where[1]
     half = mine_ref.shape[0]
@@ -107,14 +115,13 @@
         return pl.ds(pl.multiple_of(i * width, 128), width)
 
     def view(i):
-        return rest[0].at[lax.rem(i, STREAM_COLS)] if stream else grads_ref.at[:, band(i)]
+        return rest[0].at[lax.rem(i, STREAM_COLS)] if stream else source_ref.at[:, band(i)]
 
     def fetch(i):
-        return pltpu.make_async_copy(grads_ref.at[query, :, band(i)], view(i), rest[1].at[i])
-
-    if stream:
-        for i in range(STREAM_COLS):
-            fetch(i).start()
+        return pltpu.make_async_copy(source_ref.at[query, :, band(i)], view(i), rest[1].at[i])
+
+    for i in range(STREAM_COLS if stream else 0):
+        fetch(i).start()
 
     def body(i, carry):
         if stream:
@@ -134,9 +141,9 @@
     lax.fori_loop(0, COL_CHUNKS, body, 0)
 
 
-def back_of_query(where, offset, basis, grads, after):
-    rows, cols = grads.shape[-2:]
-    stream = grads.ndim == 3
+def back_of_query(where, offset, basis, source, after):
+    rows, cols = source.shape[-2:]
+    stream = source.ndim == 3
     half = RANK // CORES
     scratch = [
         pltpu.VMEM((STREAM_COLS, rows, cols // COL_CHUNKS), BF16),
@@ -152,19 +159,37 @@
         ],
         scratch_shapes=scratch if stream else [],
         cost_estimate=cost(2 * RANK * rows * cols * 8, 2 * rows * cols),
-        compiler_params=params(12 if stream else 3),
-    )(where, basis, grads, *after)
+        compiler_params=params(STREAM_MIB if stream else 1),
+    )(where, basis, source, *after)
+
+
+def total_body(*refs):
+    value = refs[0][...].astype(F32)
+    for ref in refs[1:-1]:
+        value = value + ref[...].astype(F32)
+    refs[-1][...] = value.astype(refs[-1].dtype)
+
+
+def total(parts, dtype=F32):
+    return pl.pallas_call(
+        total_body,
+        in_specs=[VMEM] * len(parts),
+        out_specs=VMEM,
+        out_shape=jax.ShapeDtypeStruct(parts[0].shape, dtype),
+        cost_estimate=cost(len(parts) * parts[0].size, 4 * len(parts) * parts[0].size),
+        compiler_params=params(),
+    )(*parts)
 
 
 def gram_body(where, *refs):
     pairs, (images_ref, gram_ref) = refs[:-2], refs[-2:]
-    chip = where[0]
     queries = images_ref.shape[0]
-    slot = 0
+    d = 0
     for held, received in zip(pairs[0::2], pairs[1::2]):
-        for i in range(held.shape[0]):
-            images_ref[chip ^ slot] = held[i] + received[i]
-            slot += 1
+        for start in range(0, held.shape[0], RANK):
+            block = pl.ds(start, RANK)
+            images_ref[where[0] ^ d] = held[block, :] + received[block, :]
+            d += 1
     for query in range(queries):
         block = images_ref[query]
         gram_ref[:, query * RANK : (query + 1) * RANK] = lax.dot_general(
@@ -174,8 +199,8 @@
 
 def local_gram(where, pairs):
     flat = [part for pair in pairs for part in pair]
-    queries = sum(held.shape[0] for held, _ in pairs)
-    rows = flat[0].shape[2]
+    rows = flat[0].shape[1]
+    queries = sum(held.shape[0] for held, _ in pairs) // RANK
     return pl.pallas_call(
         gram_body,
         in_specs=[SMEM] + [VMEM] * len(flat),
@@ -247,12 +272,6 @@
     )(where, held, received)
 
 
-def both_cores(core, mine, other, axis):
-    return jnp.concatenate(
-        [jnp.where(core == 0, mine, other), jnp.where(core == 0, other, mine)], axis=axis
-    )
-
-
 def project_out_body(where, mine_ref, other_ref, hooked_ref, out_ref, scratch):
     vectors = both_cores(where[1], mine_ref[...], other_ref[...], 1)
     queries = scratch.shape[0]
@@ -272,7 +291,7 @@
         out_shape=jax.ShapeDtypeStruct(shape, F32),
         scratch_shapes=[pltpu.VMEM(shape, F32)],
         cost_estimate=cost(4 * mine.size * hooked.shape[0], 2 * hooked.size),
-        compiler_params=params(),
+        compiler_params=params(4),
     )(where, mine, other, hooked)
 
 
@@ -292,7 +311,7 @@
         out_shape=jax.ShapeDtypeStruct((slots, RANK, tokens), F32),
         input_output_aliases={4: 0} if aliased else {},
         cost_estimate=cost(4 * mine.size * tokens, 2 * hooked.size),
-        compiler_params=params(),
+        compiler_params=params(8),
     )(where, mine, other, hooked, *([earlier] if aliased else []))
 
 
@@ -329,14 +348,15 @@
     chip, core = tok // CORES, tok % CORES
     where = jnp.stack([chip, core, par]).astype(jnp.int32)
     par_bits = [1 << i for i in range(pars.bit_length() - 1)]
-    held = [query_grads] * chips
+    held = [query_grads] + [None] * (chips - 1)
 
     def tok_swap(x, bits):
         return xor_permute(x, "tok", toks, bits)
 
     def par_pair(x):
         for b in par_bits[:-1]:
-            x = x + xor_permute(x, "par", pars, b)
+            received = xor_permute(x, "par", pars, b)
+            x = total([x, received])
         return x, xor_permute(x, "par", pars, par_bits[-1])
 
     def gathered(piece, step):
@@ -346,71 +366,76 @@
             step(d, pieces[d], other)
 
     def images_from(piece):
-        done = []
+        pairs, carry = [], None
 
         def step(d, mine, other):
-            earlier = done[-1] if d % 2 else None
-            if d < STREAMED:
-                mode = "stream"
-            else:
-                mode = "load" if held[d] is query_grads else "held"
-            images, *block = images_of_query(
-                where, d, mine, other, held[d], mode, d % 2, 2, earlier
-            )
+            nonlocal carry
+            source, mode = held[d], "held" if d else "stream"
+            if source is None:
+                source, mode = query_grads, "load"
+            images, *block = images_of_query(where, d, mine, other, carry, source, mode)
             held[d] = block[0] if block else held[d]
-            done.append(images)
+            carry = images if d in JOINED else None
+            if carry is None:
+                pairs.append(par_pair(images))
 
         gathered(piece, step)
-        return [par_pair(part) for part in done[1::2]]
+        return pairs
 
     def basis_from(pairs):
         images, gram = local_gram(where, pairs)
-        gram = gram + tok_swap(gram, 1)
+        gram = total([gram, tok_swap(gram, 1)])
         others = [tok_swap(gram, CORES * d) for d in range(1, chips)]
         return orthonormal(images, [gram] + others)
 
     def back_piece(basis):
-        after, arrived, total = [], [], None
+        after, arrived = [], []
         for d in reversed(range(chips)):
             mine, other = back_of_query(where, d, basis, held[d], after)
             after = [other]
-            total = mine + tok_swap(other, 1).astype(F32)
+            received = tok_swap(other, 1)
             if d:
-                arrived.append(tok_swap(total.astype(BF16), CORES * d))
-        for part in arrived:
-            total = total + part.astype(F32)
-        return total.astype(BF16)
+                arrived.append(tok_swap(total([mine, received], BF16), CORES * d))
+        return total([mine, received] + arrived, BF16)
+
+    def spread(basis):
+        got = basis.reshape(queries * RANK, rows)
+        owners = [0]
+        for bits in [1 << i for i in reversed(range(chips.bit_length() - 1))]:
+            sends = [
+                (((p ^ o) * CORES + c) * pars + p, ((p ^ o ^ bits) * CORES + c) * pars + p)
+                for p in range(pars)
+                for o in owners
+                for c in range(CORES)
+            ]
+            received = lax.ppermute(got, ("tok", "par"), sends)
+            got = choose(where, got, received, owners)
+            owners = owners + [o ^ bits for o in owners]
+        return got
 
     piece = start_block.T
-    basis = None
-    for _ in range(ITERS):
+    for i in range(ITERS):
         basis = basis_from(images_from(piece))
+        if i == ITERS - 1:
+            spread_rows = spread(basis)
         piece = back_piece(basis)
 
-    got = flat = basis.reshape(queries * RANK, rows)
-    owners = [0]
-    for bits in [1 << i for i in reversed(range(chips.bit_length() - 1))]:
-        sends = [
-            (((p ^ o) * CORES + c) * pars + p, ((p ^ o ^ bits) * CORES + c) * pars + p)
-            for p in range(pars)
-            for o in owners
-            for c in range(CORES)
-        ]
-        received = lax.ppermute(got, ("tok", "par"), sends)
-        got = choose(where, got, received, owners)
-        owners = owners + [o ^ bits for o in owners]
-    out_proj = project_out(where, got, tok_swap(got, 1), hooked_out)
-
     parts = []
 
     def in_proj(d, mine, other):
-        earlier = parts[-1] if d > 1 else None
-        slot, slots = max(d - 1, 0), chips - 1 if d else 1
+        last = d == chips - 1
+        earlier = parts[-1] if 0 < d and not last else None
+        slot, slots = (0, 1) if last else (d, chips - 1)
         parts.append(project_in(where, mine, other, hooked_in, slot, slots, earlier))
 
     gathered(piece, in_proj)
-    pairs = [par_pair(out_proj), par_pair(parts[0]), par_pair(parts[-1])]
+    other_rows = tok_swap(spread_rows, 1)
+    out_proj = project_out(where, spread_rows, other_rows, hooked_out)
+    pairs = [par_pair(out_proj), par_pair(parts[-2]), par_pair(parts[-1])]
     return token_scores(where, pairs)
+
+
+JOINED = (0,)
 
 
 def plain(query_grads, start_block, hooked_out, hooked_in):

time: 295 us -> 296 us (level)
    ppermute x58 -> x62, starting transfers between devices: 57.6 us -> 59 us  [xor_permute(): return lax.ppermute(x, axis, [(i, i ^ bits) for i in range(size)])]
    pallas_call x8 -> x27, Pallas kernels: 54.2 us -> 54.9 us  [the longest x8 54.2 us: images_of_query(): pl.pallas_call(functools.partial(images_body, carried=carried, mode=mode,...]
    ppermute x58 -> x62, waiting for transfers between devices: 119 us -> 118 us  [xor_permute(): return lax.ppermute(x, axis, [(i, i ^ bits) for i in range(size)])]
  transfers between devices with their start and end apart: 60 -> 64, of which waited for: 23 -> 27; matrix products, arithmetic and copies ran while one was open for 0% -> 0% of each run, Pallas kernels for 29% -> 29%
where the time goes in v3:
time: 296 us
  waiting for transfers between devices  118 us (40%)
  Pallas kernels  112 us (38%)
  starting transfers between devices  64.3 us (22%)
    ppermute x62, waiting for transfers between devices, xor_permute(): return lax.ppermute(x, axis, [(i, i ^ bits) for i in range(size)])  118 us
    ppermute x62, starting transfers between devices, xor_permute(): return lax.ppermute(x, axis, [(i, i ^ bits) for i in range(size)])  59 us
    pallas_call x8, Pallas kernels, images_of_query(): pl.pallas_call(functools.partial(images_body, carried=carried, mode=mode,...  54.2 us
    pallas_call x8, Pallas kernels, back_of_query(): pl.pallas_call(functools.partial(back_body, stream=stream, ties=len(after...  36.5 us
    pallas_call x2, Pallas kernels, orthonormal(): pl.pallas_call(basis_body, in_specs=[VMEM] * (1 + len(grams)), out_specs=...  7.73 us
    pallas_call x4, Pallas kernels, project_in(): pl.pallas_call(project_in_body, grid=(1,), in_specs=[SMEM, VMEM, VMEM, VM...  6.67 us
  transfers between devices with their start and end apart: 64, of which 27 were waited for; matrix products, arithmetic and copies ran while one was open for 0% of the time, Pallas kernels for 29%

profile of v3, /device:TPU:0, one launch (start us, length us, event | category | flops | bytes accessed | tf_op | source)
XLA Modules:
  0.0 295.6 jit_solution(6636739739648420012)
XLA Ops:
  0.0 5.1 %collective-permute-start.9 = (bf16[16,7168]{1,0:T(8,128)(2,1)}, bf16[16,7168]{1,0:T(8,128)(2,1)S(1)}, u32[]{:S(2)}, u32[]{:S(2)}) collective-permute-start(bf16[16,7168]{1,0:T(8,128)(2,1)} %bitcast.7), channel_id=1, source_target_pairs={{0,24},{4,28},{8,16},{12,20},{16,8},{20,12},{24,0},{28,4},{1,25},{... | collective-permute-start | bytes 688136 | tf_op jit(solution)/shard_map/ppermute | solution.py:341
  5.7 6.2 %collective-permute-done.9.mine_ref = bf16[16,7168]{1,0:T(8,128)(2,1)S(1)} collective-permute-done((bf16[16,7168]{1,0:T(8,128)(2,1)}, bf16[16,7168]{1,0:T(8,128)(2,1)S(1)}, u32[]{:S(2)}, u32[]{:S(2)}) %collective-permute-start.9) | collective-permute-done | bytes 229408 | tf_op jit(solution)/shard_map/ppermute | solution.py:341
  11.9 12.9 %collective-permute-done.5.mine_ref = bf16[16,7168]{1,0:T(8,128)(2,1)S(1)} collective-permute-done((bf16[16,7168]{1,0:T(8,128)(2,1)}, bf16[16,7168]{1,0:T(8,128)(2,1)S(1)}, u32[]{:S(2)}, u32[]{:S(2)}) %collective-permute-start.5) | collective-permute-done | bytes 229408 | tf_op jit(solution)/shard_map/ppermute | solution.py:341
  26.2 8.3 %shard_map.46.refs_0_ = f32[32,1024]{1,0:T(8,128)S(1)} custom-call(s32[3]{0:T(128)S(1)} %pad_add_fusion.where, bf16[16,7168]{1,0:T(8,128)(2,1)S(1)} %bitcast.11, bf16[16,7168]{1,0:T(8,128)(2,1)S(1)} %collective-permute-done.2.other_ref, bf16[4,1024,7168]{2,1,0:T(8,128)(2,1)} %source_ref.3), custom_call_target="tpu_custom_call" | custom-call | flops 3758096384 | bytes 14680064 | tf_op jit(solution)/shard_map/pallas_call | solution.py:93
  34.5 7.3 %shard_map.47 = (f32[64,1024]{1,0:T(8,128)S(1)}, bf16[1024,7168]{1,0:T(8,128)(2,1)S(1)}) custom-call(s32[3]{0:T(128)S(1)} %pad_add_fusion.where, bf16[16,7168]{1,0:T(8,128)(2,1)S(1)} %collective-permute-done.mine_ref, bf16[16,7168]{1,0:T(8,128)(2,1)S(1)} %collective-permute-done.1.other_ref, f32[32,1024]{1,0:T(8,128)S(1)} %shard_map.46.refs_0_, ...), custom_call_target="tpu_custom_call" | custom-call | flops 3758096384 | bytes 14680064 | tf_op jit(solution)/shard_map/pallas_call | solution.py:93
  43.4 7.3 %shard_map.49 = (f32[32,1024]{1,0:T(8,128)S(1)}, bf16[1024,7168]{1,0:T(8,128)(2,1)S(1)}) custom-call(s32[3]{0:T(128)S(1)} %pad_add_fusion.where, bf16[16,7168]{1,0:T(8,128)(2,1)S(1)} %collective-permute-done.5.mine_ref, bf16[16,7168]{1,0:T(8,128)(2,1)S(1)} %collective-permute-done.6.other_ref, bf16[4,1024,7168]{2,1,0:T(8,128)(2,1)} %source_ref.3), custom_call_target="tpu_custom_call" | custom-call | flops 3758096384 | bytes 14680064 | tf_op jit(solution)/shard_map/pallas_call | solution.py:93
  51.4 7.3 %shard_map.51 = (f32[32,1024]{1,0:T(8,128)S(1)}, bf16[1024,7168]{1,0:T(8,128)(2,1)S(1)}) custom-call(s32[3]{0:T(128)S(1)} %pad_add_fusion.where, bf16[16,7168]{1,0:T(8,128)(2,1)S(1)} %collective-permute-done.9.mine_ref, bf16[16,7168]{1,0:T(8,128)(2,1)S(1)} %collective-permute-done.10.other_ref, bf16[4,1024,7168]{2,1,0:T(8,128)(2,1)} %source_ref.3), custom_call_target="tpu_custom_call" | custom-call | flops 3758096384 | bytes 14680064 | tf_op jit(solution)/shard_map/pallas_call | solution.py:93
  65.4 6.6 %collective-permute-done.8.refs_3_ = f32[32,1024]{1,0:T(8,128)S(1)} collective-permute-done((f32[32,1024]{1,0:T(8,128)S(1)}, f32[32,1024]{1,0:T(8,128)S(1)}, u32[]{:S(2)}, u32[]{:S(2)}) %collective-permute-start.8) | collective-permute-done | bytes 131104 | tf_op jit(solution)/shard_map/ppermute | solution.py:341
  99.2 6.6 %shard_map.59 = (f32[16,7168]{1,0:T(8,128)S(1)}, bf16[16,7168]{1,0:T(8,128)(2,1)S(1)}) custom-call(s32[3]{0:T(128)S(1)} %pad_add_fusion.where, bf16[4,32,1024]{2,1,0:T(8,128)(2,1)S(1)} %shard_map.55.basis_ref, bf16[4,1024,7168]{2,1,0:T(8,128)(2,1)} %source_ref.3, bf16[16,7168]{1,0:T(8,128)(2,1)S(1)} %get-tuple-element.41.rest_0_), custom_call_target="tpu_custom_call" | custom-call | flops 3758096384 | bytes 14680064 | tf_op jit(solution)/shard_map/pallas_call | solution.py:152
  111.1 5.8 %collective-permute-done.19.refs_2_ = bf16[16,7168]{1,0:T(8,128)(2,1)S(1)} collective-permute-done((bf16[16,7168]{1,0:T(8,128)(2,1)S(1)}, bf16[16,7168]{1,0:T(8,128)(2,1)S(1)}, u32[]{:S(2)}, u32[]{:S(2)}) %collective-permute-start.19) | collective-permute-done | bytes 229408 | tf_op jit(solution)/shard_map/ppermute | solution.py:341
  116.9 12.3 %collective-permute-done.21.refs_3_ = bf16[16,7168]{1,0:T(8,128)(2,1)S(1)} collective-permute-done((bf16[16,7168]{1,0:T(8,128)(2,1)S(1)}, bf16[16,7168]{1,0:T(8,128)(2,1)S(1)}, u32[]{:S(2)}, u32[]{:S(2)}) %collective-permute-start.21) | collective-permute-done | bytes 229408 | tf_op jit(solution)/shard_map/ppermute | solution.py:341
  133.8 6.0 %collective-permute-done.33.mine_ref = bf16[16,7168]{1,0:T(8,128)(2,1)S(1)} collective-permute-done((bf16[16,7168]{1,0:T(8,128)(2,1)S(1)}, bf16[16,7168]{1,0:T(8,128)(2,1)S(1)}, u32[]{:S(2)}, u32[]{:S(2)}) %collective-permute-start.33) | collective-permute-done | bytes 229408 | tf_op jit(solution)/shard_map/ppermute | solution.py:341
  139.8 10.6 %collective-permute-done.29.mine_ref = bf16[16,7168]{1,0:T(8,128)(2,1)S(1)} collective-permute-done((bf16[16,7168]{1,0:T(8,128)(2,1)S(1)}, bf16[16,7168]{1,0:T(8,128)(2,1)S(1)}, u32[]{:S(2)}, u32[]{:S(2)}) %collective-permute-start.29) | collective-permute-done | bytes 229408 | tf_op jit(solution)/shard_map/ppermute | solution.py:341
  150.9 8.3 %shard_map.64.refs_0_ = f32[32,1024]{1,0:T(8,128)S(1)} custom-call(s32[3]{0:T(128)S(1)} %pad_add_fusion.where, bf16[16,7168]{1,0:T(8,128)(2,1)S(1)} %shard_map.63.mine_ref, bf16[16,7168]{1,0:T(8,128)(2,1)S(1)} %collective-permute-done.26.other_ref, bf16[4,1024,7168]{2,1,0:T(8,128)(2,1)} %source_ref.3), custom_call_target="tpu_custom_call" | custom-call | flops 3758096384 | bytes 14680064 | tf_op jit(solution)/shard_map/pallas_call | solution.py:93
  159.2 5.2 %shard_map.69.refs_0_ = f32[32,1024]{1,0:T(8,128)S(1)} custom-call(s32[3]{0:T(128)S(1)} %pad_add_fusion.where, bf16[16,7168]{1,0:T(8,128)(2,1)S(1)} %collective-permute-done.33.mine_ref, bf16[16,7168]{1,0:T(8,128)(2,1)S(1)} %collective-permute-done.34.other_ref, bf16[1024,7168]{1,0:T(8,128)(2,1)S(1)} %get-tuple-element.38.source_ref.refs_0_), custom_call_target="tpu_custom_call" | custom-call | flops 3758096384 | bytes 14680064 | tf_op jit(solution)/shard_map/pallas_call | solution.py:93
  164.9 5.2 %shard_map.65.refs_0_ = f32[64,1024]{1,0:T(8,128)S(1)} custom-call(s32[3]{0:T(128)S(1)} %pad_add_fusion.where, bf16[16,7168]{1,0:T(8,128)(2,1)S(1)} %collective-permute-done.24.mine_ref, bf16[16,7168]{1,0:T(8,128)(2,1)S(1)} %collective-permute-done.25.other_ref, f32[32,1024]{1,0:T(8,128)S(1)} %shard_map.64.refs_0_, ...), custom_call_target="tpu_custom_call" | custom-call | flops 3758096384 | bytes 14680064 | tf_op jit(solution)/shard_map/pallas_call | solution.py:93
  171.6 5.3 %shard_map.67.refs_0_ = f32[32,1024]{1,0:T(8,128)S(1)} custom-call(s32[3]{0:T(128)S(1)} %pad_add_fusion.where, bf16[16,7168]{1,0:T(8,128)(2,1)S(1)} %collective-permute-done.29.mine_ref, bf16[16,7168]{1,0:T(8,128)(2,1)S(1)} %collective-permute-done.30.other_ref, bf16[1024,7168]{1,0:T(8,128)(2,1)S(1)} %get-tuple-element.37.source_ref.refs_0_), custom_call_target="tpu_custom_call" | custom-call | flops 3758096384 | bytes 14680064 | tf_op jit(solution)/shard_map/pallas_call | solution.py:93
  183.5 5.9 %collective-permute-done.36.refs_5_ = f32[32,1024]{1,0:T(8,128)S(1)} collective-permute-done((f32[32,1024]{1,0:T(8,128)S(1)}, f32[32,1024]{1,0:T(8,128)S(1)}, u32[]{:S(2)}, u32[]{:S(2)}) %collective-permute-start.36) | collective-permute-done | bytes 131104 | tf_op jit(solution)/shard_map/ppermute | solution.py:341
  219.6 6.6 %shard_map.81 = (f32[16,7168]{1,0:T(8,128)S(1)}, bf16[16,7168]{1,0:T(8,128)(2,1)S(1)}) custom-call(s32[3]{0:T(128)S(1)} %pad_add_fusion.where, bf16[4,32,1024]{2,1,0:T(8,128)(2,1)S(1)} %shard_map.73.basis_ref, bf16[4,1024,7168]{2,1,0:T(8,128)(2,1)} %source_ref.3, bf16[16,7168]{1,0:T(8,128)(2,1)S(1)} %get-tuple-element.51.rest_0_), custom_call_target="tpu_custom_call" | custom-call | flops 3758096384 | bytes 14680064 | tf_op jit(solution)/shard_map/pallas_call | solution.py:152
  226.8 4.3 %collective-permute-start.48 = (bf16[16,7168]{1,0:T(8,128)(2,1)S(1)}, bf16[16,7168]{1,0:T(8,128)(2,1)S(1)}, u32[]{:S(2)}, u32[]{:S(2)}) collective-permute-start(bf16[16,7168]{1,0:T(8,128)(2,1)S(1)} %shard_map.82), channel_id=1, source_target_pairs={{0,24},{4,28},{8,16},{12,20},{16,8},{20,12},{24,0},{28,4},{1,25},{... | collective-permute-start | bytes 688136 | tf_op jit(solution)/shard_map/ppermute | solution.py:341
  237.1 8.8 %collective-permute-done.50.refs_3_ = bf16[16,7168]{1,0:T(8,128)(2,1)S(1)} collective-permute-done((bf16[16,7168]{1,0:T(8,128)(2,1)S(1)}, bf16[16,7168]{1,0:T(8,128)(2,1)S(1)}, u32[]{:S(2)}, u32[]{:S(2)}) %collective-permute-start.50) | collective-permute-done | bytes 229408 | tf_op jit(solution)/shard_map/ppermute | solution.py:341
  246.0 4.9 %collective-permute-start.55 = (bf16[16,7168]{1,0:T(8,128)(2,1)S(1)}, bf16[16,7168]{1,0:T(8,128)(2,1)S(1)}, u32[]{:S(2)}, u32[]{:S(2)}) collective-permute-start(bf16[16,7168]{1,0:T(8,128)(2,1)S(1)} %shard_map.85.mine_ref), channel_id=1, source_target_pairs={{0,8},{4,12},{8,0},{12,4},{16,24},{20,28},{24,16},{28,20},{1,9},{5... | collective-permute-start | bytes 688136 | tf_op jit(solution)/shard_map/ppermute | solution.py:341
  254.3 5.5 %collective-permute-done.55.mine_ref = bf16[16,7168]{1,0:T(8,128)(2,1)S(1)} collective-permute-done((bf16[16,7168]{1,0:T(8,128)(2,1)S(1)}, bf16[16,7168]{1,0:T(8,128)(2,1)S(1)}, u32[]{:S(2)}, u32[]{:S(2)}) %collective-permute-start.55) | collective-permute-done | bytes 229408 | tf_op jit(solution)/shard_map/ppermute | solution.py:341
  259.7 10.4 %collective-permute-done.53.mine_ref = bf16[16,7168]{1,0:T(8,128)(2,1)S(1)} collective-permute-done((bf16[16,7168]{1,0:T(8,128)(2,1)S(1)}, bf16[16,7168]{1,0:T(8,128)(2,1)S(1)}, u32[]{:S(2)}, u32[]{:S(2)}) %collective-permute-start.53) | collective-permute-done | bytes 229408 | tf_op jit(solution)/shard_map/ppermute | solution.py:341
  (158 shorter events, 122.6 us)
Async XLA Ops:
  5.1 19.7 %collective-permute-start.5 = (bf16[16,7168]{1,0:T(8,128)(2,1)}, bf16[16,7168]{1,0:T(8,128)(2,1)S(1)}, u32[]{:S(2)}, u32[]{:S(2)}) collective-permute-start(bf16[16,7168]{1,0:T(8,128)(2,1)} %bitcast.8), channel_id=1, source_target_pairs={{0,16},{4,20},{8,24},{12,28},{16,0},{20,4},{24,8},{28,12},{1,17},{... | collective-permute-start | bytes 688136 | tf_op jit(solution)/shard_map/ppermute | solution.py:341
  5.1 19.7 %collective-permute-start = (bf16[16,7168]{1,0:T(8,128)(2,1)}, bf16[16,7168]{1,0:T(8,128)(2,1)S(1)}, u32[]{:S(2)}, u32[]{:S(2)}) collective-permute-start(bf16[16,7168]{1,0:T(8,128)(2,1)} %bitcast.9), channel_id=1, source_target_pairs={{0,8},{4,12},{8,0},{12,4},{16,24},{20,28},{24,16},{28,20},{1,9},{5... | collective-permute-start | bytes 688136 | tf_op jit(solution)/shard_map/ppermute | solution.py:341
  5.6 19.7 %collective-permute-start.2 = (bf16[16,7168]{1,0:T(8,128)(2,1)}, bf16[16,7168]{1,0:T(8,128)(2,1)S(1)}, u32[]{:S(2)}, u32[]{:S(2)}) collective-permute-start(bf16[16,7168]{1,0:T(8,128)(2,1)} %bitcast.10), channel_id=1, source_target_pairs={{0,4},{4,0},{8,12},{12,8},{16,20},{20,16},{24,28},{28,24},{1,5},{5... | collective-permute-start | bytes 688136 | tf_op jit(solution)/shard_map/ppermute | solution.py:341
  11.9 39.5 %collective-permute-start.10 = (bf16[16,7168]{1,0:T(8,128)(2,1)S(1)}, bf16[16,7168]{1,0:T(8,128)(2,1)S(1)}, u32[]{:S(2)}, u32[]{:S(2)}) collective-permute-start(bf16[16,7168]{1,0:T(8,128)(2,1)S(1)} %collective-permute-done.9.mine_ref), channel_id=1, source_target_pairs={{0,4},{4,0},{8,12},{12,8},{16,20},{20,16},{24,28},{28,24},{1,5},{5... | collective-permute-start | bytes 688136 | tf_op jit(solution)/shard_map/ppermute | solution.py:341
  24.8 18.6 %collective-permute-start.6 = (bf16[16,7168]{1,0:T(8,128)(2,1)S(1)}, bf16[16,7168]{1,0:T(8,128)(2,1)S(1)}, u32[]{:S(2)}, u32[]{:S(2)}) collective-permute-start(bf16[16,7168]{1,0:T(8,128)(2,1)S(1)} %collective-permute-done.5.mine_ref), channel_id=1, source_target_pairs={{0,4},{4,0},{8,12},{12,8},{16,20},{20,16},{24,28},{28,24},{1,5},{5... | collective-permute-start | bytes 688136 | tf_op jit(solution)/shard_map/ppermute | solution.py:341
  41.9 18.4 %collective-permute-start.3 = (f32[64,1024]{1,0:T(8,128)S(1)}, f32[64,1024]{1,0:T(8,128)S(1)}, u32[]{:S(2)}, u32[]{:S(2)}) collective-permute-start(f32[64,1024]{1,0:T(8,128)S(1)} %get-tuple-element.31.refs_0_), channel_id=1, source_target_pairs={{0,1},{1,0},{2,3},{3,2},{4,5},{5,4},{6,7},{7,6},{8,9},{9,8},{10,11... | collective-permute-start | bytes 786440 | tf_op jit(solution)/shard_map/ppermute | solution.py:341
  90.7 15.6 %collective-permute-start.18 = (bf16[16,7168]{1,0:T(8,128)(2,1)S(1)}, bf16[16,7168]{1,0:T(8,128)(2,1)S(1)}, u32[]{:S(2)}, u32[]{:S(2)}) collective-permute-start(bf16[16,7168]{1,0:T(8,128)(2,1)S(1)} %get-tuple-element.39.rest_0_), channel_id=1, source_target_pairs={{0,4},{4,0},{8,12},{12,8},{16,20},{20,16},{24,28},{28,24},{1,5},{5... | collective-permute-start | bytes 688136 | tf_op jit(solution)/shard_map/ppermute | solution.py:341
  108.0 21.2 %collective-permute-start.21 = (bf16[16,7168]{1,0:T(8,128)(2,1)S(1)}, bf16[16,7168]{1,0:T(8,128)(2,1)S(1)}, u32[]{:S(2)}, u32[]{:S(2)}) collective-permute-start(bf16[16,7168]{1,0:T(8,128)(2,1)S(1)} %shard_map.61), channel_id=1, source_target_pairs={{0,16},{4,20},{8,24},{12,28},{16,0},{20,4},{24,8},{28,12},{1,17},{... | collective-permute-start | bytes 688136 | tf_op jit(solution)/shard_map/ppermute | solution.py:341
  109.1 20.1 %collective-permute-start.23 = (bf16[16,7168]{1,0:T(8,128)(2,1)S(1)}, bf16[16,7168]{1,0:T(8,128)(2,1)S(1)}, u32[]{:S(2)}, u32[]{:S(2)}) collective-permute-start(bf16[16,7168]{1,0:T(8,128)(2,1)S(1)} %shard_map.62), channel_id=1, source_target_pairs={{0,8},{4,12},{8,0},{12,4},{16,24},{20,28},{24,16},{28,20},{1,9},{5... | collective-permute-start | bytes 688136 | tf_op jit(solution)/shard_map/ppermute | solution.py:341
  131.9 18.5 %collective-permute-start.29 = (bf16[16,7168]{1,0:T(8,128)(2,1)S(1)}, bf16[16,7168]{1,0:T(8,128)(2,1)S(1)}, u32[]{:S(2)}, u32[]{:S(2)}) collective-permute-start(bf16[16,7168]{1,0:T(8,128)(2,1)S(1)} %shard_map.63.mine_ref), channel_id=1, source_target_pairs={{0,16},{4,20},{8,24},{12,28},{16,0},{20,4},{24,8},{28,12},{1,17},{... | collective-permute-start | bytes 688136 | tf_op jit(solution)/shard_map/ppermute | solution.py:341
  131.9 18.5 %collective-permute-start.24 = (bf16[16,7168]{1,0:T(8,128)(2,1)S(1)}, bf16[16,7168]{1,0:T(8,128)(2,1)S(1)}, u32[]{:S(2)}, u32[]{:S(2)}) collective-permute-start(bf16[16,7168]{1,0:T(8,128)(2,1)S(1)} %shard_map.63.mine_ref), channel_id=1, source_target_pairs={{0,8},{4,12},{8,0},{12,4},{16,24},{20,28},{24,16},{28,20},{1,9},{5... | collective-permute-start | bytes 688136 | tf_op jit(solution)/shard_map/ppermute | solution.py:341
  133.8 17.1 %collective-permute-start.26 = (bf16[16,7168]{1,0:T(8,128)(2,1)S(1)}, bf16[16,7168]{1,0:T(8,128)(2,1)S(1)}, u32[]{:S(2)}, u32[]{:S(2)}) collective-permute-start(bf16[16,7168]{1,0:T(8,128)(2,1)S(1)} %shard_map.63.mine_ref), channel_id=1, source_target_pairs={{0,4},{4,0},{8,12},{12,8},{16,20},{20,16},{24,28},{28,24},{1,5},{5... | collective-permute-start | bytes 688136 | tf_op jit(solution)/shard_map/ppermute | solution.py:341
  139.8 19.4 %collective-permute-start.34 = (bf16[16,7168]{1,0:T(8,128)(2,1)S(1)}, bf16[16,7168]{1,0:T(8,128)(2,1)S(1)}, u32[]{:S(2)}, u32[]{:S(2)}) collective-permute-start(bf16[16,7168]{1,0:T(8,128)(2,1)S(1)} %collective-permute-done.33.mine_ref), channel_id=1, source_target_pairs={{0,4},{4,0},{8,12},{12,8},{16,20},{20,16},{24,28},{28,24},{1,5},{5... | collective-permute-start | bytes 688136 | tf_op jit(solution)/shard_map/ppermute | solution.py:341
  150.4 21.3 %collective-permute-start.30 = (bf16[16,7168]{1,0:T(8,128)(2,1)S(1)}, bf16[16,7168]{1,0:T(8,128)(2,1)S(1)}, u32[]{:S(2)}, u32[]{:S(2)}) collective-permute-start(bf16[16,7168]{1,0:T(8,128)(2,1)S(1)} %collective-permute-done.29.mine_ref), channel_id=1, source_target_pairs={{0,4},{4,0},{8,12},{12,8},{16,20},{20,16},{24,28},{28,24},{1,5},{5... | collective-permute-start | bytes 688136 | tf_op jit(solution)/shard_map/ppermute | solution.py:341
  215.6 15.5 %collective-permute-start.41 = (bf16[128,1024]{1,0:T(8,128)(2,1)S(1)}, bf16[128,1024]{1,0:T(8,128)(2,1)S(1)}, u32[]{:S(2)}, u32[]{:S(2)}) collective-permute-start(bf16[128,1024]{1,0:T(8,128)(2,1)S(1)} %bitcast.5), channel_id=1, source_target_pairs={{0,16},{4,20},{9,25},{13,29},{18,2},{22,6},{27,11},{31,15}} | collective-permute-start | bytes 786440 | tf_op jit(solution)/shard_map/ppermute | solution.py:411
  226.5 19.3 %collective-permute-start.50 = (bf16[16,7168]{1,0:T(8,128)(2,1)S(1)}, bf16[16,7168]{1,0:T(8,128)(2,1)S(1)}, u32[]{:S(2)}, u32[]{:S(2)}) collective-permute-start(bf16[16,7168]{1,0:T(8,128)(2,1)S(1)} %shard_map.83), channel_id=1, source_target_pairs={{0,16},{4,20},{8,24},{12,28},{16,0},{20,4},{24,8},{28,12},{1,17},{... | collective-permute-start | bytes 688136 | tf_op jit(solution)/shard_map/ppermute | solution.py:341
  226.8 19.1 %collective-permute-start.48 = (bf16[16,7168]{1,0:T(8,128)(2,1)S(1)}, bf16[16,7168]{1,0:T(8,128)(2,1)S(1)}, u32[]{:S(2)}, u32[]{:S(2)}) collective-permute-start(bf16[16,7168]{1,0:T(8,128)(2,1)S(1)} %shard_map.82), channel_id=1, source_target_pairs={{0,24},{4,28},{8,16},{12,20},{16,8},{20,12},{24,0},{28,4},{1,25},{... | collective-permute-start | bytes 688136 | tf_op jit(solution)/shard_map/ppermute | solution.py:341
  231.7 19.4 %collective-permute-start.42 = (bf16[128,1024]{1,0:T(8,128)(2,1)S(1)}, bf16[128,1024]{1,0:T(8,128)(2,1)S(1)}, u32[]{:S(2)}, u32[]{:S(2)}) collective-permute-start(bf16[128,1024]{1,0:T(8,128)(2,1)S(1)} %shard_map.74.held_ref), channel_id=1, source_target_pairs={{0,8},{4,12},{16,24},{20,28},{9,1},{13,5},{25,17},{29,21},{18,26},... | collective-permute-start | bytes 786440 | tf_op jit(solution)/shard_map/ppermute | solution.py:411
  251.0 19.2 %collective-permute-start.53 = (bf16[16,7168]{1,0:T(8,128)(2,1)S(1)}, bf16[16,7168]{1,0:T(8,128)(2,1)S(1)}, u32[]{:S(2)}, u32[]{:S(2)}) collective-permute-start(bf16[16,7168]{1,0:T(8,128)(2,1)S(1)} %shard_map.85.mine_ref), channel_id=1, source_target_pairs={{0,16},{4,20},{8,24},{12,28},{16,0},{20,4},{24,8},{28,12},{1,17},{... | collective-permute-start | bytes 688136 | tf_op jit(solution)/shard_map/ppermute | solution.py:341
  251.6 19.0 %collective-permute-start.43 = (bf16[128,1024]{1,0:T(8,128)(2,1)S(1)}, bf16[128,1024]{1,0:T(8,128)(2,1)S(1)}, u32[]{:S(2)}, u32[]{:S(2)}) collective-permute-start(bf16[128,1024]{1,0:T(8,128)(2,1)S(1)} %shard_map.75.mine_ref), channel_id=1, source_target_pairs={{0,4},{4,0},{8,12},{12,8},{16,20},{20,16},{24,28},{28,24},{1,5},{5... | collective-permute-start | bytes 786440 | tf_op jit(solution)/shard_map/ppermute | solution.py:341
  251.7 18.5 %collective-permute-start.60 = (bf16[16,7168]{1,0:T(8,128)(2,1)S(1)}, bf16[16,7168]{1,0:T(8,128)(2,1)S(1)}, u32[]{:S(2)}, u32[]{:S(2)}) collective-permute-start(bf16[16,7168]{1,0:T(8,128)(2,1)S(1)} %shard_map.85.mine_ref), channel_id=1, source_target_pairs={{0,24},{4,28},{8,16},{12,20},{16,8},{20,12},{24,0},{28,4},{1,25},{... | collective-permute-start | bytes 688136 | tf_op jit(solution)/shard_map/ppermute | solution.py:341
  254.1 19.7 %collective-permute-start.57 = (bf16[16,7168]{1,0:T(8,128)(2,1)S(1)}, bf16[16,7168]{1,0:T(8,128)(2,1)S(1)}, u32[]{:S(2)}, u32[]{:S(2)}) collective-permute-start(bf16[16,7168]{1,0:T(8,128)(2,1)S(1)} %shard_map.85.mine_ref), channel_id=1, source_target_pairs={{0,4},{4,0},{8,12},{12,8},{16,20},{20,16},{24,28},{28,24},{1,5},{5... | collective-permute-start | bytes 688136 | tf_op jit(solution)/shard_map/ppermute | solution.py:341
  259.7 15.8 %collective-permute-start.56 = (bf16[16,7168]{1,0:T(8,128)(2,1)S(1)}, bf16[16,7168]{1,0:T(8,128)(2,1)S(1)}, u32[]{:S(2)}, u32[]{:S(2)}) collective-permute-start(bf16[16,7168]{1,0:T(8,128)(2,1)S(1)} %collective-permute-done.55.mine_ref), channel_id=1, source_target_pairs={{0,4},{4,0},{8,12},{12,8},{16,20},{20,16},{24,28},{28,24},{1,5},{5... | collective-permute-start | bytes 688136 | tf_op jit(solution)/shard_map/ppermute | solution.py:341
  279.0 15.5 %collective-permute-start.45 = (f32[4,32,256]{2,1,0:T(8,128)S(1)}, f32[4,32,256]{2,1,0:T(8,128)S(1)}, u32[]{:S(2)}, u32[]{:S(2)}) collective-permute-start(f32[4,32,256]{2,1,0:T(8,128)S(1)} %shard_map.77.refs_0_), channel_id=1, source_target_pairs={{0,2},{1,3},{2,0},{3,1},{4,6},{5,7},{6,4},{7,5},{8,10},{9,11},{10,... | collective-permute-start | bytes 393224 | tf_op jit(solution)/shard_map/ppermute | solution.py:341
  (43 other events, 458.5 us)

commit v4 on v3

--- a/solution.py
+++ b/solution.py
@@ -34,7 +34,7 @@
 
 ROW_CHUNKS = 4
 COL_CHUNKS = 8
-STREAM_BANDS = 2
+AHEAD = 2
 STREAM_COLS = 4
 STREAM_MIB = 9
 
@@ -45,14 +45,14 @@
     source_ref, out_ref = refs.pop(0), refs.pop(0)
     query, core = where[0] ^ offset, where[1]
     rows = out_ref.shape[1] // ROW_CHUNKS
-    ahead = STREAM_BANDS if mode == "stream" else ROW_CHUNKS
+    ahead = AHEAD
 
     def band(i):
         return pl.ds(pl.multiple_of(i * rows, 128), rows)
 
     def view(i):
         if mode == "stream":
-            return refs[0].at[lax.rem(i, STREAM_BANDS)]
+            return refs[0].at[lax.rem(i, ahead)]
         return (source_ref if mode == "held" else refs[0]).at[band(i), :]
 
     def fetch(i):
@@ -67,6 +67,12 @@
     def body(i, carry):
         if mode != "held":
             fetch(i).wait()
+        if mode == "load":
+
+            @pl.when(i + ahead < ROW_CHUNKS)
+            def _():
+                fetch(i + ahead).start()
+
         out_ref[carried:, band(i)] = lax.dot_general(
             vectors, view(i)[...], NT, preferred_element_type=F32
         )
@@ -87,7 +93,7 @@
     load = mode == "load"
     scratch = []
     if mode == "stream":
-        scratch.append(pltpu.VMEM((STREAM_BANDS, rows // ROW_CHUNKS, cols), BF16))
+        scratch.append(pltpu.VMEM((AHEAD, rows // ROW_CHUNKS, cols), BF16))
     if mode != "held":
         scratch.append(pltpu.SemaphoreType.DMA((ROW_CHUNKS,)))
     return pl.pallas_call(
@@ -409,29 +415,35 @@
                 for c in range(CORES)
             ]
             received = lax.ppermute(got, ("tok", "par"), sends)
-            got = choose(where, got, received, owners)
-            owners = owners + [o ^ bits for o in owners]
-        return got
+            if bits > 1:
+                got = chosen(got, received, owners)
+                owners = owners + [o ^ bits for o in owners]
+        return got, received, owners
+
+    def chosen(got, received, owners):
+        return choose(where, got, received, owners)
 
     piece = start_block.T
     for i in range(ITERS):
         basis = basis_from(images_from(piece))
         if i == ITERS - 1:
-            spread_rows = spread(basis)
+            spread_parts = spread(basis)
         piece = back_piece(basis)
 
     parts = []
 
     def in_proj(d, mine, other):
-        last = d == chips - 1
-        earlier = parts[-1] if 0 < d and not last else None
-        slot, slots = (0, 1) if last else (d, chips - 1)
+        group = chips // 2
+        earlier = parts[-1] if d % group else None
+        slot, slots = d % group, group
         parts.append(project_in(where, mine, other, hooked_in, slot, slots, earlier))
 
     gathered(piece, in_proj)
+    spread_rows = chosen(*spread_parts)
     other_rows = tok_swap(spread_rows, 1)
     out_proj = project_out(where, spread_rows, other_rows, hooked_out)
-    pairs = [par_pair(out_proj), par_pair(parts[-2]), par_pair(parts[-1])]
+    early, late = parts[chips // 2 - 1], parts[-1]
+    pairs = [par_pair(out_proj), par_pair(early), par_pair(late)]
     return token_scores(where, pairs)
 
 

time: 296 us -> 295 us (level)
  transfers between devices with their start and end apart: 64 -> 64, of which waited for: 27 -> 28; matrix products, arithmetic and copies ran while one was open for 0% -> 0% of each run, Pallas kernels for 29% -> 29%
where the time goes in v4:
time: 295 us; the launch traced here: 294 us
  waiting for transfers between devices  116 us (39%)
  Pallas kernels  111 us (38%)
  starting transfers between devices  64.9 us (22%)
    ppermute x62, waiting for transfers between devices, xor_permute(): return lax.ppermute(x, axis, [(i, i ^ bits) for i in range(size)])  116 us
    ppermute x62, starting transfers between devices, xor_permute(): return lax.ppermute(x, axis, [(i, i ^ bits) for i in range(size)])  59.6 us
    pallas_call x8, Pallas kernels, images_of_query(): pl.pallas_call(functools.partial(images_body, carried=carried, mode=mode,...  54.1 us
    pallas_call x8, Pallas kernels, back_of_query(): pl.pallas_call(functools.partial(back_body, stream=stream, ties=len(after...  36.5 us
    pallas_call x2, Pallas kernels, orthonormal(): pl.pallas_call(basis_body, in_specs=[VMEM] * (1 + len(grams)), out_specs=...  7.72 us
    pallas_call x4, Pallas kernels, project_in(): pl.pallas_call(project_in_body, grid=(1,), in_specs=[SMEM, VMEM, VMEM, VM...  6.66 us
  transfers between devices with their start and end apart: 64, of which 28 were waited for; matrix products, arithmetic and copies ran while one was open for 0% of the time, Pallas kernels for 29%

profile of v4, /device:TPU:0, one launch (start us, length us, event | category | flops | bytes accessed | tf_op | source)
XLA Modules:
  0.0 293.9 jit_solution(3362847237117722494)
XLA Ops:
  0.0 5.1 %collective-permute-start.9 = (bf16[16,7168]{1,0:T(8,128)(2,1)}, bf16[16,7168]{1,0:T(8,128)(2,1)S(1)}, u32[]{:S(2)}, u32[]{:S(2)}) collective-permute-start(bf16[16,7168]{1,0:T(8,128)(2,1)} %bitcast.7), channel_id=1, source_target_pairs={{0,24},{4,28},{8,16},{12,20},{16,8},{20,12},{24,0},{28,4},{1,25},{... | collective-permute-start | bytes 688136 | tf_op jit(solution)/shard_map/ppermute | solution.py:347
  5.7 6.2 %collective-permute-done.9.mine_ref = bf16[16,7168]{1,0:T(8,128)(2,1)S(1)} collective-permute-done((bf16[16,7168]{1,0:T(8,128)(2,1)}, bf16[16,7168]{1,0:T(8,128)(2,1)S(1)}, u32[]{:S(2)}, u32[]{:S(2)}) %collective-permute-start.9) | collective-permute-done | bytes 229408 | tf_op jit(solution)/shard_map/ppermute | solution.py:347
  11.9 12.9 %collective-permute-done.5.mine_ref = bf16[16,7168]{1,0:T(8,128)(2,1)S(1)} collective-permute-done((bf16[16,7168]{1,0:T(8,128)(2,1)}, bf16[16,7168]{1,0:T(8,128)(2,1)S(1)}, u32[]{:S(2)}, u32[]{:S(2)}) %collective-permute-start.5) | collective-permute-done | bytes 229408 | tf_op jit(solution)/shard_map/ppermute | solution.py:347
  26.2 8.3 %shard_map.46.refs_0_ = f32[32,1024]{1,0:T(8,128)S(1)} custom-call(s32[3]{0:T(128)S(1)} %pad_add_fusion.where, bf16[16,7168]{1,0:T(8,128)(2,1)S(1)} %bitcast.11, bf16[16,7168]{1,0:T(8,128)(2,1)S(1)} %collective-permute-done.2.other_ref, bf16[4,1024,7168]{2,1,0:T(8,128)(2,1)} %source_ref.3), custom_call_target="tpu_custom_call" | custom-call | flops 3758096384 | bytes 14680064 | tf_op jit(solution)/shard_map/pallas_call | solution.py:99
  34.5 7.3 %shard_map.47 = (f32[64,1024]{1,0:T(8,128)S(1)}, bf16[1024,7168]{1,0:T(8,128)(2,1)S(1)}) custom-call(s32[3]{0:T(128)S(1)} %pad_add_fusion.where, bf16[16,7168]{1,0:T(8,128)(2,1)S(1)} %collective-permute-done.mine_ref, bf16[16,7168]{1,0:T(8,128)(2,1)S(1)} %collective-permute-done.1.other_ref, f32[32,1024]{1,0:T(8,128)S(1)} %shard_map.46.refs_0_, ...), custom_call_target="tpu_custom_call" | custom-call | flops 3758096384 | bytes 14680064 | tf_op jit(solution)/shard_map/pallas_call | solution.py:99
  43.4 7.3 %shard_map.49 = (f32[32,1024]{1,0:T(8,128)S(1)}, bf16[1024,7168]{1,0:T(8,128)(2,1)S(1)}) custom-call(s32[3]{0:T(128)S(1)} %pad_add_fusion.where, bf16[16,7168]{1,0:T(8,128)(2,1)S(1)} %collective-permute-done.5.mine_ref, bf16[16,7168]{1,0:T(8,128)(2,1)S(1)} %collective-permute-done.6.other_ref, bf16[4,1024,7168]{2,1,0:T(8,128)(2,1)} %source_ref.3), custom_call_target="tpu_custom_call" | custom-call | flops 3758096384 | bytes 14680064 | tf_op jit(solution)/shard_map/pallas_call | solution.py:99
  51.3 7.3 %shard_map.51 = (f32[32,1024]{1,0:T(8,128)S(1)}, bf16[1024,7168]{1,0:T(8,128)(2,1)S(1)}) custom-call(s32[3]{0:T(128)S(1)} %pad_add_fusion.where, bf16[16,7168]{1,0:T(8,128)(2,1)S(1)} %collective-permute-done.9.mine_ref, bf16[16,7168]{1,0:T(8,128)(2,1)S(1)} %collective-permute-done.10.other_ref, bf16[4,1024,7168]{2,1,0:T(8,128)(2,1)} %source_ref.3), custom_call_target="tpu_custom_call" | custom-call | flops 3758096384 | bytes 14680064 | tf_op jit(solution)/shard_map/pallas_call | solution.py:99
  65.3 6.6 %collective-permute-done.8.refs_3_ = f32[32,1024]{1,0:T(8,128)S(1)} collective-permute-done((f32[32,1024]{1,0:T(8,128)S(1)}, f32[32,1024]{1,0:T(8,128)S(1)}, u32[]{:S(2)}, u32[]{:S(2)}) %collective-permute-start.8) | collective-permute-done | bytes 131104 | tf_op jit(solution)/shard_map/ppermute | solution.py:347
  99.1 6.6 %shard_map.59 = (f32[16,7168]{1,0:T(8,128)S(1)}, bf16[16,7168]{1,0:T(8,128)(2,1)S(1)}) custom-call(s32[3]{0:T(128)S(1)} %pad_add_fusion.where, bf16[4,32,1024]{2,1,0:T(8,128)(2,1)S(1)} %shard_map.55.basis_ref, bf16[4,1024,7168]{2,1,0:T(8,128)(2,1)} %source_ref.3, bf16[16,7168]{1,0:T(8,128)(2,1)S(1)} %get-tuple-element.41.rest_0_), custom_call_target="tpu_custom_call" | custom-call | flops 3758096384 | bytes 14680064 | tf_op jit(solution)/shard_map/pallas_call | solution.py:158
  111.0 5.8 %collective-permute-done.19.refs_2_ = bf16[16,7168]{1,0:T(8,128)(2,1)S(1)} collective-permute-done((bf16[16,7168]{1,0:T(8,128)(2,1)S(1)}, bf16[16,7168]{1,0:T(8,128)(2,1)S(1)}, u32[]{:S(2)}, u32[]{:S(2)}) %collective-permute-start.19) | collective-permute-done | bytes 229408 | tf_op jit(solution)/shard_map/ppermute | solution.py:347
  116.8 12.3 %collective-permute-done.21.refs_3_ = bf16[16,7168]{1,0:T(8,128)(2,1)S(1)} collective-permute-done((bf16[16,7168]{1,0:T(8,128)(2,1)S(1)}, bf16[16,7168]{1,0:T(8,128)(2,1)S(1)}, u32[]{:S(2)}, u32[]{:S(2)}) %collective-permute-start.21) | collective-permute-done | bytes 229408 | tf_op jit(solution)/shard_map/ppermute | solution.py:347
  133.7 6.0 %collective-permute-done.33.mine_ref = bf16[16,7168]{1,0:T(8,128)(2,1)S(1)} collective-permute-done((bf16[16,7168]{1,0:T(8,128)(2,1)S(1)}, bf16[16,7168]{1,0:T(8,128)(2,1)S(1)}, u32[]{:S(2)}, u32[]{:S(2)}) %collective-permute-start.33) | collective-permute-done | bytes 229408 | tf_op jit(solution)/shard_map/ppermute | solution.py:347
  139.7 10.6 %collective-permute-done.29.mine_ref = bf16[16,7168]{1,0:T(8,128)(2,1)S(1)} collective-permute-done((bf16[16,7168]{1,0:T(8,128)(2,1)S(1)}, bf16[16,7168]{1,0:T(8,128)(2,1)S(1)}, u32[]{:S(2)}, u32[]{:S(2)}) %collective-permute-start.29) | collective-permute-done | bytes 229408 | tf_op jit(solution)/shard_map/ppermute | solution.py:347
  150.8 8.3 %shard_map.64.refs_0_ = f32[32,1024]{1,0:T(8,128)S(1)} custom-call(s32[3]{0:T(128)S(1)} %pad_add_fusion.where, bf16[16,7168]{1,0:T(8,128)(2,1)S(1)} %shard_map.63.mine_ref, bf16[16,7168]{1,0:T(8,128)(2,1)S(1)} %collective-permute-done.26.other_ref, bf16[4,1024,7168]{2,1,0:T(8,128)(2,1)} %source_ref.3), custom_call_target="tpu_custom_call" | custom-call | flops 3758096384 | bytes 14680064 | tf_op jit(solution)/shard_map/pallas_call | solution.py:99
  159.1 5.2 %shard_map.69.refs_0_ = f32[32,1024]{1,0:T(8,128)S(1)} custom-call(s32[3]{0:T(128)S(1)} %pad_add_fusion.where, bf16[16,7168]{1,0:T(8,128)(2,1)S(1)} %collective-permute-done.33.mine_ref, bf16[16,7168]{1,0:T(8,128)(2,1)S(1)} %collective-permute-done.34.other_ref, bf16[1024,7168]{1,0:T(8,128)(2,1)S(1)} %get-tuple-element.38.source_ref.refs_0_), custom_call_target="tpu_custom_call" | custom-call | flops 3758096384 | bytes 14680064 | tf_op jit(solution)/shard_map/pallas_call | solution.py:99
  164.9 5.2 %shard_map.65.refs_0_ = f32[64,1024]{1,0:T(8,128)S(1)} custom-call(s32[3]{0:T(128)S(1)} %pad_add_fusion.where, bf16[16,7168]{1,0:T(8,128)(2,1)S(1)} %collective-permute-done.24.mine_ref, bf16[16,7168]{1,0:T(8,128)(2,1)S(1)} %collective-permute-done.25.other_ref, f32[32,1024]{1,0:T(8,128)S(1)} %shard_map.64.refs_0_, ...), custom_call_target="tpu_custom_call" | custom-call | flops 3758096384 | bytes 14680064 | tf_op jit(solution)/shard_map/pallas_call | solution.py:99
  171.6 5.3 %shard_map.67.refs_0_ = f32[32,1024]{1,0:T(8,128)S(1)} custom-call(s32[3]{0:T(128)S(1)} %pad_add_fusion.where, bf16[16,7168]{1,0:T(8,128)(2,1)S(1)} %collective-permute-done.29.mine_ref, bf16[16,7168]{1,0:T(8,128)(2,1)S(1)} %collective-permute-done.30.other_ref, bf16[1024,7168]{1,0:T(8,128)(2,1)S(1)} %get-tuple-element.37.source_ref.refs_0_), custom_call_target="tpu_custom_call" | custom-call | flops 3758096384 | bytes 14680064 | tf_op jit(solution)/shard_map/pallas_call | solution.py:99
  183.5 5.9 %collective-permute-done.36.refs_5_ = f32[32,1024]{1,0:T(8,128)S(1)} collective-permute-done((f32[32,1024]{1,0:T(8,128)S(1)}, f32[32,1024]{1,0:T(8,128)S(1)}, u32[]{:S(2)}, u32[]{:S(2)}) %collective-permute-start.36) | collective-permute-done | bytes 131104 | tf_op jit(solution)/shard_map/ppermute | solution.py:347
  219.5 6.6 %shard_map.81 = (f32[16,7168]{1,0:T(8,128)S(1)}, bf16[16,7168]{1,0:T(8,128)(2,1)S(1)}) custom-call(s32[3]{0:T(128)S(1)} %pad_add_fusion.where, bf16[4,32,1024]{2,1,0:T(8,128)(2,1)S(1)} %shard_map.73.basis_ref, bf16[4,1024,7168]{2,1,0:T(8,128)(2,1)} %source_ref.3, bf16[16,7168]{1,0:T(8,128)(2,1)S(1)} %get-tuple-element.51.rest_0_), custom_call_target="tpu_custom_call" | custom-call | flops 3758096384 | bytes 14680064 | tf_op jit(solution)/shard_map/pallas_call | solution.py:158
  226.7 4.3 %collective-permute-start.48 = (bf16[16,7168]{1,0:T(8,128)(2,1)S(1)}, bf16[16,7168]{1,0:T(8,128)(2,1)S(1)}, u32[]{:S(2)}, u32[]{:S(2)}) collective-permute-start(bf16[16,7168]{1,0:T(8,128)(2,1)S(1)} %shard_map.82), channel_id=1, source_target_pairs={{0,24},{4,28},{8,16},{12,20},{16,8},{20,12},{24,0},{28,4},{1,25},{... | collective-permute-start | bytes 688136 | tf_op jit(solution)/shard_map/ppermute | solution.py:347
  232.9 4.1 %collective-permute-done.52.refs_4_ = bf16[16,7168]{1,0:T(8,128)(2,1)S(1)} collective-permute-done((bf16[16,7168]{1,0:T(8,128)(2,1)S(1)}, bf16[16,7168]{1,0:T(8,128)(2,1)S(1)}, u32[]{:S(2)}, u32[]{:S(2)}) %collective-permute-start.52) | collective-permute-done | bytes 229408 | tf_op jit(solution)/shard_map/ppermute | solution.py:347
  237.0 8.8 %collective-permute-done.50.refs_3_ = bf16[16,7168]{1,0:T(8,128)(2,1)S(1)} collective-permute-done((bf16[16,7168]{1,0:T(8,128)(2,1)S(1)}, bf16[16,7168]{1,0:T(8,128)(2,1)S(1)}, u32[]{:S(2)}, u32[]{:S(2)}) %collective-permute-start.50) | collective-permute-done | bytes 229408 | tf_op jit(solution)/shard_map/ppermute | solution.py:347
  246.0 5.0 %collective-permute-start.60 = (bf16[16,7168]{1,0:T(8,128)(2,1)S(1)}, bf16[16,7168]{1,0:T(8,128)(2,1)S(1)}, u32[]{:S(2)}, u32[]{:S(2)}) collective-permute-start(bf16[16,7168]{1,0:T(8,128)(2,1)S(1)} %shard_map.85.mine_ref), channel_id=1, source_target_pairs={{0,16},{4,20},{8,24},{12,28},{16,0},{20,4},{24,8},{28,12},{1,17},{... | collective-permute-start | bytes 688136 | tf_op jit(solution)/shard_map/ppermute | solution.py:347
  254.4 12.8 %collective-permute-done.60.mine_ref = bf16[16,7168]{1,0:T(8,128)(2,1)S(1)} collective-permute-done((bf16[16,7168]{1,0:T(8,128)(2,1)S(1)}, bf16[16,7168]{1,0:T(8,128)(2,1)S(1)}, u32[]{:S(2)}, u32[]{:S(2)}) %collective-permute-start.60) | collective-permute-done | bytes 229408 | tf_op jit(solution)/shard_map/ppermute | solution.py:347
  (158 shorter events, 119.9 us)
Async XLA Ops:
  5.1 19.7 %collective-permute-start.5 = (bf16[16,7168]{1,0:T(8,128)(2,1)}, bf16[16,7168]{1,0:T(8,128)(2,1)S(1)}, u32[]{:S(2)}, u32[]{:S(2)}) collective-permute-start(bf16[16,7168]{1,0:T(8,128)(2,1)} %bitcast.8), channel_id=1, source_target_pairs={{0,16},{4,20},{8,24},{12,28},{16,0},{20,4},{24,8},{28,12},{1,17},{... | collective-permute-start | bytes 688136 | tf_op jit(solution)/shard_map/ppermute | solution.py:347
  5.1 19.7 %collective-permute-start = (bf16[16,7168]{1,0:T(8,128)(2,1)}, bf16[16,7168]{1,0:T(8,128)(2,1)S(1)}, u32[]{:S(2)}, u32[]{:S(2)}) collective-permute-start(bf16[16,7168]{1,0:T(8,128)(2,1)} %bitcast.9), channel_id=1, source_target_pairs={{0,8},{4,12},{8,0},{12,4},{16,24},{20,28},{24,16},{28,20},{1,9},{5... | collective-permute-start | bytes 688136 | tf_op jit(solution)/shard_map/ppermute | solution.py:347
  5.6 19.7 %collective-permute-start.2 = (bf16[16,7168]{1,0:T(8,128)(2,1)}, bf16[16,7168]{1,0:T(8,128)(2,1)S(1)}, u32[]{:S(2)}, u32[]{:S(2)}) collective-permute-start(bf16[16,7168]{1,0:T(8,128)(2,1)} %bitcast.10), channel_id=1, source_target_pairs={{0,4},{4,0},{8,12},{12,8},{16,20},{20,16},{24,28},{28,24},{1,5},{5... | collective-permute-start | bytes 688136 | tf_op jit(solution)/shard_map/ppermute | solution.py:347
  11.9 39.5 %collective-permute-start.10 = (bf16[16,7168]{1,0:T(8,128)(2,1)S(1)}, bf16[16,7168]{1,0:T(8,128)(2,1)S(1)}, u32[]{:S(2)}, u32[]{:S(2)}) collective-permute-start(bf16[16,7168]{1,0:T(8,128)(2,1)S(1)} %collective-permute-done.9.mine_ref), channel_id=1, source_target_pairs={{0,4},{4,0},{8,12},{12,8},{16,20},{20,16},{24,28},{28,24},{1,5},{5... | collective-permute-start | bytes 688136 | tf_op jit(solution)/shard_map/ppermute | solution.py:347
  24.8 18.6 %collective-permute-start.6 = (bf16[16,7168]{1,0:T(8,128)(2,1)S(1)}, bf16[16,7168]{1,0:T(8,128)(2,1)S(1)}, u32[]{:S(2)}, u32[]{:S(2)}) collective-permute-start(bf16[16,7168]{1,0:T(8,128)(2,1)S(1)} %collective-permute-done.5.mine_ref), channel_id=1, source_target_pairs={{0,4},{4,0},{8,12},{12,8},{16,20},{20,16},{24,28},{28,24},{1,5},{5... | collective-permute-start | bytes 688136 | tf_op jit(solution)/shard_map/ppermute | solution.py:347
  41.9 18.4 %collective-permute-start.3 = (f32[64,1024]{1,0:T(8,128)S(1)}, f32[64,1024]{1,0:T(8,128)S(1)}, u32[]{:S(2)}, u32[]{:S(2)}) collective-permute-start(f32[64,1024]{1,0:T(8,128)S(1)} %get-tuple-element.31.refs_0_), channel_id=1, source_target_pairs={{0,1},{1,0},{2,3},{3,2},{4,5},{5,4},{6,7},{7,6},{8,9},{9,8},{10,11... | collective-permute-start | bytes 786440 | tf_op jit(solution)/shard_map/ppermute | solution.py:347
  90.6 15.6 %collective-permute-start.18 = (bf16[16,7168]{1,0:T(8,128)(2,1)S(1)}, bf16[16,7168]{1,0:T(8,128)(2,1)S(1)}, u32[]{:S(2)}, u32[]{:S(2)}) collective-permute-start(bf16[16,7168]{1,0:T(8,128)(2,1)S(1)} %get-tuple-element.39.rest_0_), channel_id=1, source_target_pairs={{0,4},{4,0},{8,12},{12,8},{16,20},{20,16},{24,28},{28,24},{1,5},{5... | collective-permute-start | bytes 688136 | tf_op jit(solution)/shard_map/ppermute | solution.py:347
  108.0 21.2 %collective-permute-start.21 = (bf16[16,7168]{1,0:T(8,128)(2,1)S(1)}, bf16[16,7168]{1,0:T(8,128)(2,1)S(1)}, u32[]{:S(2)}, u32[]{:S(2)}) collective-permute-start(bf16[16,7168]{1,0:T(8,128)(2,1)S(1)} %shard_map.61), channel_id=1, source_target_pairs={{0,16},{4,20},{8,24},{12,28},{16,0},{20,4},{24,8},{28,12},{1,17},{... | collective-permute-start | bytes 688136 | tf_op jit(solution)/shard_map/ppermute | solution.py:347
  109.0 20.1 %collective-permute-start.23 = (bf16[16,7168]{1,0:T(8,128)(2,1)S(1)}, bf16[16,7168]{1,0:T(8,128)(2,1)S(1)}, u32[]{:S(2)}, u32[]{:S(2)}) collective-permute-start(bf16[16,7168]{1,0:T(8,128)(2,1)S(1)} %shard_map.62), channel_id=1, source_target_pairs={{0,8},{4,12},{8,0},{12,4},{16,24},{20,28},{24,16},{28,20},{1,9},{5... | collective-permute-start | bytes 688136 | tf_op jit(solution)/shard_map/ppermute | solution.py:347
  131.8 18.5 %collective-permute-start.29 = (bf16[16,7168]{1,0:T(8,128)(2,1)S(1)}, bf16[16,7168]{1,0:T(8,128)(2,1)S(1)}, u32[]{:S(2)}, u32[]{:S(2)}) collective-permute-start(bf16[16,7168]{1,0:T(8,128)(2,1)S(1)} %shard_map.63.mine_ref), channel_id=1, source_target_pairs={{0,16},{4,20},{8,24},{12,28},{16,0},{20,4},{24,8},{28,12},{1,17},{... | collective-permute-start | bytes 688136 | tf_op jit(solution)/shard_map/ppermute | solution.py:347
  131.8 18.5 %collective-permute-start.24 = (bf16[16,7168]{1,0:T(8,128)(2,1)S(1)}, bf16[16,7168]{1,0:T(8,128)(2,1)S(1)}, u32[]{:S(2)}, u32[]{:S(2)}) collective-permute-start(bf16[16,7168]{1,0:T(8,128)(2,1)S(1)} %shard_map.63.mine_ref), channel_id=1, source_target_pairs={{0,8},{4,12},{8,0},{12,4},{16,24},{20,28},{24,16},{28,20},{1,9},{5... | collective-permute-start | bytes 688136 | tf_op jit(solution)/shard_map/ppermute | solution.py:347
  133.7 17.1 %collective-permute-start.26 = (bf16[16,7168]{1,0:T(8,128)(2,1)S(1)}, bf16[16,7168]{1,0:T(8,128)(2,1)S(1)}, u32[]{:S(2)}, u32[]{:S(2)}) collective-permute-start(bf16[16,7168]{1,0:T(8,128)(2,1)S(1)} %shard_map.63.mine_ref), channel_id=1, source_target_pairs={{0,4},{4,0},{8,12},{12,8},{16,20},{20,16},{24,28},{28,24},{1,5},{5... | collective-permute-start | bytes 688136 | tf_op jit(solution)/shard_map/ppermute | solution.py:347
  139.7 19.4 %collective-permute-start.34 = (bf16[16,7168]{1,0:T(8,128)(2,1)S(1)}, bf16[16,7168]{1,0:T(8,128)(2,1)S(1)}, u32[]{:S(2)}, u32[]{:S(2)}) collective-permute-start(bf16[16,7168]{1,0:T(8,128)(2,1)S(1)} %collective-permute-done.33.mine_ref), channel_id=1, source_target_pairs={{0,4},{4,0},{8,12},{12,8},{16,20},{20,16},{24,28},{28,24},{1,5},{5... | collective-permute-start | bytes 688136 | tf_op jit(solution)/shard_map/ppermute | solution.py:347
  150.3 21.3 %collective-permute-start.30 = (bf16[16,7168]{1,0:T(8,128)(2,1)S(1)}, bf16[16,7168]{1,0:T(8,128)(2,1)S(1)}, u32[]{:S(2)}, u32[]{:S(2)}) collective-permute-start(bf16[16,7168]{1,0:T(8,128)(2,1)S(1)} %collective-permute-done.29.mine_ref), channel_id=1, source_target_pairs={{0,4},{4,0},{8,12},{12,8},{16,20},{20,16},{24,28},{28,24},{1,5},{5... | collective-permute-start | bytes 688136 | tf_op jit(solution)/shard_map/ppermute | solution.py:347
  150.3 14.6 %collective-permute-start.25 = (bf16[16,7168]{1,0:T(8,128)(2,1)S(1)}, bf16[16,7168]{1,0:T(8,128)(2,1)S(1)}, u32[]{:S(2)}, u32[]{:S(2)}) collective-permute-start(bf16[16,7168]{1,0:T(8,128)(2,1)S(1)} %collective-permute-done.24.mine_ref), channel_id=1, source_target_pairs={{0,4},{4,0},{8,12},{12,8},{16,20},{20,16},{24,28},{28,24},{1,5},{5... | collective-permute-start | bytes 688136 | tf_op jit(solution)/shard_map/ppermute | solution.py:347
  164.3 15.3 %collective-permute-start.35 = (f32[32,1024]{1,0:T(8,128)S(1)}, f32[32,1024]{1,0:T(8,128)S(1)}, u32[]{:S(2)}, u32[]{:S(2)}) collective-permute-start(f32[32,1024]{1,0:T(8,128)S(1)} %shard_map.69.refs_0_), channel_id=1, source_target_pairs={{0,1},{1,0},{2,3},{3,2},{4,5},{5,4},{6,7},{7,6},{8,9},{9,8},{10,11... | collective-permute-start | bytes 393224 | tf_op jit(solution)/shard_map/ppermute | solution.py:347
  215.5 15.5 %collective-permute-start.41 = (bf16[128,1024]{1,0:T(8,128)(2,1)S(1)}, bf16[128,1024]{1,0:T(8,128)(2,1)S(1)}, u32[]{:S(2)}, u32[]{:S(2)}) collective-permute-start(bf16[128,1024]{1,0:T(8,128)(2,1)S(1)} %bitcast.5), channel_id=1, source_target_pairs={{0,16},{4,20},{9,25},{13,29},{18,2},{22,6},{27,11},{31,15}} | collective-permute-start | bytes 786440 | tf_op jit(solution)/shard_map/ppermute | solution.py:417
  226.5 19.3 %collective-permute-start.50 = (bf16[16,7168]{1,0:T(8,128)(2,1)S(1)}, bf16[16,7168]{1,0:T(8,128)(2,1)S(1)}, u32[]{:S(2)}, u32[]{:S(2)}) collective-permute-start(bf16[16,7168]{1,0:T(8,128)(2,1)S(1)} %shard_map.83), channel_id=1, source_target_pairs={{0,16},{4,20},{8,24},{12,28},{16,0},{20,4},{24,8},{28,12},{1,17},{... | collective-permute-start | bytes 688136 | tf_op jit(solution)/shard_map/ppermute | solution.py:347
  226.7 19.1 %collective-permute-start.48 = (bf16[16,7168]{1,0:T(8,128)(2,1)S(1)}, bf16[16,7168]{1,0:T(8,128)(2,1)S(1)}, u32[]{:S(2)}, u32[]{:S(2)}) collective-permute-start(bf16[16,7168]{1,0:T(8,128)(2,1)S(1)} %shard_map.82), channel_id=1, source_target_pairs={{0,24},{4,28},{8,16},{12,20},{16,8},{20,12},{24,0},{28,4},{1,25},{... | collective-permute-start | bytes 688136 | tf_op jit(solution)/shard_map/ppermute | solution.py:347
  231.6 21.7 %collective-permute-start.42 = (bf16[128,1024]{1,0:T(8,128)(2,1)S(1)}, bf16[128,1024]{1,0:T(8,128)(2,1)S(1)}, u32[]{:S(2)}, u32[]{:S(2)}) collective-permute-start(bf16[128,1024]{1,0:T(8,128)(2,1)S(1)} %shard_map.74.held_ref), channel_id=1, source_target_pairs={{0,8},{4,12},{16,24},{20,28},{9,1},{13,5},{25,17},{29,21},{18,26},... | collective-permute-start | bytes 786440 | tf_op jit(solution)/shard_map/ppermute | solution.py:417
  246.0 21.3 %collective-permute-start.60 = (bf16[16,7168]{1,0:T(8,128)(2,1)S(1)}, bf16[16,7168]{1,0:T(8,128)(2,1)S(1)}, u32[]{:S(2)}, u32[]{:S(2)}) collective-permute-start(bf16[16,7168]{1,0:T(8,128)(2,1)S(1)} %shard_map.85.mine_ref), channel_id=1, source_target_pairs={{0,16},{4,20},{8,24},{12,28},{16,0},{20,4},{24,8},{28,12},{1,17},{... | collective-permute-start | bytes 688136 | tf_op jit(solution)/shard_map/ppermute | solution.py:347
  250.9 16.3 %collective-permute-start.58 = (bf16[16,7168]{1,0:T(8,128)(2,1)S(1)}, bf16[16,7168]{1,0:T(8,128)(2,1)S(1)}, u32[]{:S(2)}, u32[]{:S(2)}) collective-permute-start(bf16[16,7168]{1,0:T(8,128)(2,1)S(1)} %shard_map.85.mine_ref), channel_id=1, source_target_pairs={{0,24},{4,28},{8,16},{12,20},{16,8},{20,12},{24,0},{28,4},{1,25},{... | collective-permute-start | bytes 688136 | tf_op jit(solution)/shard_map/ppermute | solution.py:347
  253.9 16.3 %collective-permute-start.55 = (bf16[16,7168]{1,0:T(8,128)(2,1)S(1)}, bf16[16,7168]{1,0:T(8,128)(2,1)S(1)}, u32[]{:S(2)}, u32[]{:S(2)}) collective-permute-start(bf16[16,7168]{1,0:T(8,128)(2,1)S(1)} %shard_map.85.mine_ref), channel_id=1, source_target_pairs={{0,4},{4,0},{8,12},{12,8},{16,20},{20,16},{24,28},{28,24},{1,5},{5... | collective-permute-start | bytes 688136 | tf_op jit(solution)/shard_map/ppermute | solution.py:347
  267.8 14.6 %collective-permute-start.54 = (bf16[16,7168]{1,0:T(8,128)(2,1)S(1)}, bf16[16,7168]{1,0:T(8,128)(2,1)S(1)}, u32[]{:S(2)}, u32[]{:S(2)}) collective-permute-start(bf16[16,7168]{1,0:T(8,128)(2,1)S(1)} %collective-permute-done.53.mine_ref), channel_id=1, source_target_pairs={{0,4},{4,0},{8,12},{12,8},{16,20},{20,16},{24,28},{28,24},{1,5},{5... | collective-permute-start | bytes 688136 | tf_op jit(solution)/shard_map/ppermute | solution.py:347
  (43 other events, 443.6 us)

commit v5 on v4

--- a/solution.py
+++ b/solution.py
@@ -34,9 +34,9 @@
 
 ROW_CHUNKS = 4
 COL_CHUNKS = 8
-AHEAD = 2
-STREAM_COLS = 4
-STREAM_MIB = 9
+AHEAD = 3
+STREAM_COLS = 6
+STREAM_MIB = 12
 
 
 def images_body(where, mine_ref, other_ref, *refs, carried, mode, offset):

time: 295 us -> 293 us (level)
  transfers between devices with their start and end apart: 64 -> 64, of which waited for: 28 -> 28; matrix products, arithmetic and copies ran while one was open for 0% -> 0% of each run, Pallas kernels for 29% -> 28%
where the time goes in v5:
time: 293 us; the launch traced here: 292 us
  waiting for transfers between devices  116 us (40%)
  Pallas kernels  109 us (37%)
  starting transfers between devices  64.9 us (22%)
    ppermute x62, waiting for transfers between devices, xor_permute(): return lax.ppermute(x, axis, [(i, i ^ bits) for i in range(size)])  116 us
    ppermute x62, starting transfers between devices, xor_permute(): return lax.ppermute(x, axis, [(i, i ^ bits) for i in range(size)])  59.6 us
    pallas_call x8, Pallas kernels, images_of_query(): pl.pallas_call(functools.partial(images_body, carried=carried, mode=mode,...  52.1 us
    pallas_call x8, Pallas kernels, back_of_query(): pl.pallas_call(functools.partial(back_body, stream=stream, ties=len(after...  36.4 us
    pallas_call x2, Pallas kernels, orthonormal(): pl.pallas_call(basis_body, in_specs=[VMEM] * (1 + len(grams)), out_specs=...  7.73 us
    pallas_call x4, Pallas kernels, project_in(): pl.pallas_call(project_in_body, grid=(1,), in_specs=[SMEM, VMEM, VMEM, VM...  6.66 us
  transfers between devices with their start and end apart: 64, of which 28 were waited for; matrix products, arithmetic and copies ran while one was open for 0% of the time, Pallas kernels for 28%

profile of v5, /device:TPU:0, one launch (start us, length us, event | category | flops | bytes accessed | tf_op | source)
XLA Modules:
  0.0 291.8 jit_solution(4068051640074784019)
XLA Ops:
  0.0 5.1 %collective-permute-start.9 = (bf16[16,7168]{1,0:T(8,128)(2,1)}, bf16[16,7168]{1,0:T(8,128)(2,1)S(1)}, u32[]{:S(2)}, u32[]{:S(2)}) collective-permute-start(bf16[16,7168]{1,0:T(8,128)(2,1)} %bitcast.7), channel_id=1, source_target_pairs={{0,24},{4,28},{8,16},{12,20},{16,8},{20,12},{24,0},{28,4},{1,25},{... | collective-permute-start | bytes 688136 | tf_op jit(solution)/shard_map/ppermute | solution.py:347
  5.7 6.2 %collective-permute-done.9.mine_ref = bf16[16,7168]{1,0:T(8,128)(2,1)S(1)} collective-permute-done((bf16[16,7168]{1,0:T(8,128)(2,1)}, bf16[16,7168]{1,0:T(8,128)(2,1)S(1)}, u32[]{:S(2)}, u32[]{:S(2)}) %collective-permute-start.9) | collective-permute-done | bytes 229408 | tf_op jit(solution)/shard_map/ppermute | solution.py:347
  11.9 12.9 %collective-permute-done.5.mine_ref = bf16[16,7168]{1,0:T(8,128)(2,1)S(1)} collective-permute-done((bf16[16,7168]{1,0:T(8,128)(2,1)}, bf16[16,7168]{1,0:T(8,128)(2,1)S(1)}, u32[]{:S(2)}, u32[]{:S(2)}) %collective-permute-start.5) | collective-permute-done | bytes 229408 | tf_op jit(solution)/shard_map/ppermute | solution.py:347
  26.2 7.3 %shard_map.46.refs_0_ = f32[32,1024]{1,0:T(8,128)S(1)} custom-call(s32[3]{0:T(128)S(1)} %pad_add_fusion.where, bf16[16,7168]{1,0:T(8,128)(2,1)S(1)} %bitcast.11, bf16[16,7168]{1,0:T(8,128)(2,1)S(1)} %collective-permute-done.2.other_ref, bf16[4,1024,7168]{2,1,0:T(8,128)(2,1)} %source_ref.3), custom_call_target="tpu_custom_call" | custom-call | flops 3758096384 | bytes 14680064 | tf_op jit(solution)/shard_map/pallas_call | solution.py:99
  33.6 7.3 %shard_map.47 = (f32[64,1024]{1,0:T(8,128)S(1)}, bf16[1024,7168]{1,0:T(8,128)(2,1)S(1)}) custom-call(s32[3]{0:T(128)S(1)} %pad_add_fusion.where, bf16[16,7168]{1,0:T(8,128)(2,1)S(1)} %collective-permute-done.mine_ref, bf16[16,7168]{1,0:T(8,128)(2,1)S(1)} %collective-permute-done.1.other_ref, f32[32,1024]{1,0:T(8,128)S(1)} %shard_map.46.refs_0_, ...), custom_call_target="tpu_custom_call" | custom-call | flops 3758096384 | bytes 14680064 | tf_op jit(solution)/shard_map/pallas_call | solution.py:99
  42.4 7.3 %shard_map.49 = (f32[32,1024]{1,0:T(8,128)S(1)}, bf16[1024,7168]{1,0:T(8,128)(2,1)S(1)}) custom-call(s32[3]{0:T(128)S(1)} %pad_add_fusion.where, bf16[16,7168]{1,0:T(8,128)(2,1)S(1)} %collective-permute-done.5.mine_ref, bf16[16,7168]{1,0:T(8,128)(2,1)S(1)} %collective-permute-done.6.other_ref, bf16[4,1024,7168]{2,1,0:T(8,128)(2,1)} %source_ref.3), custom_call_target="tpu_custom_call" | custom-call | flops 3758096384 | bytes 14680064 | tf_op jit(solution)/shard_map/pallas_call | solution.py:99
  50.3 7.3 %shard_map.51 = (f32[32,1024]{1,0:T(8,128)S(1)}, bf16[1024,7168]{1,0:T(8,128)(2,1)S(1)}) custom-call(s32[3]{0:T(128)S(1)} %pad_add_fusion.where, bf16[16,7168]{1,0:T(8,128)(2,1)S(1)} %collective-permute-done.9.mine_ref, bf16[16,7168]{1,0:T(8,128)(2,1)S(1)} %collective-permute-done.10.other_ref, bf16[4,1024,7168]{2,1,0:T(8,128)(2,1)} %source_ref.3), custom_call_target="tpu_custom_call" | custom-call | flops 3758096384 | bytes 14680064 | tf_op jit(solution)/shard_map/pallas_call | solution.py:99
  64.2 6.6 %collective-permute-done.8.refs_3_ = f32[32,1024]{1,0:T(8,128)S(1)} collective-permute-done((f32[32,1024]{1,0:T(8,128)S(1)}, f32[32,1024]{1,0:T(8,128)S(1)}, u32[]{:S(2)}, u32[]{:S(2)}) %collective-permute-start.8) | collective-permute-done | bytes 131104 | tf_op jit(solution)/shard_map/ppermute | solution.py:347
  98.0 6.6 %shard_map.59 = (f32[16,7168]{1,0:T(8,128)S(1)}, bf16[16,7168]{1,0:T(8,128)(2,1)S(1)}) custom-call(s32[3]{0:T(128)S(1)} %pad_add_fusion.where, bf16[4,32,1024]{2,1,0:T(8,128)(2,1)S(1)} %shard_map.55.basis_ref, bf16[4,1024,7168]{2,1,0:T(8,128)(2,1)} %source_ref.3, bf16[16,7168]{1,0:T(8,128)(2,1)S(1)} %get-tuple-element.41.rest_0_), custom_call_target="tpu_custom_call" | custom-call | flops 3758096384 | bytes 14680064 | tf_op jit(solution)/shard_map/pallas_call | solution.py:158
  109.9 5.8 %collective-permute-done.19.refs_2_ = bf16[16,7168]{1,0:T(8,128)(2,1)S(1)} collective-permute-done((bf16[16,7168]{1,0:T(8,128)(2,1)S(1)}, bf16[16,7168]{1,0:T(8,128)(2,1)S(1)}, u32[]{:S(2)}, u32[]{:S(2)}) %collective-permute-start.19) | collective-permute-done | bytes 229408 | tf_op jit(solution)/shard_map/ppermute | solution.py:347
  115.7 12.3 %collective-permute-done.21.refs_3_ = bf16[16,7168]{1,0:T(8,128)(2,1)S(1)} collective-permute-done((bf16[16,7168]{1,0:T(8,128)(2,1)S(1)}, bf16[16,7168]{1,0:T(8,128)(2,1)S(1)}, u32[]{:S(2)}, u32[]{:S(2)}) %collective-permute-start.21) | collective-permute-done | bytes 229408 | tf_op jit(solution)/shard_map/ppermute | solution.py:347
  132.6 6.0 %collective-permute-done.33.mine_ref = bf16[16,7168]{1,0:T(8,128)(2,1)S(1)} collective-permute-done((bf16[16,7168]{1,0:T(8,128)(2,1)S(1)}, bf16[16,7168]{1,0:T(8,128)(2,1)S(1)}, u32[]{:S(2)}, u32[]{:S(2)}) %collective-permute-start.33) | collective-permute-done | bytes 229408 | tf_op jit(solution)/shard_map/ppermute | solution.py:347
  138.6 10.6 %collective-permute-done.29.mine_ref = bf16[16,7168]{1,0:T(8,128)(2,1)S(1)} collective-permute-done((bf16[16,7168]{1,0:T(8,128)(2,1)S(1)}, bf16[16,7168]{1,0:T(8,128)(2,1)S(1)}, u32[]{:S(2)}, u32[]{:S(2)}) %collective-permute-start.29) | collective-permute-done | bytes 229408 | tf_op jit(solution)/shard_map/ppermute | solution.py:347
  149.7 7.3 %shard_map.64.refs_0_ = f32[32,1024]{1,0:T(8,128)S(1)} custom-call(s32[3]{0:T(128)S(1)} %pad_add_fusion.where, bf16[16,7168]{1,0:T(8,128)(2,1)S(1)} %shard_map.63.mine_ref, bf16[16,7168]{1,0:T(8,128)(2,1)S(1)} %collective-permute-done.26.other_ref, bf16[4,1024,7168]{2,1,0:T(8,128)(2,1)} %source_ref.3), custom_call_target="tpu_custom_call" | custom-call | flops 3758096384 | bytes 14680064 | tf_op jit(solution)/shard_map/pallas_call | solution.py:99
  157.1 5.2 %shard_map.69.refs_0_ = f32[32,1024]{1,0:T(8,128)S(1)} custom-call(s32[3]{0:T(128)S(1)} %pad_add_fusion.where, bf16[16,7168]{1,0:T(8,128)(2,1)S(1)} %collective-permute-done.33.mine_ref, bf16[16,7168]{1,0:T(8,128)(2,1)S(1)} %collective-permute-done.34.other_ref, bf16[1024,7168]{1,0:T(8,128)(2,1)S(1)} %get-tuple-element.38.source_ref.refs_0_), custom_call_target="tpu_custom_call" | custom-call | flops 3758096384 | bytes 14680064 | tf_op jit(solution)/shard_map/pallas_call | solution.py:99
  162.8 5.2 %shard_map.65.refs_0_ = f32[64,1024]{1,0:T(8,128)S(1)} custom-call(s32[3]{0:T(128)S(1)} %pad_add_fusion.where, bf16[16,7168]{1,0:T(8,128)(2,1)S(1)} %collective-permute-done.24.mine_ref, bf16[16,7168]{1,0:T(8,128)(2,1)S(1)} %collective-permute-done.25.other_ref, f32[32,1024]{1,0:T(8,128)S(1)} %shard_map.64.refs_0_, ...), custom_call_target="tpu_custom_call" | custom-call | flops 3758096384 | bytes 14680064 | tf_op jit(solution)/shard_map/pallas_call | solution.py:99
  169.5 5.3 %shard_map.67.refs_0_ = f32[32,1024]{1,0:T(8,128)S(1)} custom-call(s32[3]{0:T(128)S(1)} %pad_add_fusion.where, bf16[16,7168]{1,0:T(8,128)(2,1)S(1)} %collective-permute-done.29.mine_ref, bf16[16,7168]{1,0:T(8,128)(2,1)S(1)} %collective-permute-done.30.other_ref, bf16[1024,7168]{1,0:T(8,128)(2,1)S(1)} %get-tuple-element.37.source_ref.refs_0_), custom_call_target="tpu_custom_call" | custom-call | flops 3758096384 | bytes 14680064 | tf_op jit(solution)/shard_map/pallas_call | solution.py:99
  181.4 5.9 %collective-permute-done.36.refs_5_ = f32[32,1024]{1,0:T(8,128)S(1)} collective-permute-done((f32[32,1024]{1,0:T(8,128)S(1)}, f32[32,1024]{1,0:T(8,128)S(1)}, u32[]{:S(2)}, u32[]{:S(2)}) %collective-permute-start.36) | collective-permute-done | bytes 131104 | tf_op jit(solution)/shard_map/ppermute | solution.py:347
  217.4 6.6 %shard_map.81 = (f32[16,7168]{1,0:T(8,128)S(1)}, bf16[16,7168]{1,0:T(8,128)(2,1)S(1)}) custom-call(s32[3]{0:T(128)S(1)} %pad_add_fusion.where, bf16[4,32,1024]{2,1,0:T(8,128)(2,1)S(1)} %shard_map.73.basis_ref, bf16[4,1024,7168]{2,1,0:T(8,128)(2,1)} %source_ref.3, bf16[16,7168]{1,0:T(8,128)(2,1)S(1)} %get-tuple-element.51.rest_0_), custom_call_target="tpu_custom_call" | custom-call | flops 3758096384 | bytes 14680064 | tf_op jit(solution)/shard_map/pallas_call | solution.py:158
  224.6 4.3 %collective-permute-start.48 = (bf16[16,7168]{1,0:T(8,128)(2,1)S(1)}, bf16[16,7168]{1,0:T(8,128)(2,1)S(1)}, u32[]{:S(2)}, u32[]{:S(2)}) collective-permute-start(bf16[16,7168]{1,0:T(8,128)(2,1)S(1)} %shard_map.82), channel_id=1, source_target_pairs={{0,24},{4,28},{8,16},{12,20},{16,8},{20,12},{24,0},{28,4},{1,25},{... | collective-permute-start | bytes 688136 | tf_op jit(solution)/shard_map/ppermute | solution.py:347
  230.9 4.1 %collective-permute-done.52.refs_4_ = bf16[16,7168]{1,0:T(8,128)(2,1)S(1)} collective-permute-done((bf16[16,7168]{1,0:T(8,128)(2,1)S(1)}, bf16[16,7168]{1,0:T(8,128)(2,1)S(1)}, u32[]{:S(2)}, u32[]{:S(2)}) %collective-permute-start.52) | collective-permute-done | bytes 229408 | tf_op jit(solution)/shard_map/ppermute | solution.py:347
  234.9 8.8 %collective-permute-done.50.refs_3_ = bf16[16,7168]{1,0:T(8,128)(2,1)S(1)} collective-permute-done((bf16[16,7168]{1,0:T(8,128)(2,1)S(1)}, bf16[16,7168]{1,0:T(8,128)(2,1)S(1)}, u32[]{:S(2)}, u32[]{:S(2)}) %collective-permute-start.50) | collective-permute-done | bytes 229408 | tf_op jit(solution)/shard_map/ppermute | solution.py:347
  243.9 5.0 %collective-permute-start.60 = (bf16[16,7168]{1,0:T(8,128)(2,1)S(1)}, bf16[16,7168]{1,0:T(8,128)(2,1)S(1)}, u32[]{:S(2)}, u32[]{:S(2)}) collective-permute-start(bf16[16,7168]{1,0:T(8,128)(2,1)S(1)} %shard_map.85.mine_ref), channel_id=1, source_target_pairs={{0,16},{4,20},{8,24},{12,28},{16,0},{20,4},{24,8},{28,12},{1,17},{... | collective-permute-start | bytes 688136 | tf_op jit(solution)/shard_map/ppermute | solution.py:347
  252.3 12.8 %collective-permute-done.60.mine_ref = bf16[16,7168]{1,0:T(8,128)(2,1)S(1)} collective-permute-done((bf16[16,7168]{1,0:T(8,128)(2,1)S(1)}, bf16[16,7168]{1,0:T(8,128)(2,1)S(1)}, u32[]{:S(2)}, u32[]{:S(2)}) %collective-permute-start.60) | collective-permute-done | bytes 229408 | tf_op jit(solution)/shard_map/ppermute | solution.py:347
  (158 shorter events, 119.9 us)
Async XLA Ops:
  5.1 19.7 %collective-permute-start.5 = (bf16[16,7168]{1,0:T(8,128)(2,1)}, bf16[16,7168]{1,0:T(8,128)(2,1)S(1)}, u32[]{:S(2)}, u32[]{:S(2)}) collective-permute-start(bf16[16,7168]{1,0:T(8,128)(2,1)} %bitcast.8), channel_id=1, source_target_pairs={{0,16},{4,20},{8,24},{12,28},{16,0},{20,4},{24,8},{28,12},{1,17},{... | collective-permute-start | bytes 688136 | tf_op jit(solution)/shard_map/ppermute | solution.py:347
  5.1 19.7 %collective-permute-start = (bf16[16,7168]{1,0:T(8,128)(2,1)}, bf16[16,7168]{1,0:T(8,128)(2,1)S(1)}, u32[]{:S(2)}, u32[]{:S(2)}) collective-permute-start(bf16[16,7168]{1,0:T(8,128)(2,1)} %bitcast.9), channel_id=1, source_target_pairs={{0,8},{4,12},{8,0},{12,4},{16,24},{20,28},{24,16},{28,20},{1,9},{5... | collective-permute-start | bytes 688136 | tf_op jit(solution)/shard_map/ppermute | solution.py:347
  5.6 19.7 %collective-permute-start.2 = (bf16[16,7168]{1,0:T(8,128)(2,1)}, bf16[16,7168]{1,0:T(8,128)(2,1)S(1)}, u32[]{:S(2)}, u32[]{:S(2)}) collective-permute-start(bf16[16,7168]{1,0:T(8,128)(2,1)} %bitcast.10), channel_id=1, source_target_pairs={{0,4},{4,0},{8,12},{12,8},{16,20},{20,16},{24,28},{28,24},{1,5},{5... | collective-permute-start | bytes 688136 | tf_op jit(solution)/shard_map/ppermute | solution.py:347
  11.9 38.4 %collective-permute-start.10 = (bf16[16,7168]{1,0:T(8,128)(2,1)S(1)}, bf16[16,7168]{1,0:T(8,128)(2,1)S(1)}, u32[]{:S(2)}, u32[]{:S(2)}) collective-permute-start(bf16[16,7168]{1,0:T(8,128)(2,1)S(1)} %collective-permute-done.9.mine_ref), channel_id=1, source_target_pairs={{0,4},{4,0},{8,12},{12,8},{16,20},{20,16},{24,28},{28,24},{1,5},{5... | collective-permute-start | bytes 688136 | tf_op jit(solution)/shard_map/ppermute | solution.py:347
  24.8 17.6 %collective-permute-start.6 = (bf16[16,7168]{1,0:T(8,128)(2,1)S(1)}, bf16[16,7168]{1,0:T(8,128)(2,1)S(1)}, u32[]{:S(2)}, u32[]{:S(2)}) collective-permute-start(bf16[16,7168]{1,0:T(8,128)(2,1)S(1)} %collective-permute-done.5.mine_ref), channel_id=1, source_target_pairs={{0,4},{4,0},{8,12},{12,8},{16,20},{20,16},{24,28},{28,24},{1,5},{5... | collective-permute-start | bytes 688136 | tf_op jit(solution)/shard_map/ppermute | solution.py:347
  40.9 18.3 %collective-permute-start.3 = (f32[64,1024]{1,0:T(8,128)S(1)}, f32[64,1024]{1,0:T(8,128)S(1)}, u32[]{:S(2)}, u32[]{:S(2)}) collective-permute-start(f32[64,1024]{1,0:T(8,128)S(1)} %get-tuple-element.31.refs_0_), channel_id=1, source_target_pairs={{0,1},{1,0},{2,3},{3,2},{4,5},{5,4},{6,7},{7,6},{8,9},{9,8},{10,11... | collective-permute-start | bytes 786440 | tf_op jit(solution)/shard_map/ppermute | solution.py:347
  89.5 15.6 %collective-permute-start.18 = (bf16[16,7168]{1,0:T(8,128)(2,1)S(1)}, bf16[16,7168]{1,0:T(8,128)(2,1)S(1)}, u32[]{:S(2)}, u32[]{:S(2)}) collective-permute-start(bf16[16,7168]{1,0:T(8,128)(2,1)S(1)} %get-tuple-element.39.rest_0_), channel_id=1, source_target_pairs={{0,4},{4,0},{8,12},{12,8},{16,20},{20,16},{24,28},{28,24},{1,5},{5... | collective-permute-start | bytes 688136 | tf_op jit(solution)/shard_map/ppermute | solution.py:347
  106.8 21.2 %collective-permute-start.21 = (bf16[16,7168]{1,0:T(8,128)(2,1)S(1)}, bf16[16,7168]{1,0:T(8,128)(2,1)S(1)}, u32[]{:S(2)}, u32[]{:S(2)}) collective-permute-start(bf16[16,7168]{1,0:T(8,128)(2,1)S(1)} %shard_map.61), channel_id=1, source_target_pairs={{0,16},{4,20},{8,24},{12,28},{16,0},{20,4},{24,8},{28,12},{1,17},{... | collective-permute-start | bytes 688136 | tf_op jit(solution)/shard_map/ppermute | solution.py:347
  107.9 20.1 %collective-permute-start.23 = (bf16[16,7168]{1,0:T(8,128)(2,1)S(1)}, bf16[16,7168]{1,0:T(8,128)(2,1)S(1)}, u32[]{:S(2)}, u32[]{:S(2)}) collective-permute-start(bf16[16,7168]{1,0:T(8,128)(2,1)S(1)} %shard_map.62), channel_id=1, source_target_pairs={{0,8},{4,12},{8,0},{12,4},{16,24},{20,28},{24,16},{28,20},{1,9},{5... | collective-permute-start | bytes 688136 | tf_op jit(solution)/shard_map/ppermute | solution.py:347
  130.7 18.5 %collective-permute-start.29 = (bf16[16,7168]{1,0:T(8,128)(2,1)S(1)}, bf16[16,7168]{1,0:T(8,128)(2,1)S(1)}, u32[]{:S(2)}, u32[]{:S(2)}) collective-permute-start(bf16[16,7168]{1,0:T(8,128)(2,1)S(1)} %shard_map.63.mine_ref), channel_id=1, source_target_pairs={{0,16},{4,20},{8,24},{12,28},{16,0},{20,4},{24,8},{28,12},{1,17},{... | collective-permute-start | bytes 688136 | tf_op jit(solution)/shard_map/ppermute | solution.py:347
  130.7 18.5 %collective-permute-start.24 = (bf16[16,7168]{1,0:T(8,128)(2,1)S(1)}, bf16[16,7168]{1,0:T(8,128)(2,1)S(1)}, u32[]{:S(2)}, u32[]{:S(2)}) collective-permute-start(bf16[16,7168]{1,0:T(8,128)(2,1)S(1)} %shard_map.63.mine_ref), channel_id=1, source_target_pairs={{0,8},{4,12},{8,0},{12,4},{16,24},{20,28},{24,16},{28,20},{1,9},{5... | collective-permute-start | bytes 688136 | tf_op jit(solution)/shard_map/ppermute | solution.py:347
  132.6 17.1 %collective-permute-start.26 = (bf16[16,7168]{1,0:T(8,128)(2,1)S(1)}, bf16[16,7168]{1,0:T(8,128)(2,1)S(1)}, u32[]{:S(2)}, u32[]{:S(2)}) collective-permute-start(bf16[16,7168]{1,0:T(8,128)(2,1)S(1)} %shard_map.63.mine_ref), channel_id=1, source_target_pairs={{0,4},{4,0},{8,12},{12,8},{16,20},{20,16},{24,28},{28,24},{1,5},{5... | collective-permute-start | bytes 688136 | tf_op jit(solution)/shard_map/ppermute | solution.py:347
  138.6 18.5 %collective-permute-start.34 = (bf16[16,7168]{1,0:T(8,128)(2,1)S(1)}, bf16[16,7168]{1,0:T(8,128)(2,1)S(1)}, u32[]{:S(2)}, u32[]{:S(2)}) collective-permute-start(bf16[16,7168]{1,0:T(8,128)(2,1)S(1)} %collective-permute-done.33.mine_ref), channel_id=1, source_target_pairs={{0,4},{4,0},{8,12},{12,8},{16,20},{20,16},{24,28},{28,24},{1,5},{5... | collective-permute-start | bytes 688136 | tf_op jit(solution)/shard_map/ppermute | solution.py:347
  149.2 20.3 %collective-permute-start.30 = (bf16[16,7168]{1,0:T(8,128)(2,1)S(1)}, bf16[16,7168]{1,0:T(8,128)(2,1)S(1)}, u32[]{:S(2)}, u32[]{:S(2)}) collective-permute-start(bf16[16,7168]{1,0:T(8,128)(2,1)S(1)} %collective-permute-done.29.mine_ref), channel_id=1, source_target_pairs={{0,4},{4,0},{8,12},{12,8},{16,20},{20,16},{24,28},{28,24},{1,5},{5... | collective-permute-start | bytes 688136 | tf_op jit(solution)/shard_map/ppermute | solution.py:347
  162.2 15.3 %collective-permute-start.35 = (f32[32,1024]{1,0:T(8,128)S(1)}, f32[32,1024]{1,0:T(8,128)S(1)}, u32[]{:S(2)}, u32[]{:S(2)}) collective-permute-start(f32[32,1024]{1,0:T(8,128)S(1)} %shard_map.69.refs_0_), channel_id=1, source_target_pairs={{0,1},{1,0},{2,3},{3,2},{4,5},{5,4},{6,7},{7,6},{8,9},{9,8},{10,11... | collective-permute-start | bytes 393224 | tf_op jit(solution)/shard_map/ppermute | solution.py:347
  213.5 15.5 %collective-permute-start.41 = (bf16[128,1024]{1,0:T(8,128)(2,1)S(1)}, bf16[128,1024]{1,0:T(8,128)(2,1)S(1)}, u32[]{:S(2)}, u32[]{:S(2)}) collective-permute-start(bf16[128,1024]{1,0:T(8,128)(2,1)S(1)} %bitcast.5), channel_id=1, source_target_pairs={{0,16},{4,20},{9,25},{13,29},{18,2},{22,6},{27,11},{31,15}} | collective-permute-start | bytes 786440 | tf_op jit(solution)/shard_map/ppermute | solution.py:417
  224.4 19.3 %collective-permute-start.50 = (bf16[16,7168]{1,0:T(8,128)(2,1)S(1)}, bf16[16,7168]{1,0:T(8,128)(2,1)S(1)}, u32[]{:S(2)}, u32[]{:S(2)}) collective-permute-start(bf16[16,7168]{1,0:T(8,128)(2,1)S(1)} %shard_map.83), channel_id=1, source_target_pairs={{0,16},{4,20},{8,24},{12,28},{16,0},{20,4},{24,8},{28,12},{1,17},{... | collective-permute-start | bytes 688136 | tf_op jit(solution)/shard_map/ppermute | solution.py:347
  224.6 19.1 %collective-permute-start.48 = (bf16[16,7168]{1,0:T(8,128)(2,1)S(1)}, bf16[16,7168]{1,0:T(8,128)(2,1)S(1)}, u32[]{:S(2)}, u32[]{:S(2)}) collective-permute-start(bf16[16,7168]{1,0:T(8,128)(2,1)S(1)} %shard_map.82), channel_id=1, source_target_pairs={{0,24},{4,28},{8,16},{12,20},{16,8},{20,12},{24,0},{28,4},{1,25},{... | collective-permute-start | bytes 688136 | tf_op jit(solution)/shard_map/ppermute | solution.py:347
  229.5 21.6 %collective-permute-start.42 = (bf16[128,1024]{1,0:T(8,128)(2,1)S(1)}, bf16[128,1024]{1,0:T(8,128)(2,1)S(1)}, u32[]{:S(2)}, u32[]{:S(2)}) collective-permute-start(bf16[128,1024]{1,0:T(8,128)(2,1)S(1)} %shard_map.74.held_ref), channel_id=1, source_target_pairs={{0,8},{4,12},{16,24},{20,28},{9,1},{13,5},{25,17},{29,21},{18,26},... | collective-permute-start | bytes 786440 | tf_op jit(solution)/shard_map/ppermute | solution.py:417
  243.9 21.3 %collective-permute-start.60 = (bf16[16,7168]{1,0:T(8,128)(2,1)S(1)}, bf16[16,7168]{1,0:T(8,128)(2,1)S(1)}, u32[]{:S(2)}, u32[]{:S(2)}) collective-permute-start(bf16[16,7168]{1,0:T(8,128)(2,1)S(1)} %shard_map.85.mine_ref), channel_id=1, source_target_pairs={{0,16},{4,20},{8,24},{12,28},{16,0},{20,4},{24,8},{28,12},{1,17},{... | collective-permute-start | bytes 688136 | tf_op jit(solution)/shard_map/ppermute | solution.py:347
  248.8 16.3 %collective-permute-start.58 = (bf16[16,7168]{1,0:T(8,128)(2,1)S(1)}, bf16[16,7168]{1,0:T(8,128)(2,1)S(1)}, u32[]{:S(2)}, u32[]{:S(2)}) collective-permute-start(bf16[16,7168]{1,0:T(8,128)(2,1)S(1)} %shard_map.85.mine_ref), channel_id=1, source_target_pairs={{0,24},{4,28},{8,16},{12,20},{16,8},{20,12},{24,0},{28,4},{1,25},{... | collective-permute-start | bytes 688136 | tf_op jit(solution)/shard_map/ppermute | solution.py:347
  251.2 14.5 %collective-permute-start.53 = (bf16[16,7168]{1,0:T(8,128)(2,1)S(1)}, bf16[16,7168]{1,0:T(8,128)(2,1)S(1)}, u32[]{:S(2)}, u32[]{:S(2)}) collective-permute-start(bf16[16,7168]{1,0:T(8,128)(2,1)S(1)} %shard_map.85.mine_ref), channel_id=1, source_target_pairs={{0,8},{4,12},{8,0},{12,4},{16,24},{20,28},{24,16},{28,20},{1,9},{5... | collective-permute-start | bytes 688136 | tf_op jit(solution)/shard_map/ppermute | solution.py:347
  251.8 16.3 %collective-permute-start.55 = (bf16[16,7168]{1,0:T(8,128)(2,1)S(1)}, bf16[16,7168]{1,0:T(8,128)(2,1)S(1)}, u32[]{:S(2)}, u32[]{:S(2)}) collective-permute-start(bf16[16,7168]{1,0:T(8,128)(2,1)S(1)} %shard_map.85.mine_ref), channel_id=1, source_target_pairs={{0,4},{4,0},{8,12},{12,8},{16,20},{20,16},{24,28},{28,24},{1,5},{5... | collective-permute-start | bytes 688136 | tf_op jit(solution)/shard_map/ppermute | solution.py:347
  265.7 14.7 %collective-permute-start.54 = (bf16[16,7168]{1,0:T(8,128)(2,1)S(1)}, bf16[16,7168]{1,0:T(8,128)(2,1)S(1)}, u32[]{:S(2)}, u32[]{:S(2)}) collective-permute-start(bf16[16,7168]{1,0:T(8,128)(2,1)S(1)} %collective-permute-done.53.mine_ref), channel_id=1, source_target_pairs={{0,4},{4,0},{8,12},{12,8},{16,20},{20,16},{24,28},{28,24},{1,5},{5... | collective-permute-start | bytes 688136 | tf_op jit(solution)/shard_map/ppermute | solution.py:347
  (43 other events, 441.6 us)
